TPU v7x, 32 devices: a whole 2x2x4 slice. The times are simulated.
32 devices in a mesh: fsdp: 32 (over z, y, x, core).
Axes of the slice: x: 2, y: 2, z: 4, core: 2. Of those that a mesh axis runs over, the one named last changes fastest.
Arguments:
- hidden_in: bfloat16 [16384, 768], P('fsdp'), may hold values from -6 to 6
- segment_ids: int32 [32, 512], P('fsdp'), may hold values from 0 to 7, never falling along the last dimension, each value on 1 to 128 neighbouring positions
- cotangent: bfloat16 [16384, 768], P('fsdp'), may hold values from -6 to 6
- w_in: bfloat16 [768, 3352], P('fsdp'), may hold values from -0.21875 to 0.21875
- w_out: bfloat16 [1536, 768], P('fsdp'), may hold values from -0.15625 to 0.15625
- conv_taps: bfloat16 [5, 1792], P(None, 'fsdp'), may hold values from -3 to 3
- gains: bfloat16 [2304], P('fsdp'), may hold values from 0.5 to 1.5
- a_log: float32 [24], replicated, may hold values from 0 to 2.77
- d_skip: float32 [24], replicated, may hold values from 0.5 to 1.5
- dt_bias: float32 [24], replicated, may hold values from -6.9 to -2.3
Outputs:
- output: bfloat16 [16384, 768], P('fsdp')
- input_grad: float32 [16384, 768], P('fsdp')
- grad_w_in: float32 [768, 3352], P('fsdp')
- grad_w_out: float32 [1536, 768], P('fsdp')
- grad_conv_taps: float32 [5, 1792], P(None, 'fsdp')
- grad_gains: float32 [2304], P('fsdp')
- grad_a_log: float32 [24], replicated
- grad_d_skip: float32 [24], replicated
- grad_dt_bias: float32 [24], replicated
Inputs may be any that keep to these rules, and one draw needn't show every extreme that they name: `segment_ids`: within each sequence the numbers never fall; each segment has 1 to 128 positions, and one has exactly 128.
All inputs are finite; a program needn't handle non-finite values.
Results may differ from a plain program's by a relative error of at most 0.0068.
Values may be sent and summed in bfloat16 or wider, within the bound.
No kernel may reach another device: no remote copies, remote signals or barrier semaphores. Data moves between devices by JAX's collectives and lax.ppermute only.
A program may use at most 192 MiB of HBM per device.

v0:
```python
import jax
import jax.numpy as jnp
import numpy as np
from jax import lax
from jax.experimental import pallas as pl
from jax.experimental.pallas import tpu as pltpu
from jax.sharding import PartitionSpec as P


BLK = 128
LOG2E = 1.4426950408889634
F32 = jnp.float32
BF16 = jnp.bfloat16
HIGH = lax.Precision.HIGHEST


def mm(a, b):
    return lax.dot_general(a, b, (((1,), (0,)), ((), ())), preferred_element_type=F32)


def mm_nt(a, b):
    return lax.dot_general(a, b, (((1,), (1,)), ((), ())), preferred_element_type=F32)


def mm_tn(a, b):
    return lax.dot_general(a, b, (((0,), (0,)), ((), ())), preferred_element_type=F32)


def split2(x):
    hi = x.astype(BF16)
    return hi, (x - hi.astype(F32)).astype(BF16)


def iota(shape, dim):
    return lax.broadcasted_iota(jnp.int32, shape, dim)


def perm_matrix(dvec, width):
    return (iota((width, width), 0) == dvec).astype(F32).astype(BF16)


def rows_of(refs, lanes=slice(None)):
    return jnp.concatenate([ref[:, lanes] for ref in refs], axis=0)


def normed_of(hid_ref, gain, dvec_ref, xn_ref):
    tokens = hid_ref[...].astype(F32)
    scale = lax.rsqrt(jnp.mean(tokens * tokens, axis=-1, keepdims=True) + 1e-05)
    normed = (tokens * scale * gain).astype(BF16)
    perm = perm_matrix(dvec_ref[...], tokens.shape[1])
    xn_ref[...] = mm(normed, perm).astype(BF16)


def norm_kernel(hid_ref, gains_ref, dvec_ref, xn_ref):
    normed_of(hid_ref, gains_ref[:, : hid_ref.shape[1]], dvec_ref, xn_ref)


def prep_kernel(at, taps_n, hid_ref, dvec_ref, owner_ref, where_ref, *refs):
    pieces, (xn_ref, taps_ref, gains_ref) = refs[:-3], refs[-3:]
    held = rows_of(pieces)
    devices = owner_ref.shape[0]
    rows_in = held.shape[0] // devices
    row = iota((8 * devices, held.shape[0]), 0)
    bits = devices.bit_length() - 1
    source = (row & (devices - 1)) * rows_in + lax.shift_right_logical(row, bits)
    pick = (iota(row.shape, 1) == source).astype(F32).astype(BF16)
    small = mm(pick, held).astype(BF16)

    def spread(part, line, width):
        lane, owner = where_ref[line : line + 1, :width], where_ref[line + 1 : line + 2, :width]
        chosen = (iota((BLK, width), 0) == lane + at).astype(F32).astype(BF16)
        wide = mm(part, chosen)
        return jnp.sum(jnp.where(owner_ref[...] == owner, wide, 0.0), axis=0, keepdims=True)

    channels, width = taps_ref.shape[1], gains_ref.shape[1]
    taps_ref[...] = jnp.zeros_like(taps_ref)
    for j in range(taps_n):
        taps_ref[j : j + 1, :] = spread(small[j * devices : (j + 1) * devices], 0, channels)
    gains_ref[...] = spread(small[taps_n * devices : (taps_n + 1) * devices], 2, width)
    normed_of(hid_ref, gains_ref[:, : hid_ref.shape[1]], dvec_ref, xn_ref)


def head_setup(dt_raw, heads_ref, step_ref, cc_ref, al_ref, ew_ref, wq_ref, cct_ref):
    length = dt_raw.shape[0]
    biased = dt_raw + heads_ref[2:3, :]
    step = jnp.maximum(biased, 0.0) + jnp.log1p(jnp.exp(-jnp.abs(biased)))
    step_ref[...] = step
    rate = step * (jnp.exp(heads_ref[0:1, :]) * (-LOG2E))
    lower = (iota((BLK, BLK), 0) >= iota((BLK, BLK), 1)).astype(F32)
    for i in range(length // BLK):
        rows = slice(i * BLK, (i + 1) * BLK)
        cc = jnp.dot(lower, rate[rows], precision=HIGH, preferred_element_type=F32)
        cc_ref[rows, :] = cc
        al_ref[rows, :] = jnp.exp2(cc)
        ew = jnp.exp2(jnp.minimum(cc[BLK - 1 : BLK, :] - cc, 0.0))
        ew_ref[rows, :] = ew
        wq_ref[rows, :] = ew * step[rows]
        cct_ref[:, rows] = cc.T[: cct_ref.shape[0]]


def mask_setup(segc_ref, mask_ref):
    seg = segc_ref[...]
    length = seg.shape[0]
    pos = iota((length, BLK), 0)
    segb = jnp.broadcast_to(seg, (length, BLK))
    for j in range(1, mask_ref.shape[0] + 1):
        prev = pltpu.roll(segb, j, axis=0)
        mask_ref[j - 1] = ((prev == segb) & (pos >= j)).astype(F32)


def conv_parts(x, taps_ref, lanes, mask_ref):
    kernel = mask_ref.shape[0] + 1
    shifts = [x] + [pltpu.roll(x, j, axis=0) * mask_ref[j - 1] for j in range(1, kernel)]
    pre = taps_ref[kernel : kernel + 1, lanes] + taps_ref[kernel - 1 : kernel, lanes] * x
    for j in range(1, kernel):
        pre = pre + taps_ref[kernel - 1 - j : kernel - j, lanes] * shifts[j]
    return shifts, pre


def sigmoid(x):
    return 0.5 * jnp.tanh(0.5 * x) + 0.5


def score_setup(bmat, cmat, segc_ref, segr_ref, sd_ref, so_ref, sdt_ref, sot_ref):
    length = bmat.shape[0]
    bb, cb = bmat.astype(BF16), cmat.astype(BF16)
    causal = iota((BLK, BLK), 0) >= iota((BLK, BLK), 1)
    for i in range(length // BLK):
        rows = slice(i * BLK, (i + 1) * BLK)
        before = slice((i - 1) * BLK, i * BLK)
        same = (segc_ref[rows, :] == segr_ref[:, rows]) & causal
        diag = jnp.where(same, mm_nt(cb[rows], bb[rows]), 0.0)
        if sd_ref is not None:
            sd_ref[i] = diag
        if sdt_ref is not None:
            sdt_ref[i] = diag.T
        if i > 0:
            linked = segc_ref[rows, :] == segr_ref[:, before]
            off = jnp.where(linked, mm_nt(cb[rows], bb[before]), 0.0)
            so_ref[i] = off.astype(BF16)
            if sot_ref is not None:
                sot_ref[i] = off.T.astype(BF16)


def pair_lanes(ref, shift, low):
    both = pltpu.roll(ref[...], shift, axis=1)
    return jnp.where(low, both[:, 0:1], both[:, 1:2])


def block_diag(x, low):
    zero = jnp.zeros_like(x)
    return jnp.concatenate([jnp.where(low, x, zero), jnp.where(low, zero, x)], axis=0)


def scan_fwd_kernel(pieces, *refs):
    w_refs = refs[:pieces]
    (
        xn_ref, taps_ref, segc_ref, segr_ref, heads_ref, skip_ref,
        ci_ref, dt_ref, sc_ref, yd_ref,
        step_ref, cc_ref, al_ref, ew_ref, wq_ref, cct_ref, mask_ref, sd_ref, so_ref,
    ) = refs[pieces:]
    t = pl.program_id(0)
    length = xn_ref.shape[0]
    channels = ci_ref.shape[1]
    states = BLK
    inner = channels - 2 * states

    @pl.when(t == 0)
    def _():
        xn = xn_ref[...]
        ci_ref[...] = mm(xn, rows_of(w_refs, slice(0, channels)))
        dt_ref[...] = mm(xn, rows_of(w_refs, slice(channels, channels + BLK)))
        head_setup(dt_ref[...], heads_ref, step_ref, cc_ref, al_ref, ew_ref, wq_ref, cct_ref)
        mask_setup(segc_ref, mask_ref)
        lanes_b = slice(inner, inner + states)
        lanes_c = slice(inner + states, channels)
        _, pre_b = conv_parts(ci_ref[:, lanes_b], taps_ref, lanes_b, mask_ref)
        _, pre_c = conv_parts(ci_ref[:, lanes_c], taps_ref, lanes_c, mask_ref)
        score_setup(
            pre_b * sigmoid(pre_b), pre_c * sigmoid(pre_c),
            segc_ref, segr_ref, sd_ref, so_ref, None, None,
        )

    lanes = pl.ds(pl.multiple_of(t * BLK, BLK), BLK)
    _, pre = conv_parts(ci_ref[:, lanes], taps_ref, lanes, mask_ref)
    v = pre * sigmoid(pre)
    low = iota((1, BLK), 1) < BLK // 2
    shift = lax.rem(BLK - 2 * t, BLK)
    vt = (v * pair_lanes(step_ref, shift, low)).astype(BF16)
    vp = (v * pair_lanes(wq_ref, shift, low)).astype(BF16)
    al2 = pair_lanes(al_ref, shift, low)
    c2 = pltpu.roll(cc_ref[...], shift, axis=1)
    r2 = pltpu.roll(cct_ref[...], lax.rem(cct_ref.shape[0] - 2 * t, cct_ref.shape[0]), axis=0)
    for i in range(length // BLK):
        rows = slice(i * BLK, (i + 1) * BLK)
        before = slice((i - 1) * BLK, i * BLK)
        ms = []
        for k in range(2):
            row = r2[k : k + 1, rows]
            d = jnp.exp2(jnp.minimum(c2[rows, k : k + 1] - row, 0.0))
            ms.append((sd_ref[i] * d).astype(BF16))
        yd = mm(jnp.concatenate(ms, axis=1), block_diag(vt[rows], low))
        yd_ref[rows, :] = yd
        y = yd + skip_ref[...] * v[rows]
        if i > 0:
            y = y + al2[rows] * mm(so_ref[i], vp[before])
        sc_ref[rows, :] = y


def mid_kernel(pieces, *refs):
    gw_refs, ow_refs = refs[:pieces], refs[pieces : 2 * pieces]
    (
        order_ref, xn_ref, sc_ref, gains_ref, cot_ref,
        lo_ref, hi_ref, g_ref, dgate_ref, mixed_ref, ginner_ref, wo_ref,
        gate_ref, dm_ref, nat_ref,
    ) = refs[2 * pieces :]
    devices = order_ref.shape[0]
    share = wo_ref.shape[0] // devices
    per = ow_refs[0].shape[0] // share
    gain = slice(xn_ref.shape[1], gains_ref.shape[1])
    inner = sc_ref.shape[1]
    width = cot_ref.shape[1]
    rows_in = xn_ref.shape[1] // devices
    xn = xn_ref[...]
    gate_ref[...] = mm(xn, rows_of(gw_refs))
    if share % 16:
        wo_ref[...] = rows_of(ow_refs)
    else:
        for p in range(devices):
            at = pl.multiple_of(order_ref[p] * share, 16)
            row = (p % per) * share
            wo_ref[pl.ds(at, share), :] = ow_refs[p // per][row : row + share, :]
    dm_ref[...] = mm_nt(cot_ref[...], wo_ref[...])
    length = xn_ref.shape[0]
    sub = 32
    ginner_ref[...] = jnp.zeros_like(ginner_ref)

    def body(k, carry):
        rows = pl.ds(pl.multiple_of(k * sub, sub), sub)
        gate = gate_ref[rows, :]
        sig = sigmoid(gate)
        silu = gate * sig
        scanned = sc_ref[rows, :]
        gated = scanned * silu
        scale = lax.rsqrt(jnp.mean(gated * gated, axis=-1, keepdims=True) + 1e-05)
        dm = dm_ref[rows, :]
        unit = gated * scale
        mixed_ref[rows, :] = (unit * gains_ref[:, gain]).astype(BF16)
        ginner_ref[...] += jnp.sum((dm * unit).reshape(sub // 8, 8, -1), axis=0)
        dunit = dm * gains_ref[:, gain]
        dot = jnp.mean(unit * dunit, axis=-1, keepdims=True)
        du = scale * (dunit - unit * dot)
        g_ref[rows, :] = du * silu
        dgate_ref[rows, :] = (du * scanned * (sig * (1.0 + gate * (1.0 - sig)))).astype(BF16)
        return carry

    lax.fori_loop(0, length // sub, body, 0)
    if rows_in % 8:
        lo_ref[...] = mm_tn(xn, dgate_ref[...]).astype(BF16)
        hi_ref[...] = mm_tn(mixed_ref[...], cot_ref[...]).astype(BF16)
        return
    gg = mm_tn(xn, dgate_ref[...]).astype(BF16)
    half = gg.shape[0] // 2
    lo_ref[:, :inner] = gg[:half]
    hi_ref[:, :inner] = gg[half:]
    nat_ref[...] = mm_tn(mixed_ref[...], cot_ref[...])
    for p in range(0, devices, 2):
        target = lo_ref if p < devices // 2 else hi_ref
        row = (p % (devices // 2)) * rows_in
        for k in range(2):
            both = [
                nat_ref[pl.ds(pl.multiple_of(order_ref[q] * share + k * rows_in, 8), rows_in), :]
                for q in (p, p + 1)
            ]
            lanes = slice(inner + k * width, inner + (k + 1) * width)
            target[row : row + 2 * rows_in, lanes] = jnp.concatenate(both, axis=0).astype(BF16)


def branch_kernel(mixed_ref, wo_ref, hid_ref, out_ref):
    out_ref[...] = (hid_ref[...].astype(F32) + mm(mixed_ref[...], wo_ref[...])).astype(BF16)


def conv_back(dpre, x, taps_ref, lanes, mask_ref, dtaps_ref, dp_ref, to):
    kernel = mask_ref.shape[0] + 1
    length = dpre.shape[0]

    def total(z):
        return jnp.sum(z, axis=0, keepdims=True)

    dtaps_ref[kernel : kernel + 1, to] = total(dpre)
    dtaps_ref[kernel - 1 : kernel, to] = total(dpre * x)
    dx = taps_ref[kernel - 1 : kernel, lanes] * dpre
    for j in range(1, kernel):
        masked = dpre * mask_ref[j - 1]
        tap = slice(kernel - 1 - j, kernel - j)
        dtaps_ref[tap, to] = total(masked * pltpu.roll(x, j, axis=0))
        dx = dx + taps_ref[tap, lanes] * pltpu.roll(masked, length - j, axis=0)
    dp_ref[:, to] = dx.astype(BF16)


def silu_and_slope(pre):
    sig = sigmoid(pre)
    return pre * sig, sig * (1.0 + pre * (1.0 - sig))


def scan_bwd_kernel(
    g_ref, yd_ref, ci_ref, dt_ref, taps_ref, segc_ref, segr_ref, heads_ref, skip_ref,
    dp_ref, dtaps_ref, dskip_ref, dheads_ref,
    step_ref, cc_ref, al_ref, ew_ref, wq_ref, cct_ref, mask_ref,
    sdt_ref, so_ref, sot_ref, dsdt_ref, dso_ref, acc_ref, dpre_ref,
):
    t = pl.program_id(0)
    length = ci_ref.shape[0]
    blocks = length // BLK
    channels = ci_ref.shape[1]
    states = BLK
    inner = channels - 2 * states
    nheads = inner // (BLK // 2)
    lanes_b = slice(inner, inner + states)
    lanes_c = slice(inner + states, channels)

    @pl.when(t == 0)
    def _():
        head_setup(dt_ref[...], heads_ref, step_ref, cc_ref, al_ref, ew_ref, wq_ref, cct_ref)
        mask_setup(segc_ref, mask_ref)
        dheads_ref[...] = jnp.zeros_like(dheads_ref)
        dtaps_ref[...] = jnp.zeros_like(dtaps_ref)
        _, pre_b = conv_parts(ci_ref[:, lanes_b], taps_ref, lanes_b, mask_ref)
        _, pre_c = conv_parts(ci_ref[:, lanes_c], taps_ref, lanes_c, mask_ref)
        score_setup(
            pre_b * sigmoid(pre_b), pre_c * sigmoid(pre_c),
            segc_ref, segr_ref, None, so_ref, sdt_ref, sot_ref,
        )
        dsdt_ref[...] = jnp.zeros_like(dsdt_ref)
        dso_ref[...] = jnp.zeros_like(dso_ref)
        acc_ref[...] = jnp.zeros_like(acc_ref)

    lanes = pl.ds(pl.multiple_of(t * BLK, BLK), BLK)
    x = ci_ref[:, lanes]
    _, pre = conv_parts(x, taps_ref, lanes, mask_ref)
    v, slope = silu_and_slope(pre)
    low = iota((1, BLK), 1) < BLK // 2
    shift = lax.rem(BLK - 2 * t, BLK)
    st2 = pair_lanes(step_ref, shift, low)
    wq2 = pair_lanes(wq_ref, shift, low)
    ew2 = pair_lanes(ew_ref, shift, low)
    al2 = pair_lanes(al_ref, shift, low)
    c2 = pltpu.roll(cc_ref[...], shift, axis=1)
    r2 = pltpu.roll(cct_ref[...], lax.rem(cct_ref.shape[0] - 2 * t, cct_ref.shape[0]), axis=0)
    vtb = (v * st2).astype(BF16)
    vpb = (v * wq2).astype(BF16)
    g = g_ref[...]
    gb = g.astype(BF16)
    gpb = (al2 * g).astype(BF16)
    dskip_ref[...] = jnp.sum(g * v, axis=0, keepdims=True)
    k_row = iota((4 * BLK, BLK), 0)
    target = jnp.where(k_row >= 2 * BLK, BLK // 2, 0) + 2 * t
    target = target + jnp.where((k_row & (BLK - 1)) >= BLK // 2, 1, 0)
    collect = (iota((4 * BLK, BLK), 1) == target).astype(F32).astype(BF16)
    for i in range(blocks):
        rows = slice(i * BLK, (i + 1) * BLK)
        before = slice((i - 1) * BLK, i * BLK)
        after = slice((i + 1) * BLK, (i + 2) * BLK)
        gdiag = block_diag(gb[rows], low)
        both = mm_nt(vtb[rows], gdiag)
        ms = []
        part = jnp.zeros((BLK, BLK), F32)
        for k in range(2):
            row = r2[k : k + 1, rows]
            d = jnp.exp2(jnp.minimum(row - c2[rows, k : k + 1], 0.0))
            ms.append((sdt_ref[i] * d).astype(BF16))
            part = part + both[:, k * BLK : (k + 1) * BLK] * d
        dsdt_ref[i] += part
        dvt = mm(jnp.concatenate(ms, axis=1), gdiag)
        x1 = gb[rows].astype(F32) * yd_ref[rows, :] - dvt * vtb[rows].astype(F32)
        dv = st2[rows] * dvt + skip_ref[...] * g[rows]
        dstep = dvt
        if i > 0:
            z = mm(so_ref[i], vpb[before])
            x1 = x1 + gpb[rows].astype(F32) * z
            dso_ref[i] += mm_nt(gpb[rows], vpb[before])
        if i + 1 < blocks:
            dvp = mm(sot_ref[i + 1], gpb[after])
            x1 = x1 - dvp * vpb[rows].astype(F32)
            dv = dv + wq2[rows] * dvp
            dstep = dstep + ew2[rows] * dvp
        h1, l1 = split2(x1)
        h2, l2 = split2(dstep * v[rows])
        acc_ref[rows, :] += mm(jnp.concatenate([h1, l1, h2, l2], axis=1), collect)
        dpre_ref[rows, :] = dv * slope[rows]
    conv_back(dpre_ref[...], x, taps_ref, lanes, mask_ref, dtaps_ref, dp_ref, lanes)

    @pl.when(t == pl.num_programs(0) - 1)
    def _():
        xb, xc = ci_ref[:, lanes_b], ci_ref[:, lanes_c]
        _, pre_b = conv_parts(xb, taps_ref, lanes_b, mask_ref)
        _, pre_c = conv_parts(xc, taps_ref, lanes_c, mask_ref)
        bmat, slope_b = silu_and_slope(pre_b)
        cmat, slope_c = silu_and_slope(pre_c)
        bb, cb = bmat.astype(BF16), cmat.astype(BF16)
        causal_t = iota((BLK, BLK), 1) >= iota((BLK, BLK), 0)
        upper = causal_t.astype(F32)
        dst, dso = [], [None]
        for i in range(blocks):
            rows = slice(i * BLK, (i + 1) * BLK)
            before = slice((i - 1) * BLK, i * BLK)
            same = (segc_ref[rows, :] == segr_ref[:, rows]) & causal_t
            dst.append(jnp.where(same, dsdt_ref[i], 0.0))
            if i > 0:
                linked = segc_ref[rows, :] == segr_ref[:, before]
                dso.append(jnp.where(linked, dso_ref[i], 0.0))
        for i in range(blocks):
            rows = slice(i * BLK, (i + 1) * BLK)
            before = slice((i - 1) * BLK, i * BLK)
            after = slice((i + 1) * BLK, (i + 2) * BLK)
            dc = mm(dst[i].T.astype(BF16), bb[rows])
            if i > 0:
                dc = dc + mm(dso[i].astype(BF16), bb[before])
            dpre_ref[rows, :] = dc * slope_c[rows]
        conv_back(dpre_ref[...], xc, taps_ref, lanes_c, mask_ref, dtaps_ref, dp_ref, lanes_c)
        for i in range(blocks):
            rows = slice(i * BLK, (i + 1) * BLK)
            after = slice((i + 1) * BLK, (i + 2) * BLK)
            db = mm(dst[i].astype(BF16), cb[rows])
            if i + 1 < blocks:
                db = db + mm(dso[i + 1].T.astype(BF16), cb[after])
            dpre_ref[rows, :] = db * slope_b[rows]
        conv_back(dpre_ref[...], xb, taps_ref, lanes_b, mask_ref, dtaps_ref, dp_ref, lanes_b)

        decay = jnp.exp(heads_ref[0:1, :])
        later = jnp.zeros((1, BLK), F32)
        dalog = jnp.zeros((1, BLK), F32)
        dbias = jnp.zeros((1, BLK), F32)
        for i in reversed(range(blocks)):
            rows = slice(i * BLK, (i + 1) * BLK)
            dcum = acc_ref[rows, :]
            drate = later + jnp.dot(upper, dcum, precision=HIGH, preferred_element_type=F32)
            later = drate[0:1, :]
            step = step_ref[rows, :]
            dalog = dalog - jnp.sum(drate * step, axis=0, keepdims=True) * decay
            dstep = pltpu.roll(dcum, BLK // 2, axis=1) - drate * decay
            ddt = dstep * sigmoid(dt_ref[rows, :] + heads_ref[2:3, :])
            dbias = dbias + jnp.sum(ddt, axis=0, keepdims=True)
            dp_ref[rows, channels:] = jnp.where(iota((1, BLK), 1) < nheads, ddt, 0.0).astype(BF16)
        dheads_ref[0:1, :] = dalog
        dheads_ref[1:2, :] = dbias


def grad_in_kernel(xn_ref, dp_ref, lo_ref, hi_ref):
    grad = mm_tn(xn_ref[...], dp_ref[...]).astype(BF16)
    half = grad.shape[0] // 2
    lo_ref[...] = grad[:half]
    hi_ref[...] = grad[half:]


def input_kernel(pieces, *refs):
    cw_refs, gw_refs = refs[:pieces], refs[pieces : 2 * pieces]
    (
        dp_ref, dgate_ref, dvec_ref, hid_ref, cot_ref, gains_ref,
        dtaps_ref, ginner_ref, dskip_ref, dheads_ref,
        ig_ref, sums_ref,
    ) = refs[2 * pieces :]
    dn = mm_nt(dp_ref[...], rows_of(cw_refs)) + mm_nt(dgate_ref[...], rows_of(gw_refs))
    perm = perm_matrix(dvec_ref[...], dn.shape[1])
    hi, lo = split2(dn)
    dn = mm_nt(hi, perm) + mm_nt(lo, perm)
    tokens = hid_ref[...].astype(F32)
    scale = lax.rsqrt(jnp.mean(tokens * tokens, axis=-1, keepdims=True) + 1e-05)
    unit = tokens * scale
    width = tokens.shape[1]
    sums_ref[...] = jnp.zeros_like(sums_ref)
    sums_ref[0:5, : dtaps_ref.shape[1]] = dtaps_ref[0:5, :]
    sums_ref[5:6, :width] = jnp.sum(dn * unit, axis=0, keepdims=True)
    sums_ref[5:6, width:] = jnp.sum(ginner_ref[...], axis=0, keepdims=True)
    sums_ref[6:7, : dskip_ref.shape[1]] = dskip_ref[...]
    sums_ref[7:8, :BLK] = dheads_ref[0:1, :]
    sums_ref[7:8, BLK : 2 * BLK] = dheads_ref[1:2, :]
    dunit = dn * gains_ref[:, :width]
    inner = jnp.mean(unit * dunit, axis=-1, keepdims=True)
    ig_ref[...] = cot_ref[...].astype(F32) + scale * (dunit - unit * inner)


def fold_kernel(count, *refs):
    total = refs[0][...].astype(F32)
    for ref in refs[1:count]:
        total = total + ref[...].astype(F32)
    size = total.shape[0] // len(refs[count:])
    for k, ref in enumerate(refs[count:]):
        ref[...] = total[k * size : (k + 1) * size].astype(ref.dtype)


def last_out_kernel(a_ref, b_ref, c_ref, d_ref, gate_ref, out_ref):
    total = a_ref[...].astype(F32) + b_ref[...].astype(F32) + c_ref[...].astype(F32) + d_ref[...].astype(F32)
    inner = gate_ref.shape[1]
    rows, width = a_ref.shape[0], out_ref.shape[1]
    gate_ref[...] = total[:, :inner]
    out_ref[:rows, :] = total[:, inner : inner + width]
    out_ref[rows:, :] = total[:, inner + width :]


def last_in_kernel(a_ref, b_ref, c_ref, d_ref, gate_ref, in_ref):
    total = a_ref[...].astype(F32) + b_ref[...].astype(F32) + c_ref[...].astype(F32) + d_ref[...].astype(F32)
    inner = gate_ref.shape[1]
    in_ref[:, :inner] = gate_ref[...]
    in_ref[:, inner:] = total[:, : in_ref.shape[1] - inner]


def sds(shape, dtype):
    return jax.ShapeDtypeStruct(shape, dtype)


PARAMS = dict(compiler_params=pltpu.CompilerParams(vmem_limit_bytes=60 * 1024 * 1024))


def head_scratch(length, inner):
    nheads = -(-2 * inner // (8 * BLK)) * 8
    return [pltpu.VMEM((length, BLK), F32)] * 5 + [pltpu.VMEM((nheads, length), F32)]


def full(shape):
    return pl.BlockSpec(shape, lambda t: (0,) * len(shape))


def tile(rows):
    return pl.BlockSpec((rows, BLK), lambda t: (0, t))


def scan_fwd(weights, xn, taps, segc, segr, heads, skip_row):
    length = xn.shape[0]
    channels, inner = taps.shape[1], skip_row.shape[1]
    kernel = 4
    blocks = length // BLK
    ins = tuple(weights) + (xn, taps, segc, segr, heads, skip_row)
    count = len(weights)
    return pl.pallas_call(
        lambda *refs: scan_fwd_kernel(count, *refs),
        grid=(inner // BLK,),
        in_specs=[full(a.shape) for a in ins[:-1]] + [tile(1)],
        out_specs=[full((length, channels)), full((length, BLK)), tile(length), tile(length)],
        out_shape=[
            sds((length, channels), F32), sds((length, BLK), F32),
            sds((length, inner), F32), sds((length, inner), F32),
        ],
        scratch_shapes=head_scratch(length, inner) + [
            pltpu.VMEM((kernel - 1, length, BLK), F32),
            pltpu.VMEM((blocks, BLK, BLK), F32),
            pltpu.VMEM((blocks, BLK, BLK), BF16),
        ],
        name="scan_fwd",
        **PARAMS,
    )(*ins)


def scan_bwd(g, yd, ci, dt, taps, segc, segr, heads, skip_row):
    length, channels = ci.shape
    inner = skip_row.shape[1]
    kernel = 4
    blocks = length // BLK
    ins = (g, yd, ci, dt, taps, segc, segr, heads, skip_row)
    score = (blocks, BLK, BLK)
    return pl.pallas_call(
        scan_bwd_kernel,
        grid=(inner // BLK,),
        in_specs=[tile(length), tile(length)] + [full(a.shape) for a in ins[2:8]] + [tile(1)],
        out_specs=[full((length, channels + BLK)), full(taps.shape), tile(1), full((8, BLK))],
        out_shape=[
            sds((length, channels + BLK), BF16), sds(taps.shape, F32), sds((1, inner), F32), sds((8, BLK), F32),
        ],
        scratch_shapes=head_scratch(length, inner) + [
            pltpu.VMEM((kernel - 1, length, BLK), F32),
            pltpu.VMEM(score, F32),
            pltpu.VMEM(score, BF16),
            pltpu.VMEM(score, BF16),
            pltpu.VMEM(score, F32),
            pltpu.VMEM(score, F32),
            pltpu.VMEM((length, BLK), F32),
            pltpu.VMEM((length, BLK), F32),
        ],
        name="scan_bwd",
        **PARAMS,
    )(*ins)


def prep(at, taps_n, hidden, dvec, owner, where, pieces, channels, width):
    ins = (hidden, dvec, owner, where) + tuple(pieces)
    last = pieces[0].shape[1] // BLK - 1
    outs = (sds(hidden.shape, BF16), sds((8, channels), F32), sds((1, width), F32))
    return pl.pallas_call(
        lambda *refs: prep_kernel(at, taps_n, *refs),
        grid=(1,),
        in_specs=[full(a.shape) for a in ins[:4]]
        + [pl.BlockSpec((a.shape[0], BLK), lambda t: (0, last)) for a in pieces],
        out_specs=[full(a.shape) for a in outs],
        out_shape=outs,
        name="prep",
        **PARAMS,
    )(*ins)


def call(kernel, outs, *ins, scratch=(), scalar=None):
    specs = [
        pl.BlockSpec(memory_space=pltpu.SMEM if k == scalar else pltpu.VMEM) for k in range(len(ins))
    ]
    return pl.pallas_call(
        kernel, out_shape=outs, in_specs=specs, scratch_shapes=list(scratch), **PARAMS
    )(*ins)


def stages(devices):
    masks = [1 << b for b in range(devices.bit_length() - 1)]
    groups = []
    for end in range(len(masks), 1, -2):
        part = masks[max(end - 2, 1) : end]
        groups.append(part if len(part) == 1 else [part[0], part[1], part[0] | part[1]])
    return groups + [masks[:1]]


def order_table(devices):
    table = np.zeros((1,), np.int32)
    for group in stages(devices):
        table = np.concatenate([table] + [table ^ m for m in group])
    return table


def send(x, devices, mask):
    return lax.ppermute(x, "fsdp", [(i, i ^ mask) for i in range(devices)])


def send_all(parts, devices, stage):
    return [send(part, devices, m) for part, m in zip(parts, stages(devices)[stage])]


def gather(x, devices):
    groups = stages(devices)
    core = len(groups) - 1
    pieces = [x]
    for stage in range(core):
        x = pieces[0] if len(pieces) == 1 else jnp.concatenate(pieces, axis=0)
        pieces = [x] + send_all([x] * len(groups[stage]), devices, stage)
    return pieces + [send(a, devices, 1) for a in pieces]


def fold(parts, fan, dtype):
    rows, cols = parts[0].shape
    size = rows // fan
    if size % 8:
        total = sum(part.astype(F32) for part in parts).astype(dtype)
        return [total[k * size : (k + 1) * size] for k in range(fan)]
    count = len(parts)
    return call(
        lambda *refs: fold_kernel(count, *refs), tuple(sds((size, cols), dtype) for _ in range(fan)), *parts
    )


def reduce_shares(lo, hi, devices):
    groups = stages(devices)
    parts = [lo, hi]
    for stage in reversed(range(len(groups))):
        parts = [parts[0]] + send_all(parts[1:], devices, stage)
        if stage:
            parts = fold(parts, len(groups[stage - 1]) + 1, BF16)
    return parts


def total_of(x, devices):
    for stage in reversed(range(len(stages(devices)))):
        group = stages(devices)[stage]
        got = send_all([x] * len(group), devices, stage)
        x = x + got[0] if len(got) == 1 else (x + got[0]) + (got[1] + got[2])
    return x


def layer(
    hidden, segment_ids, cot, w_in, w_out, conv_taps, gains, a_log, d_skip, dt_bias
):
    length = segment_ids.shape[1]
    width = hidden.shape[1]
    devices = lax.axis_size("fsdp")
    me = lax.axis_index("fsdp")
    nheads = a_log.shape[0]
    taps_n, tap_share = conv_taps.shape
    channels = tap_share * devices
    gain_share = gains.shape[0]
    inner = w_out.shape[0] * devices
    proj = w_in.shape[1]
    rows_in, rows_out = w_in.shape[0], w_out.shape[0]

    table = order_table(devices)
    inverse = np.argsort(table).astype(np.int32)
    order = jnp.asarray(table) ^ me
    place = jnp.asarray(inverse)[me ^ jnp.arange(devices)]
    dvec = (order[:, None] * rows_in + jnp.arange(rows_in)[None, :]).reshape(1, width)

    spare = BLK - (proj - inner - channels)
    packed = rows_in > taps_n and max(tap_share, gain_share) <= spare
    small = jnp.zeros((rows_in if packed else 8, BLK if not packed else spare), BF16)
    small = small.at[:taps_n, :tap_share].set(conv_taps)
    small = small.at[taps_n, :gain_share].set(gains)
    if packed:
        w_conv = jnp.concatenate([w_in[:, inner:], small], axis=1)
    else:
        w_conv = jnp.pad(w_in[:, inner:], ((0, 0), (0, spare)))
    cw = gather(w_conv, devices)
    gw = gather(w_in[:, :inner], devices)
    ow = gather(w_out, devices)
    count = len(cw)

    heads = jnp.zeros((8, BLK), F32)
    heads = heads.at[0, :nheads].set(a_log).at[1, :nheads].set(d_skip).at[2, :nheads].set(dt_bias)
    skip_row = jnp.repeat(d_skip, inner // nheads)[None]
    segc = segment_ids.reshape(length, 1)

    if packed:
        at = np.arange(width + inner)
        where = np.stack([at % tap_share, at // tap_share, at % gain_share, at // gain_share])
        where = jnp.asarray(np.pad(where, ((0, 4), (0, 0))).astype(np.int32))
        xn, taps, gains_all = prep(
            proj - inner - channels, taps_n, hidden, dvec, order.reshape(devices, 1), where, cw,
            channels, width + inner,
        )
    else:
        rows = jnp.concatenate(gather(small.astype(F32)[None], devices), axis=0)[place]
        taps = jnp.moveaxis(rows[:, :, :tap_share], 0, 1).reshape(8, channels)
        gains_all = rows[:, taps_n, :gain_share].reshape(1, width + inner)
        xn = call(norm_kernel, sds((length, width), BF16), hidden, gains_all, dvec)
    ci, dt, sc, yd = scan_fwd(cw, xn, taps, segc, segment_ids, heads, skip_row)
    if rows_out % 16:
        wo_all = jnp.concatenate(ow, axis=0).reshape(devices, rows_out, width)[place].reshape(inner, width)
        ow = [wo_all[k * (inner // count) : (k + 1) * (inner // count)] for k in range(count)]
    aligned = rows_in % 8 == 0
    if aligned:
        halves = (sds((width // 2, inner + 2 * width), BF16), sds((width // 2, inner + 2 * width), BF16))
    else:
        halves = (sds((width, inner), BF16), sds((inner, width), BF16))
    lo, hi, g, dgate, mixed, ginner, wo = call(
        lambda *refs: mid_kernel(count, *refs),
        halves + (
            sds((length, inner), F32), sds((length, inner), BF16), sds((length, inner), BF16),
            sds((8, inner), F32), sds((inner, width), BF16),
        ),
        *gw, *ow, order, xn, sc, gains_all, cot,
        scratch=(
            pltpu.VMEM((length, inner), F32), pltpu.VMEM((length, inner), F32),
            pltpu.VMEM((inner, width), F32),
        ),
        scalar=2 * count,
    )
    if not aligned:
        gwo = hi.reshape(devices, 2, rows_in, width)[order]
        both = jnp.concatenate([lo, gwo[:, 0].reshape(width, width), gwo[:, 1].reshape(width, width)], axis=1)
        lo, hi = both[: width // 2], both[width // 2 :]
    mid_parts = reduce_shares(lo, hi, devices)
    output = call(branch_kernel, sds((length, width), BF16), mixed, wo, hidden)
    dp, dtaps, dskip, dheads = scan_bwd(g, yd, ci, dt, taps, segc, segment_ids, heads, skip_row)
    half = sds((width // 2, dp.shape[1]), BF16)
    clo, chi = call(grad_in_kernel, (half, half), xn, dp)
    conv_parts_in = reduce_shares(clo, chi, devices)
    input_grad, sums = call(
        lambda *refs: input_kernel(count, *refs),
        (sds((length, width), F32), sds((8, width + inner), F32)),
        *cw, *gw, dp, dgate, dvec, hidden, cot, gains_all, dtaps, ginner, dskip, dheads,
    )
    if aligned and len(mid_parts) == 4:
        gate_share, out_share = call(
            last_out_kernel,
            (sds((rows_in, inner), F32), sds((rows_out, width), F32)), *mid_parts,
        )
        in_share = call(last_in_kernel, sds((rows_in, proj), F32), *conv_parts_in, gate_share)
    else:
        total = sum(part.astype(F32) for part in mid_parts)
        out_share = jnp.concatenate([total[:, inner : inner + width], total[:, inner + width :]], axis=0)
        conv_total = sum(part.astype(F32) for part in conv_parts_in)
        in_share = jnp.concatenate([total[:, :inner], conv_total], axis=1)[:, :proj]

    sums = total_of(sums, devices)
    taps_share = lax.dynamic_slice_in_dim(sums[:taps_n, :channels], me * tap_share, tap_share, axis=1)
    gains_share = lax.dynamic_slice_in_dim(sums[5], me * gain_share, gain_share)
    return (
        output, input_grad, in_share, out_share, taps_share, gains_share,
        sums[7, :nheads], sums[6, :inner].reshape(nheads, -1).sum(axis=1), sums[7, BLK : BLK + nheads],
    )


def solution(mesh):
    axis = P("fsdp")
    rows = P("fsdp", None)
    cols = P(None, "fsdp")
    return jax.shard_map(
        layer,
        mesh=mesh,
        in_specs=(rows, rows, rows, rows, rows, cols, axis, P(), P(), P()),
        out_specs=(rows, rows, rows, rows, cols, axis, P(), P(), P()),
        check_vma=False,
    )
```

profile of v0, /device:TPU:0, one launch (start us, length us, event | category | flops | bytes accessed | tf_op | source)
XLA Modules:
  0.0 267.4 jit_solution(2319875557715133048)
XLA Ops:
  3.1 3.1 %collective-permute-start.20 = (bf16[24,1920]{1,0:T(8,128)(2,1)S(1)}, bf16[24,1920]{1,0:T(8,128)(2,1)S(1)}, u32[]{:S(2)}, u32[]{:S(2)}) collective-permute-start(bf16[24,1920]{1,0:T(8,128)(2,1)S(1)} %pad_maximum_fusion.2), channel_id=1, source_target_pairs={{0,8},{1,9},{2,10},{3,11},{4,12},{5,13},{6,14},{7,15},{8,0},{9,1},... | collective-permute-start | bytes 276488 | tf_op jit(solution)/shard_map/ppermute | solution.py:626
  6.2 2.6 collective-permute-start.21
  10.1 3.9 %collective-permute-start.2 = (bf16[24,1536]{1,0:T(8,128)(2,1)S(1)}, bf16[24,1536]{1,0:T(8,128)(2,1)S(1)}, u32[]{:S(2)}, u32[]{:S(2)}) collective-permute-start(bf16[24,1536]{1,0:T(8,128)(2,1)S(1)} %slice.114), channel_id=1, source_target_pairs={{0,24},{1,25},{2,26},{3,27},{4,28},{5,29},{6,30},{7,31},{8,16},{9,... | collective-permute-start | bytes 221192 | tf_op jit(solution)/shard_map/ppermute | solution.py:626
  16.1 3.8 %collective-permute-done.1 = bf16[24,1536]{1,0:T(8,128)(2,1)S(1)} collective-permute-done((bf16[24,1536]{1,0:T(8,128)(2,1)S(1)}, bf16[24,1536]{1,0:T(8,128)(2,1)S(1)}, u32[]{:S(2)}, u32[]{:S(2)}) %collective-permute-start.1) | collective-permute-done | bytes 73760 | tf_op jit(solution)/shard_map/ppermute | solution.py:626
  19.8 4.0 %collective-permute-start.11 = (bf16[48,768]{1,0:T(8,128)(2,1)}, bf16[48,768]{1,0:T(8,128)(2,1)S(1)}, u32[]{:S(2)}, u32[]{:S(2)}) collective-permute-start(bf16[48,768]{1,0:T(8,128)(2,1)} %param.26), channel_id=1, source_target_pairs={{0,16},{1,17},{2,18},{3,19},{4,20},{5,21},{6,22},{7,23},{8,24},{9,... | collective-permute-start | bytes 221192 | tf_op jit(solution)/shard_map/ppermute | solution.py:626
  26.4 2.9 %collective-permute-start.12 = (bf16[48,768]{1,0:T(8,128)(2,1)}, bf16[48,768]{1,0:T(8,128)(2,1)S(1)}, u32[]{:S(2)}, u32[]{:S(2)}) collective-permute-start(bf16[48,768]{1,0:T(8,128)(2,1)} %param.26), channel_id=1, source_target_pairs={{0,24},{1,25},{2,26},{3,27},{4,28},{5,29},{6,30},{7,31},{8,16},{9,... | collective-permute-start | bytes 221192 | tf_op jit(solution)/shard_map/ppermute | solution.py:626
  29.3 3.6 %collective-permute-done.12 = bf16[48,768]{1,0:T(8,128)(2,1)S(1)} collective-permute-done((bf16[48,768]{1,0:T(8,128)(2,1)}, bf16[48,768]{1,0:T(8,128)(2,1)S(1)}, u32[]{:S(2)}, u32[]{:S(2)}) %collective-permute-start.12) | collective-permute-done | bytes 73760 | tf_op jit(solution)/shard_map/ppermute | solution.py:626
  38.0 9.9 %collective-permute-done.4.refs_2_.refs_10_ = bf16[96,1536]{1,0:T(8,128)(2,1)} collective-permute-done((bf16[96,1536]{1,0:T(8,128)(2,1)S(1)}, bf16[96,1536]{1,0:T(8,128)(2,1)}, u32[]{:S(2)}, u32[]{:S(2)}) %collective-permute-start.4) | collective-permute-done | bytes 294944 | tf_op jit(solution)/shard_map/ppermute | solution.py:626
  52.8 2.2 collective-permute-done.14.refs_10_
  55.0 15.6 %collective-permute-done.15.refs_11_ = bf16[192,768]{1,0:T(8,128)(2,1)S(1)} collective-permute-done((bf16[192,768]{1,0:T(8,128)(2,1)S(1)}, bf16[192,768]{1,0:T(8,128)(2,1)S(1)}, u32[]{:S(2)}, u32[]{:S(2)}) %collective-permute-start.15) | collective-permute-done | bytes 294944 | tf_op jit(solution)/shard_map/ppermute | solution.py:626
  71.0 2.9 %collective-permute-done.24.refs_6_.refs_2_ = bf16[96,1920]{1,0:T(8,128)(2,1)S(1)} collective-permute-done((bf16[96,1920]{1,0:T(8,128)(2,1)S(1)}, bf16[96,1920]{1,0:T(8,128)(2,1)S(1)}, u32[]{:S(2)}, u32[]{:S(2)}) %collective-permute-start.24) | collective-permute-done | bytes 368672 | tf_op jit(solution)/shard_map/ppermute | solution.py:626
  85.6 4.1 %prep.1 = (bf16[512,768]{1,0:T(8,128)(2,1)}, f32[8,1792]{1,0:T(8,128)}, f32[1,2304]{1,0:T(1,128)}) custom-call(bf16[512,768]{1,0:T(8,128)(2,1)} %refs_19_.1, s32[1,768]{1,0:T(1,128)} %add.67.refs_1_.refs_18_, s32[32,1]{1,0:T(8,128)} %copy.22.refs_2_, s32[8,2304]{1,0:T(8,128)} %constant.157.clone.refs_3_, bf16[96,1920]{1,0:T(8,128)(2,1)} %copy-done, ...), custom_call_target="tpu_custom_call" | custom-call | tf_op jit(solution)/shard_map/prep/pallas_call | solution.py:588
  89.7 21.1 %scan_fwd.1 = (f32[512,1792]{1,0:T(8,128)}, f32[512,128]{1,0:T(8,128)}, f32[512,1536]{1,0:T(8,128)}, f32[512,1536]{1,0:T(8,128)}) custom-call(bf16[96,1920]{1,0:T(8,128)(2,1)} %copy-done, bf16[96,1920]{1,0:T(8,128)(2,1)} %copy-done.1, bf16[96,1920]{1,0:T(8,128)(2,1)} %copy-done.2, bf16[96,1920]{1,0:T(8,128)(2,1)} %copy-done.3, bf16[96,1920]{1,0:T(8,128)(2,1)} %copy-done.4, ...), custom_call_target="tpu_custom_call" | custom-call | tf_op jit(solution)/shard_map/scan_fwd/pallas_call | solution.py:535
  110.8 18.7 %shard_map.187 = (bf16[384,3072]{1,0:T(8,128)(2,1)}, bf16[384,3072]{1,0:T(8,128)(2,1)}, f32[512,1536]{1,0:T(8,128)}, bf16[512,1536]{1,0:T(8,128)(2,1)}, bf16[512...) custom-call(bf16[96,1536]{1,0:T(8,128)(2,1)} %copy-done.8, bf16[96,1536]{1,0:T(8,128)(2,1)} %copy-done.10, ...), custom_call_target="tpu_custom_call" | custom-call | tf_op jit(solution)/shard_map/pallas_call | solution.py:604
  129.8 29.4 %scan_bwd.1 = (bf16[512,1920]{1,0:T(8,128)(2,1)}, f32[8,1792]{1,0:T(8,128)}, f32[1,1536]{1,0:T(1,128)}, f32[8,128]{1,0:T(8,128)}) custom-call(f32[512,1536]{1,0:T(8,128)} %get-tuple-element.115.g_ref, f32[512,1536]{1,0:T(8,128)} %get-tuple-element.116.yd_ref, f32[512,1792]{1,0:T(8,128)} %get-tuple-element.117.ci_ref, f32[512,128]{1,0:T(8,128)} %get-tuple-element.118.dt_ref, ...), custom_call_target="tpu_custom_call" | custom-call | tf_op jit(solution)/shard_map/scan_bwd/pallas_call | solution.py:561
  159.2 5.1 %shard_map.190 = (bf16[384,1920]{1,0:T(8,128)(2,1)}, bf16[384,1920]{1,0:T(8,128)(2,1)}) custom-call(bf16[512,768]{1,0:T(8,128)(2,1)} %get-tuple-element.109.refs_8_.refs_17_.xn_ref, bf16[512,1920]{1,0:T(8,128)(2,1)} %get-tuple-element.119.refs_16_.dp_ref), custom_call_target="tpu_custom_call" | custom-call | tf_op jit(solution)/shard_map/pallas_call | solution.py:604
  164.7 11.9 %shard_map.189 = (f32[512,768]{1,0:T(8,128)}, f32[8,2304]{1,0:T(8,128)}) custom-call(bf16[96,1920]{1,0:T(8,128)(2,1)} %copy-done, bf16[96,1920]{1,0:T(8,128)(2,1)} %copy-done.1, bf16[96,1920]{1,0:T(8,128)(2,1)} %copy-done.2, bf16[96,1920]{1,0:T(8,128)(2,1)} %copy-done.3, bf16[96,1920]{1,0:T(8,128)(2,1)} %copy-done.4, bf16[96,1920]{1,0:T(8,128)(2,1)} %copy-done.5, ...), custom_call_target="tpu_custom_call" | custom-call | tf_op jit(solution)/shard_map/pallas_call | solution.py:604
  184.9 2.4 collective-permute-done.47
  187.4 2.1 collective-permute-start.49
  189.5 2.3 collective-permute-start.50
  191.8 4.6 %shard_map.188 = bf16[512,768]{1,0:T(8,128)(2,1)} custom-call(bf16[512,1536]{1,0:T(8,128)(2,1)} %get-tuple-element.113.mixed_ref, bf16[1536,768]{1,0:T(8,128)(2,1)} %get-tuple-element.114.wo_ref, bf16[512,768]{1,0:T(8,128)(2,1)} %refs_19_.1), custom_call_target="tpu_custom_call" | custom-call | tf_op jit(solution)/shard_map/pallas_call | solution.py:604
  196.4 3.0 %shard_map.191 = (bf16[96,1920]{1,0:T(8,128)(2,1)}, bf16[96,1920]{1,0:T(8,128)(2,1)}, bf16[96,1920]{1,0:T(8,128)(2,1)}, bf16[96,1920]{1,0:T(8,128)(2,1)}) custom-call(bf16[384,1920]{1,0:T(8,128)(2,1)} %get-tuple-element.126.refs_0_, bf16[384,1920]{1,0:T(8,128)(2,1)} %collective-permute-done.30.refs_1_), custom_call_target="tpu_custom_call" | custom-call | tf_op jit(solution)/shard_map/pallas_call | solution.py:604
  201.4 4.0 %shard_map.193 = (bf16[96,3072]{1,0:T(8,128)(2,1)}, bf16[96,3072]{1,0:T(8,128)(2,1)}, bf16[96,3072]{1,0:T(8,128)(2,1)}, bf16[96,3072]{1,0:T(8,128)(2,1)}) custom-call(bf16[384,3072]{1,0:T(8,128)(2,1)} %get-tuple-element.136.refs_0_, bf16[384,3072]{1,0:T(8,128)(2,1)} %copy-done.9), custom_call_target="tpu_custom_call" | custom-call | tf_op jit(solution)/shard_map/pallas_call | solution.py:604
  210.5 12.0 %collective-permute-done.38.refs_1_ = bf16[96,3072]{1,0:T(8,128)(2,1)S(1)} collective-permute-done((bf16[96,3072]{1,0:T(8,128)(2,1)}, bf16[96,3072]{1,0:T(8,128)(2,1)S(1)}, u32[]{:S(2)}, u32[]{:S(2)}) %collective-permute-start.38) | collective-permute-done | bytes 589856 | tf_op jit(solution)/shard_map/ppermute | solution.py:626
  223.9 19.9 %collective-permute-done.39.refs_2_ = bf16[96,3072]{1,0:T(8,128)(2,1)S(1)} collective-permute-done((bf16[96,3072]{1,0:T(8,128)(2,1)}, bf16[96,3072]{1,0:T(8,128)(2,1)S(1)}, u32[]{:S(2)}, u32[]{:S(2)}) %collective-permute-start.39) | collective-permute-done | bytes 589856 | tf_op jit(solution)/shard_map/ppermute | solution.py:626
  244.8 2.5 shard_map.194
  247.4 2.2 collective-permute-start.42
  249.6 2.3 collective-permute-start.43
  254.1 2.1 shard_map.192
  256.3 2.1 collective-permute-start.35
  258.4 2.3 collective-permute-start.36
  261.9 1.9 shard_map.195
  (177 shorter events, 56.1 us)
Async XLA Ops:
  3.1 31.2 %collective-permute-start.20 = (bf16[24,1920]{1,0:T(8,128)(2,1)S(1)}, bf16[24,1920]{1,0:T(8,128)(2,1)S(1)}, u32[]{:S(2)}, u32[]{:S(2)}) collective-permute-start(bf16[24,1920]{1,0:T(8,128)(2,1)S(1)} %pad_maximum_fusion.2), channel_id=1, source_target_pairs={{0,8},{1,9},{2,10},{3,11},{4,12},{5,13},{6,14},{7,15},{8,0},{9,1},... | collective-permute-start | bytes 276488 | tf_op jit(solution)/shard_map/ppermute | solution.py:626
  6.2 29.6 %collective-permute-start.21 = (bf16[24,1920]{1,0:T(8,128)(2,1)S(1)}, bf16[24,1920]{1,0:T(8,128)(2,1)S(1)}, u32[]{:S(2)}, u32[]{:S(2)}) collective-permute-start(bf16[24,1920]{1,0:T(8,128)(2,1)S(1)} %pad_maximum_fusion.2), channel_id=1, source_target_pairs={{0,16},{1,17},{2,18},{3,19},{4,20},{5,21},{6,22},{7,23},{8,24},{9,... | collective-permute-start | bytes 276488 | tf_op jit(solution)/shard_map/ppermute | solution.py:626
  14.9 20.9 %collective-permute-start.22 = (bf16[24,1920]{1,0:T(8,128)(2,1)S(1)}, bf16[24,1920]{1,0:T(8,128)(2,1)S(1)}, u32[]{:S(2)}, u32[]{:S(2)}) collective-permute-start(bf16[24,1920]{1,0:T(8,128)(2,1)S(1)} %pad_maximum_fusion.2), channel_id=1, source_target_pairs={{0,24},{1,25},{2,26},{3,27},{4,28},{5,29},{6,30},{7,31},{8,16},{9,... | collective-permute-start | bytes 276488 | tf_op jit(solution)/shard_map/ppermute | solution.py:626
  24.6 11.9 %collective-permute-start.3 = (bf16[96,1536]{1,0:T(8,128)(2,1)S(1)}, bf16[96,1536]{1,0:T(8,128)(2,1)S(1)}, u32[]{:S(2)}, u32[]{:S(2)}) collective-permute-start(bf16[96,1536]{1,0:T(8,128)(2,1)S(1)} %pad_maximum_fusion.1.refs_0_.refs_8_), channel_id=1, source_target_pairs={{0,2},{1,3},{2,0},{3,1},{4,6},{5,7},{6,4},{7,5},{8,10},{9,11},{10,... | collective-permute-start | bytes 884744 | tf_op jit(solution)/shard_map/ppermute | solution.py:626
  32.8 15.0 %collective-permute-start.4 = (bf16[96,1536]{1,0:T(8,128)(2,1)S(1)}, bf16[96,1536]{1,0:T(8,128)(2,1)}, u32[]{:S(2)}, u32[]{:S(2)}) collective-permute-start(bf16[96,1536]{1,0:T(8,128)(2,1)S(1)} %pad_maximum_fusion.1.refs_0_.refs_8_), channel_id=1, source_target_pairs={{0,4},{1,5},{2,6},{3,7},{4,0},{5,1},{6,2},{7,3},{8,12},{9,13},{10,... | collective-permute-start | bytes 884744 | tf_op jit(solution)/shard_map/ppermute | solution.py:626
  34.3 15.0 %collective-permute-start.5 = (bf16[96,1536]{1,0:T(8,128)(2,1)S(1)}, bf16[96,1536]{1,0:T(8,128)(2,1)}, u32[]{:S(2)}, u32[]{:S(2)}) collective-permute-start(bf16[96,1536]{1,0:T(8,128)(2,1)S(1)} %pad_maximum_fusion.1.refs_0_.refs_8_), channel_id=1, source_target_pairs={{0,6},{1,7},{2,4},{3,5},{4,2},{5,3},{6,0},{7,1},{8,14},{9,15},{10,... | collective-permute-start | bytes 884744 | tf_op jit(solution)/shard_map/ppermute | solution.py:626
  35.8 14.1 %collective-permute-start.6 = (bf16[96,1536]{1,0:T(8,128)(2,1)S(1)}, bf16[96,1536]{1,0:T(8,128)(2,1)}, u32[]{:S(2)}, u32[]{:S(2)}) collective-permute-start(bf16[96,1536]{1,0:T(8,128)(2,1)S(1)} %pad_maximum_fusion.1.refs_0_.refs_8_), channel_id=1, source_target_pairs={{0,1},{1,0},{2,3},{3,2},{4,5},{5,4},{6,7},{7,6},{8,9},{9,8},{10,11... | collective-permute-start | bytes 884744 | tf_op jit(solution)/shard_map/ppermute | solution.py:626
  35.8 15.5 %collective-permute-start.13 = (bf16[192,768]{1,0:T(8,128)(2,1)S(1)}, bf16[192,768]{1,0:T(8,128)(2,1)S(1)}, u32[]{:S(2)}, u32[]{:S(2)}) collective-permute-start(bf16[192,768]{1,0:T(8,128)(2,1)S(1)} %constant_dynamic-update-slice_fusion.refs_8_), channel_id=1, source_target_pairs={{0,2},{1,3},{2,0},{3,1},{4,6},{5,7},{6,4},{7,5},{8,10},{9,11},{10,... | collective-permute-start | bytes 884744 | tf_op jit(solution)/shard_map/ppermute | solution.py:626
  36.4 18.5 %collective-permute-start.14 = (bf16[192,768]{1,0:T(8,128)(2,1)S(1)}, bf16[192,768]{1,0:T(8,128)(2,1)S(1)}, u32[]{:S(2)}, u32[]{:S(2)}) collective-permute-start(bf16[192,768]{1,0:T(8,128)(2,1)S(1)} %constant_dynamic-update-slice_fusion.refs_8_), channel_id=1, source_target_pairs={{0,4},{1,5},{2,6},{3,7},{4,0},{5,1},{6,2},{7,3},{8,12},{9,13},{10,... | collective-permute-start | bytes 884744 | tf_op jit(solution)/shard_map/ppermute | solution.py:626
  47.8 22.7 %collective-permute-start.23 = (bf16[96,1920]{1,0:T(8,128)(2,1)S(1)}, bf16[96,1920]{1,0:T(8,128)(2,1)S(1)}, u32[]{:S(2)}, u32[]{:S(2)}) collective-permute-start(bf16[96,1920]{1,0:T(8,128)(2,1)S(1)} %pad_maximum_fusion.refs_4_.refs_0_), channel_id=1, source_target_pairs={{0,2},{1,3},{2,0},{3,1},{4,6},{5,7},{6,4},{7,5},{8,10},{9,11},{10,... | collective-permute-start | bytes 1105928 | tf_op jit(solution)/shard_map/ppermute | solution.py:626
  49.3 24.6 %collective-permute-start.24 = (bf16[96,1920]{1,0:T(8,128)(2,1)S(1)}, bf16[96,1920]{1,0:T(8,128)(2,1)S(1)}, u32[]{:S(2)}, u32[]{:S(2)}) collective-permute-start(bf16[96,1920]{1,0:T(8,128)(2,1)S(1)} %pad_maximum_fusion.refs_4_.refs_0_), channel_id=1, source_target_pairs={{0,4},{1,5},{2,6},{3,7},{4,0},{5,1},{6,2},{7,3},{8,12},{9,13},{10,... | collective-permute-start | bytes 1105928 | tf_op jit(solution)/shard_map/ppermute | solution.py:626
  49.8 24.1 %collective-permute-start.25 = (bf16[96,1920]{1,0:T(8,128)(2,1)S(1)}, bf16[96,1920]{1,0:T(8,128)(2,1)S(1)}, u32[]{:S(2)}, u32[]{:S(2)}) collective-permute-start(bf16[96,1920]{1,0:T(8,128)(2,1)S(1)} %pad_maximum_fusion.refs_4_.refs_0_), channel_id=1, source_target_pairs={{0,6},{1,7},{2,4},{3,5},{4,2},{5,3},{6,0},{7,1},{8,14},{9,15},{10,... | collective-permute-start | bytes 1105928 | tf_op jit(solution)/shard_map/ppermute | solution.py:626
  51.3 19.2 %collective-permute-start.15 = (bf16[192,768]{1,0:T(8,128)(2,1)S(1)}, bf16[192,768]{1,0:T(8,128)(2,1)S(1)}, u32[]{:S(2)}, u32[]{:S(2)}) collective-permute-start(bf16[192,768]{1,0:T(8,128)(2,1)S(1)} %constant_dynamic-update-slice_fusion.refs_8_), channel_id=1, source_target_pairs={{0,6},{1,7},{2,4},{3,5},{4,2},{5,3},{6,0},{7,1},{8,14},{9,15},{10,... | collective-permute-start | bytes 884744 | tf_op jit(solution)/shard_map/ppermute | solution.py:626
  55.0 19.5 %collective-permute-start.16 = (bf16[192,768]{1,0:T(8,128)(2,1)S(1)}, bf16[192,768]{1,0:T(8,128)(2,1)S(1)}, u32[]{:S(2)}, u32[]{:S(2)}) collective-permute-start(bf16[192,768]{1,0:T(8,128)(2,1)S(1)} %constant_dynamic-update-slice_fusion.refs_8_), channel_id=1, source_target_pairs={{0,1},{1,0},{2,3},{3,2},{4,5},{5,4},{6,7},{7,6},{8,9},{9,8},{10,11... | collective-permute-start | bytes 884744 | tf_op jit(solution)/shard_map/ppermute | solution.py:626
  75.2 35.6 %collective-permute-start.8 = (bf16[96,1536]{1,0:T(8,128)(2,1)}, bf16[96,1536]{1,0:T(8,128)(2,1)}, u32[]{:S(2)}, u32[]{:S(2)}) collective-permute-start(bf16[96,1536]{1,0:T(8,128)(2,1)} %collective-permute-done.4.refs_2_.refs_10_), channel_id=1, source_target_pairs={{0,1},{1,0},{2,3},{3,2},{4,5},{5,4},{6,7},{7,6},{8,9},{9,8},{10,11... | collective-permute-start | bytes 884744 | tf_op jit(solution)/shard_map/ppermute | solution.py:626
  76.7 34.1 %collective-permute-start.9 = (bf16[96,1536]{1,0:T(8,128)(2,1)}, bf16[96,1536]{1,0:T(8,128)(2,1)}, u32[]{:S(2)}, u32[]{:S(2)}) collective-permute-start(bf16[96,1536]{1,0:T(8,128)(2,1)} %collective-permute-done.5.refs_3_.refs_11_), channel_id=1, source_target_pairs={{0,1},{1,0},{2,3},{3,2},{4,5},{5,4},{6,7},{7,6},{8,9},{9,8},{10,11... | collective-permute-start | bytes 884744 | tf_op jit(solution)/shard_map/ppermute | solution.py:626
  76.9 33.9 %collective-permute-start.17 = (bf16[192,768]{1,0:T(8,128)(2,1)}, bf16[192,768]{1,0:T(8,128)(2,1)}, u32[]{:S(2)}, u32[]{:S(2)}) collective-permute-start(bf16[192,768]{1,0:T(8,128)(2,1)} %copy-done.18), channel_id=1, source_target_pairs={{0,1},{1,0},{2,3},{3,2},{4,5},{5,4},{6,7},{7,6},{8,9},{9,8},{10,11... | collective-permute-start | bytes 884744 | tf_op jit(solution)/shard_map/ppermute | solution.py:626
  77.2 33.6 %collective-permute-start.18 = (bf16[192,768]{1,0:T(8,128)(2,1)}, bf16[192,768]{1,0:T(8,128)(2,1)}, u32[]{:S(2)}, u32[]{:S(2)}) collective-permute-start(bf16[192,768]{1,0:T(8,128)(2,1)} %copy-done.19), channel_id=1, source_target_pairs={{0,1},{1,0},{2,3},{3,2},{4,5},{5,4},{6,7},{7,6},{8,9},{9,8},{10,11... | collective-permute-start | bytes 884744 | tf_op jit(solution)/shard_map/ppermute | solution.py:626
  77.4 33.4 %collective-permute-start.19 = (bf16[192,768]{1,0:T(8,128)(2,1)}, bf16[192,768]{1,0:T(8,128)(2,1)}, u32[]{:S(2)}, u32[]{:S(2)}) collective-permute-start(bf16[192,768]{1,0:T(8,128)(2,1)} %copy-done.20), channel_id=1, source_target_pairs={{0,1},{1,0},{2,3},{3,2},{4,5},{5,4},{6,7},{7,6},{8,9},{9,8},{10,11... | collective-permute-start | bytes 884744 | tf_op jit(solution)/shard_map/ppermute | solution.py:626
  129.6 70.4 %collective-permute-start.37 = (bf16[384,3072]{1,0:T(8,128)(2,1)}, bf16[384,3072]{1,0:T(8,128)(2,1)S(1)}, u32[]{:S(2)}, u32[]{:S(2)}) collective-permute-start(bf16[384,3072]{1,0:T(8,128)(2,1)} %get-tuple-element.137), channel_id=1, source_target_pairs={{0,1},{1,0},{2,3},{3,2},{4,5},{5,4},{6,7},{7,6},{8,9},{9,8},{10,11... | collective-permute-start | bytes 7077896 | tf_op jit(solution)/shard_map/ppermute | solution.py:626
  164.3 32.1 %collective-permute-start.30 = (bf16[384,1920]{1,0:T(8,128)(2,1)}, bf16[384,1920]{1,0:T(8,128)(2,1)}, u32[]{:S(2)}, u32[]{:S(2)}) collective-permute-start(bf16[384,1920]{1,0:T(8,128)(2,1)} %get-tuple-element.127), channel_id=1, source_target_pairs={{0,1},{1,0},{2,3},{3,2},{4,5},{5,4},{6,7},{7,6},{8,9},{9,8},{10,11... | collective-permute-start | bytes 4423688 | tf_op jit(solution)/shard_map/ppermute | solution.py:626
  187.4 19.5 %collective-permute-start.48 = (f32[8,2304]{1,0:T(8,128)S(1)}, f32[8,2304]{1,0:T(8,128)S(1)}, u32[]{:S(2)}, u32[]{:S(2)}) collective-permute-start(f32[8,2304]{1,0:T(8,128)S(1)} %add_add_fusion.1), channel_id=1, source_target_pairs={{0,8},{1,9},{2,10},{3,11},{4,12},{5,13},{6,14},{7,15},{8,0},{9,1},... | collective-permute-start | bytes 221192 | tf_op jit(solution)/shard_map/ppermute | solution.py:626
  187.4 20.1 %collective-permute-start.49 = (f32[8,2304]{1,0:T(8,128)S(1)}, f32[8,2304]{1,0:T(8,128)S(1)}, u32[]{:S(2)}, u32[]{:S(2)}) collective-permute-start(f32[8,2304]{1,0:T(8,128)S(1)} %add_add_fusion.1), channel_id=1, source_target_pairs={{0,16},{1,17},{2,18},{3,19},{4,20},{5,21},{6,22},{7,23},{8,24},{9,... | collective-permute-start | bytes 221192 | tf_op jit(solution)/shard_map/ppermute | solution.py:626
  189.5 19.3 %collective-permute-start.50 = (f32[8,2304]{1,0:T(8,128)S(1)}, f32[8,2304]{1,0:T(8,128)}, u32[]{:S(2)}, u32[]{:S(2)}) collective-permute-start(f32[8,2304]{1,0:T(8,128)S(1)} %add_add_fusion.1), channel_id=1, source_target_pairs={{0,24},{1,25},{2,26},{3,27},{4,28},{5,29},{6,30},{7,31},{8,16},{9,... | collective-permute-start | bytes 221192 | tf_op jit(solution)/shard_map/ppermute | solution.py:626
  199.4 50.2 %collective-permute-start.31 = (bf16[96,1920]{1,0:T(8,128)(2,1)}, bf16[96,1920]{1,0:T(8,128)(2,1)S(1)}, u32[]{:S(2)}, u32[]{:S(2)}) collective-permute-start(bf16[96,1920]{1,0:T(8,128)(2,1)} %get-tuple-element.129), channel_id=1, source_target_pairs={{0,2},{1,3},{2,0},{3,1},{4,6},{5,7},{6,4},{7,5},{8,10},{9,11},{10,... | collective-permute-start | bytes 1105928 | tf_op jit(solution)/shard_map/ppermute | solution.py:626
  205.3 17.2 %collective-permute-start.38 = (bf16[96,3072]{1,0:T(8,128)(2,1)}, bf16[96,3072]{1,0:T(8,128)(2,1)S(1)}, u32[]{:S(2)}, u32[]{:S(2)}) collective-permute-start(bf16[96,3072]{1,0:T(8,128)(2,1)} %get-tuple-element.139), channel_id=1, source_target_pairs={{0,2},{1,3},{2,0},{3,1},{4,6},{5,7},{6,4},{7,5},{8,10},{9,11},{10,... | collective-permute-start | bytes 1769480 | tf_op jit(solution)/shard_map/ppermute | solution.py:626
  206.8 37.0 %collective-permute-start.39 = (bf16[96,3072]{1,0:T(8,128)(2,1)}, bf16[96,3072]{1,0:T(8,128)(2,1)S(1)}, u32[]{:S(2)}, u32[]{:S(2)}) collective-permute-start(bf16[96,3072]{1,0:T(8,128)(2,1)} %get-tuple-element.140), channel_id=1, source_target_pairs={{0,4},{1,5},{2,6},{3,7},{4,0},{5,1},{6,2},{7,3},{8,12},{9,13},{10,... | collective-permute-start | bytes 1769480 | tf_op jit(solution)/shard_map/ppermute | solution.py:626
  207.5 36.3 %collective-permute-start.40 = (bf16[96,3072]{1,0:T(8,128)(2,1)}, bf16[96,3072]{1,0:T(8,128)(2,1)S(1)}, u32[]{:S(2)}, u32[]{:S(2)}) collective-permute-start(bf16[96,3072]{1,0:T(8,128)(2,1)} %get-tuple-element.141), channel_id=1, source_target_pairs={{0,6},{1,7},{2,4},{3,5},{4,2},{5,3},{6,0},{7,1},{8,14},{9,15},{10,... | collective-permute-start | bytes 1769480 | tf_op jit(solution)/shard_map/ppermute | solution.py:626
  209.7 43.5 %collective-permute-start.32 = (bf16[96,1920]{1,0:T(8,128)(2,1)}, bf16[96,1920]{1,0:T(8,128)(2,1)S(1)}, u32[]{:S(2)}, u32[]{:S(2)}) collective-permute-start(bf16[96,1920]{1,0:T(8,128)(2,1)} %get-tuple-element.130), channel_id=1, source_target_pairs={{0,4},{1,5},{2,6},{3,7},{4,0},{5,1},{6,2},{7,3},{8,12},{9,13},{10,... | collective-permute-start | bytes 1105928 | tf_op jit(solution)/shard_map/ppermute | solution.py:626
  222.5 30.7 %collective-permute-start.33 = (bf16[96,1920]{1,0:T(8,128)(2,1)S(1)}, bf16[96,1920]{1,0:T(8,128)(2,1)S(1)}, u32[]{:S(2)}, u32[]{:S(2)}) collective-permute-start(bf16[96,1920]{1,0:T(8,128)(2,1)S(1)} %copy-done.30), channel_id=1, source_target_pairs={{0,6},{1,7},{2,4},{3,5},{4,2},{5,3},{6,0},{7,1},{8,14},{9,15},{10,... | collective-permute-start | bytes 1105928 | tf_op jit(solution)/shard_map/ppermute | solution.py:626
  247.4 13.8 %collective-permute-start.42 = (bf16[24,3072]{1,0:T(8,128)(2,1)}, bf16[24,3072]{1,0:T(8,128)(2,1)S(1)}, u32[]{:S(2)}, u32[]{:S(2)}) collective-permute-start(bf16[24,3072]{1,0:T(8,128)(2,1)} %get-tuple-element.144), channel_id=1, source_target_pairs={{0,16},{1,17},{2,18},{3,19},{4,20},{5,21},{6,22},{7,23},{8,24},{9,... | collective-permute-start | bytes 442376 | tf_op jit(solution)/shard_map/ppermute | solution.py:626
  249.6 11.6 %collective-permute-start.43 = (bf16[24,3072]{1,0:T(8,128)(2,1)}, bf16[24,3072]{1,0:T(8,128)(2,1)S(1)}, u32[]{:S(2)}, u32[]{:S(2)}) collective-permute-start(bf16[24,3072]{1,0:T(8,128)(2,1)} %get-tuple-element.145), channel_id=1, source_target_pairs={{0,24},{1,25},{2,26},{3,27},{4,28},{5,29},{6,30},{7,31},{8,16},{9,... | collective-permute-start | bytes 442376 | tf_op jit(solution)/shard_map/ppermute | solution.py:626
  (50 other events, 576.3 us)
where the time goes:
time: 268 us; the launch traced here: 267 us
  Pallas kernels  110 us (41%)
  waiting for transfers between devices  79.4 us (30%)
  starting transfers between devices  55.1 us (21%)
  local copies, waits for them, and re-layouts  18.4 us (7%)
  other arithmetic  3.19 us (1%)
    ppermute x51, waiting for transfers between devices, send(): return lax.ppermute(x, 'fsdp', [(i, i ^ mask) for i in range(devices)])  79.4 us
    pallas_call x10, Pallas kernels, call(): pl.pallas_call(kernel, out_shape=outs, in_specs=specs, scratch_shapes=lis...  55.7 us
    ppermute x51, starting transfers between devices, send(): return lax.ppermute(x, 'fsdp', [(i, i ^ mask) for i in range(devices)])  55.1 us
    pallas_call x1, Pallas kernels, scan_bwd(): pl.pallas_call(scan_bwd_kernel, grid=(inner // BLK,), in_specs=[tile(leng...  29.4 us
    pallas_call x1, Pallas kernels, scan_fwd(): pl.pallas_call(lambda *refs: scan_fwd_kernel(count, *refs), grid=(inner /...  21.1 us
    unnamed x65, local copies, waits for them, and re-layouts  6.13 us
  transfers between devices with their start and end apart: 51, of which 16 were waited for; matrix products, arithmetic and copies ran while one was open for 5% of the time, Pallas kernels for 34%

commit v1 on v0

--- a/solution.py
+++ b/solution.py
@@ -57,14 +57,15 @@
 
 def prep_kernel(at, taps_n, hid_ref, dvec_ref, owner_ref, where_ref, *refs):
     pieces, (xn_ref, taps_ref, gains_ref) = refs[:-3], refs[-3:]
-    held = rows_of(pieces)
+    last = pieces[0].shape[1] - BLK
+    tail = rows_of(pieces, slice(last, last + BLK))
     devices = owner_ref.shape[0]
-    rows_in = held.shape[0] // devices
-    row = iota((8 * devices, held.shape[0]), 0)
+    rows_in = tail.shape[0] // devices
+    row = iota((8 * devices, tail.shape[0]), 0)
     bits = devices.bit_length() - 1
     source = (row & (devices - 1)) * rows_in + lax.shift_right_logical(row, bits)
     pick = (iota(row.shape, 1) == source).astype(F32).astype(BF16)
-    small = mm(pick, held).astype(BF16)
+    small = mm(pick, tail).astype(BF16)
 
     def spread(part, line, width):
         lane, owner = where_ref[line : line + 1, :width], where_ref[line + 1 : line + 2, :width]
@@ -159,52 +160,53 @@
         ci_ref, dt_ref, sc_ref, yd_ref,
         step_ref, cc_ref, al_ref, ew_ref, wq_ref, cct_ref, mask_ref, sd_ref, so_ref,
     ) = refs[pieces:]
-    t = pl.program_id(0)
     length = xn_ref.shape[0]
     channels = ci_ref.shape[1]
     states = BLK
     inner = channels - 2 * states
 
-    @pl.when(t == 0)
-    def _():
-        xn = xn_ref[...]
-        ci_ref[...] = mm(xn, rows_of(w_refs, slice(0, channels)))
-        dt_ref[...] = mm(xn, rows_of(w_refs, slice(channels, channels + BLK)))
-        head_setup(dt_ref[...], heads_ref, step_ref, cc_ref, al_ref, ew_ref, wq_ref, cct_ref)
-        mask_setup(segc_ref, mask_ref)
-        lanes_b = slice(inner, inner + states)
-        lanes_c = slice(inner + states, channels)
-        _, pre_b = conv_parts(ci_ref[:, lanes_b], taps_ref, lanes_b, mask_ref)
-        _, pre_c = conv_parts(ci_ref[:, lanes_c], taps_ref, lanes_c, mask_ref)
-        score_setup(
-            pre_b * sigmoid(pre_b), pre_c * sigmoid(pre_c),
-            segc_ref, segr_ref, sd_ref, so_ref, None, None,
-        )
-
-    lanes = pl.ds(pl.multiple_of(t * BLK, BLK), BLK)
-    _, pre = conv_parts(ci_ref[:, lanes], taps_ref, lanes, mask_ref)
-    v = pre * sigmoid(pre)
-    low = iota((1, BLK), 1) < BLK // 2
-    shift = lax.rem(BLK - 2 * t, BLK)
-    vt = (v * pair_lanes(step_ref, shift, low)).astype(BF16)
-    vp = (v * pair_lanes(wq_ref, shift, low)).astype(BF16)
-    al2 = pair_lanes(al_ref, shift, low)
-    c2 = pltpu.roll(cc_ref[...], shift, axis=1)
-    r2 = pltpu.roll(cct_ref[...], lax.rem(cct_ref.shape[0] - 2 * t, cct_ref.shape[0]), axis=0)
-    for i in range(length // BLK):
-        rows = slice(i * BLK, (i + 1) * BLK)
-        before = slice((i - 1) * BLK, i * BLK)
-        ms = []
-        for k in range(2):
-            row = r2[k : k + 1, rows]
-            d = jnp.exp2(jnp.minimum(c2[rows, k : k + 1] - row, 0.0))
-            ms.append((sd_ref[i] * d).astype(BF16))
-        yd = mm(jnp.concatenate(ms, axis=1), block_diag(vt[rows], low))
-        yd_ref[rows, :] = yd
-        y = yd + skip_ref[...] * v[rows]
-        if i > 0:
-            y = y + al2[rows] * mm(so_ref[i], vp[before])
-        sc_ref[rows, :] = y
+    xn = xn_ref[...]
+    ci_ref[...] = mm(xn, rows_of(w_refs, slice(0, channels)))
+    dt_ref[...] = mm(xn, rows_of(w_refs, slice(channels, channels + BLK)))
+    head_setup(dt_ref[...], heads_ref, step_ref, cc_ref, al_ref, ew_ref, wq_ref, cct_ref)
+    mask_setup(segc_ref, mask_ref)
+    lanes_b = slice(inner, inner + states)
+    lanes_c = slice(inner + states, channels)
+    _, pre_b = conv_parts(ci_ref[:, lanes_b], taps_ref, lanes_b, mask_ref)
+    _, pre_c = conv_parts(ci_ref[:, lanes_c], taps_ref, lanes_c, mask_ref)
+    score_setup(
+        pre_b * sigmoid(pre_b), pre_c * sigmoid(pre_c),
+        segc_ref, segr_ref, sd_ref, so_ref, None, None,
+    )
+
+    def body(t, carry):
+        lanes = pl.ds(pl.multiple_of(t * BLK, BLK), BLK)
+        _, pre = conv_parts(ci_ref[:, lanes], taps_ref, lanes, mask_ref)
+        v = pre * sigmoid(pre)
+        low = iota((1, BLK), 1) < BLK // 2
+        shift = lax.rem(BLK - 2 * t, BLK)
+        vt = (v * pair_lanes(step_ref, shift, low)).astype(BF16)
+        vp = (v * pair_lanes(wq_ref, shift, low)).astype(BF16)
+        al2 = pair_lanes(al_ref, shift, low)
+        c2 = pltpu.roll(cc_ref[...], shift, axis=1)
+        r2 = pltpu.roll(cct_ref[...], lax.rem(cct_ref.shape[0] - 2 * t, cct_ref.shape[0]), axis=0)
+        for i in range(length // BLK):
+            rows = slice(i * BLK, (i + 1) * BLK)
+            before = slice((i - 1) * BLK, i * BLK)
+            ms = []
+            for k in range(2):
+                row = r2[k : k + 1, rows]
+                d = jnp.exp2(jnp.minimum(c2[rows, k : k + 1] - row, 0.0))
+                ms.append((sd_ref[i] * d).astype(BF16))
+            yd = mm(jnp.concatenate(ms, axis=1), block_diag(vt[rows], low))
+            yd_ref[rows, lanes] = yd
+            y = yd + skip_ref[:, lanes] * v[rows]
+            if i > 0:
+                y = y + al2[rows] * mm(so_ref[i], vp[before])
+            sc_ref[rows, lanes] = y
+        return carry
+
+    lax.fori_loop(0, inner // BLK, body, 0)
 
 
 def mid_kernel(pieces, *refs):
@@ -309,7 +311,6 @@
     step_ref, cc_ref, al_ref, ew_ref, wq_ref, cct_ref, mask_ref,
     sdt_ref, so_ref, sot_ref, dsdt_ref, dso_ref, acc_ref, dpre_ref,
 ):
-    t = pl.program_id(0)
     length = ci_ref.shape[0]
     blocks = length // BLK
     channels = ci_ref.shape[1]
@@ -319,131 +320,130 @@
     lanes_b = slice(inner, inner + states)
     lanes_c = slice(inner + states, channels)
 
-    @pl.when(t == 0)
-    def _():
-        head_setup(dt_ref[...], heads_ref, step_ref, cc_ref, al_ref, ew_ref, wq_ref, cct_ref)
-        mask_setup(segc_ref, mask_ref)
-        dheads_ref[...] = jnp.zeros_like(dheads_ref)
-        dtaps_ref[...] = jnp.zeros_like(dtaps_ref)
-        _, pre_b = conv_parts(ci_ref[:, lanes_b], taps_ref, lanes_b, mask_ref)
-        _, pre_c = conv_parts(ci_ref[:, lanes_c], taps_ref, lanes_c, mask_ref)
-        score_setup(
-            pre_b * sigmoid(pre_b), pre_c * sigmoid(pre_c),
-            segc_ref, segr_ref, None, so_ref, sdt_ref, sot_ref,
-        )
-        dsdt_ref[...] = jnp.zeros_like(dsdt_ref)
-        dso_ref[...] = jnp.zeros_like(dso_ref)
-        acc_ref[...] = jnp.zeros_like(acc_ref)
-
-    lanes = pl.ds(pl.multiple_of(t * BLK, BLK), BLK)
-    x = ci_ref[:, lanes]
-    _, pre = conv_parts(x, taps_ref, lanes, mask_ref)
-    v, slope = silu_and_slope(pre)
-    low = iota((1, BLK), 1) < BLK // 2
-    shift = lax.rem(BLK - 2 * t, BLK)
-    st2 = pair_lanes(step_ref, shift, low)
-    wq2 = pair_lanes(wq_ref, shift, low)
-    ew2 = pair_lanes(ew_ref, shift, low)
-    al2 = pair_lanes(al_ref, shift, low)
-    c2 = pltpu.roll(cc_ref[...], shift, axis=1)
-    r2 = pltpu.roll(cct_ref[...], lax.rem(cct_ref.shape[0] - 2 * t, cct_ref.shape[0]), axis=0)
-    vtb = (v * st2).astype(BF16)
-    vpb = (v * wq2).astype(BF16)
-    g = g_ref[...]
-    gb = g.astype(BF16)
-    gpb = (al2 * g).astype(BF16)
-    dskip_ref[...] = jnp.sum(g * v, axis=0, keepdims=True)
-    k_row = iota((4 * BLK, BLK), 0)
-    target = jnp.where(k_row >= 2 * BLK, BLK // 2, 0) + 2 * t
-    target = target + jnp.where((k_row & (BLK - 1)) >= BLK // 2, 1, 0)
-    collect = (iota((4 * BLK, BLK), 1) == target).astype(F32).astype(BF16)
+    head_setup(dt_ref[...], heads_ref, step_ref, cc_ref, al_ref, ew_ref, wq_ref, cct_ref)
+    mask_setup(segc_ref, mask_ref)
+    dheads_ref[...] = jnp.zeros_like(dheads_ref)
+    dtaps_ref[...] = jnp.zeros_like(dtaps_ref)
+    _, pre_b = conv_parts(ci_ref[:, lanes_b], taps_ref, lanes_b, mask_ref)
+    _, pre_c = conv_parts(ci_ref[:, lanes_c], taps_ref, lanes_c, mask_ref)
+    score_setup(
+        pre_b * sigmoid(pre_b), pre_c * sigmoid(pre_c),
+        segc_ref, segr_ref, None, so_ref, sdt_ref, sot_ref,
+    )
+    dsdt_ref[...] = jnp.zeros_like(dsdt_ref)
+    dso_ref[...] = jnp.zeros_like(dso_ref)
+    acc_ref[...] = jnp.zeros_like(acc_ref)
+
+    def body(t, carry):
+        lanes = pl.ds(pl.multiple_of(t * BLK, BLK), BLK)
+        x = ci_ref[:, lanes]
+        _, pre = conv_parts(x, taps_ref, lanes, mask_ref)
+        v, slope = silu_and_slope(pre)
+        low = iota((1, BLK), 1) < BLK // 2
+        shift = lax.rem(BLK - 2 * t, BLK)
+        st2 = pair_lanes(step_ref, shift, low)
+        wq2 = pair_lanes(wq_ref, shift, low)
+        ew2 = pair_lanes(ew_ref, shift, low)
+        al2 = pair_lanes(al_ref, shift, low)
+        c2 = pltpu.roll(cc_ref[...], shift, axis=1)
+        r2 = pltpu.roll(cct_ref[...], lax.rem(cct_ref.shape[0] - 2 * t, cct_ref.shape[0]), axis=0)
+        vtb = (v * st2).astype(BF16)
+        vpb = (v * wq2).astype(BF16)
+        g = g_ref[:, lanes]
+        gb = g.astype(BF16)
+        gpb = (al2 * g).astype(BF16)
+        dskip_ref[:, lanes] = jnp.sum(g * v, axis=0, keepdims=True)
+        k_row = iota((4 * BLK, BLK), 0)
+        target = jnp.where(k_row >= 2 * BLK, BLK // 2, 0) + 2 * t
+        target = target + jnp.where((k_row & (BLK - 1)) >= BLK // 2, 1, 0)
+        collect = (iota((4 * BLK, BLK), 1) == target).astype(F32).astype(BF16)
+        for i in range(blocks):
+            rows = slice(i * BLK, (i + 1) * BLK)
+            before = slice((i - 1) * BLK, i * BLK)
+            after = slice((i + 1) * BLK, (i + 2) * BLK)
+            gdiag = block_diag(gb[rows], low)
+            both = mm_nt(vtb[rows], gdiag)
+            ms = []
+            part = jnp.zeros((BLK, BLK), F32)
+            for k in range(2):
+                row = r2[k : k + 1, rows]
+                d = jnp.exp2(jnp.minimum(row - c2[rows, k : k + 1], 0.0))
+                ms.append((sdt_ref[i] * d).astype(BF16))
+                part = part + both[:, k * BLK : (k + 1) * BLK] * d
+            dsdt_ref[i] += part
+            dvt = mm(jnp.concatenate(ms, axis=1), gdiag)
+            x1 = gb[rows].astype(F32) * yd_ref[rows, lanes] - dvt * vtb[rows].astype(F32)
+            dv = st2[rows] * dvt + skip_ref[:, lanes] * g[rows]
+            dstep = dvt
+            if i > 0:
+                z = mm(so_ref[i], vpb[before])
+                x1 = x1 + gpb[rows].astype(F32) * z
+                dso_ref[i] += mm_nt(gpb[rows], vpb[before])
+            if i + 1 < blocks:
+                dvp = mm(sot_ref[i + 1], gpb[after])
+                x1 = x1 - dvp * vpb[rows].astype(F32)
+                dv = dv + wq2[rows] * dvp
+                dstep = dstep + ew2[rows] * dvp
+            h1, l1 = split2(x1)
+            h2, l2 = split2(dstep * v[rows])
+            acc_ref[rows, :] += mm(jnp.concatenate([h1, l1, h2, l2], axis=1), collect)
+            dpre_ref[rows, :] = dv * slope[rows]
+        conv_back(dpre_ref[...], x, taps_ref, lanes, mask_ref, dtaps_ref, dp_ref, lanes)
+        return carry
+
+    lax.fori_loop(0, inner // BLK, body, 0)
+    xb, xc = ci_ref[:, lanes_b], ci_ref[:, lanes_c]
+    _, pre_b = conv_parts(xb, taps_ref, lanes_b, mask_ref)
+    _, pre_c = conv_parts(xc, taps_ref, lanes_c, mask_ref)
+    bmat, slope_b = silu_and_slope(pre_b)
+    cmat, slope_c = silu_and_slope(pre_c)
+    bb, cb = bmat.astype(BF16), cmat.astype(BF16)
+    causal_t = iota((BLK, BLK), 1) >= iota((BLK, BLK), 0)
+    upper = causal_t.astype(F32)
+    dst, dso = [], [None]
+    for i in range(blocks):
+        rows = slice(i * BLK, (i + 1) * BLK)
+        before = slice((i - 1) * BLK, i * BLK)
+        same = (segc_ref[rows, :] == segr_ref[:, rows]) & causal_t
+        dst.append(jnp.where(same, dsdt_ref[i], 0.0))
+        if i > 0:
+            linked = segc_ref[rows, :] == segr_ref[:, before]
+            dso.append(jnp.where(linked, dso_ref[i], 0.0))
     for i in range(blocks):
         rows = slice(i * BLK, (i + 1) * BLK)
         before = slice((i - 1) * BLK, i * BLK)
         after = slice((i + 1) * BLK, (i + 2) * BLK)
-        gdiag = block_diag(gb[rows], low)
-        both = mm_nt(vtb[rows], gdiag)
-        ms = []
-        part = jnp.zeros((BLK, BLK), F32)
-        for k in range(2):
-            row = r2[k : k + 1, rows]
-            d = jnp.exp2(jnp.minimum(row - c2[rows, k : k + 1], 0.0))
-            ms.append((sdt_ref[i] * d).astype(BF16))
-            part = part + both[:, k * BLK : (k + 1) * BLK] * d
-        dsdt_ref[i] += part
-        dvt = mm(jnp.concatenate(ms, axis=1), gdiag)
-        x1 = gb[rows].astype(F32) * yd_ref[rows, :] - dvt * vtb[rows].astype(F32)
-        dv = st2[rows] * dvt + skip_ref[...] * g[rows]
-        dstep = dvt
+        dc = mm(dst[i].T.astype(BF16), bb[rows])
         if i > 0:
-            z = mm(so_ref[i], vpb[before])
-            x1 = x1 + gpb[rows].astype(F32) * z
-            dso_ref[i] += mm_nt(gpb[rows], vpb[before])
+            dc = dc + mm(dso[i].astype(BF16), bb[before])
+        dpre_ref[rows, :] = dc * slope_c[rows]
+    conv_back(dpre_ref[...], xc, taps_ref, lanes_c, mask_ref, dtaps_ref, dp_ref, lanes_c)
+    for i in range(blocks):
+        rows = slice(i * BLK, (i + 1) * BLK)
+        after = slice((i + 1) * BLK, (i + 2) * BLK)
+        db = mm(dst[i].astype(BF16), cb[rows])
         if i + 1 < blocks:
-            dvp = mm(sot_ref[i + 1], gpb[after])
-            x1 = x1 - dvp * vpb[rows].astype(F32)
-            dv = dv + wq2[rows] * dvp
-            dstep = dstep + ew2[rows] * dvp
-        h1, l1 = split2(x1)
-        h2, l2 = split2(dstep * v[rows])
-        acc_ref[rows, :] += mm(jnp.concatenate([h1, l1, h2, l2], axis=1), collect)
-        dpre_ref[rows, :] = dv * slope[rows]
-    conv_back(dpre_ref[...], x, taps_ref, lanes, mask_ref, dtaps_ref, dp_ref, lanes)
-
-    @pl.when(t == pl.num_programs(0) - 1)
-    def _():
-        xb, xc = ci_ref[:, lanes_b], ci_ref[:, lanes_c]
-        _, pre_b = conv_parts(xb, taps_ref, lanes_b, mask_ref)
-        _, pre_c = conv_parts(xc, taps_ref, lanes_c, mask_ref)
-        bmat, slope_b = silu_and_slope(pre_b)
-        cmat, slope_c = silu_and_slope(pre_c)
-        bb, cb = bmat.astype(BF16), cmat.astype(BF16)
-        causal_t = iota((BLK, BLK), 1) >= iota((BLK, BLK), 0)
-        upper = causal_t.astype(F32)
-        dst, dso = [], [None]
-        for i in range(blocks):
-            rows = slice(i * BLK, (i + 1) * BLK)
-            before = slice((i - 1) * BLK, i * BLK)
-            same = (segc_ref[rows, :] == segr_ref[:, rows]) & causal_t
-            dst.append(jnp.where(same, dsdt_ref[i], 0.0))
-            if i > 0:
-                linked = segc_ref[rows, :] == segr_ref[:, before]
-                dso.append(jnp.where(linked, dso_ref[i], 0.0))
-        for i in range(blocks):
-            rows = slice(i * BLK, (i + 1) * BLK)
-            before = slice((i - 1) * BLK, i * BLK)
-            after = slice((i + 1) * BLK, (i + 2) * BLK)
-            dc = mm(dst[i].T.astype(BF16), bb[rows])
-            if i > 0:
-                dc = dc + mm(dso[i].astype(BF16), bb[before])
-            dpre_ref[rows, :] = dc * slope_c[rows]
-        conv_back(dpre_ref[...], xc, taps_ref, lanes_c, mask_ref, dtaps_ref, dp_ref, lanes_c)
-        for i in range(blocks):
-            rows = slice(i * BLK, (i + 1) * BLK)
-            after = slice((i + 1) * BLK, (i + 2) * BLK)
-            db = mm(dst[i].astype(BF16), cb[rows])
-            if i + 1 < blocks:
-                db = db + mm(dso[i + 1].T.astype(BF16), cb[after])
-            dpre_ref[rows, :] = db * slope_b[rows]
-        conv_back(dpre_ref[...], xb, taps_ref, lanes_b, mask_ref, dtaps_ref, dp_ref, lanes_b)
-
-        decay = jnp.exp(heads_ref[0:1, :])
-        later = jnp.zeros((1, BLK), F32)
-        dalog = jnp.zeros((1, BLK), F32)
-        dbias = jnp.zeros((1, BLK), F32)
-        for i in reversed(range(blocks)):
-            rows = slice(i * BLK, (i + 1) * BLK)
-            dcum = acc_ref[rows, :]
-            drate = later + jnp.dot(upper, dcum, precision=HIGH, preferred_element_type=F32)
-            later = drate[0:1, :]
-            step = step_ref[rows, :]
-            dalog = dalog - jnp.sum(drate * step, axis=0, keepdims=True) * decay
-            dstep = pltpu.roll(dcum, BLK // 2, axis=1) - drate * decay
-            ddt = dstep * sigmoid(dt_ref[rows, :] + heads_ref[2:3, :])
-            dbias = dbias + jnp.sum(ddt, axis=0, keepdims=True)
-            dp_ref[rows, channels:] = jnp.where(iota((1, BLK), 1) < nheads, ddt, 0.0).astype(BF16)
-        dheads_ref[0:1, :] = dalog
-        dheads_ref[1:2, :] = dbias
+            db = db + mm(dso[i + 1].T.astype(BF16), cb[after])
+        dpre_ref[rows, :] = db * slope_b[rows]
+    conv_back(dpre_ref[...], xb, taps_ref, lanes_b, mask_ref, dtaps_ref, dp_ref, lanes_b)
+
+    decay = jnp.exp(heads_ref[0:1, :])
+    later = jnp.zeros((1, BLK), F32)
+    dalog = jnp.zeros((1, BLK), F32)
+    dbias = jnp.zeros((1, BLK), F32)
+    for i in reversed(range(blocks)):
+        rows = slice(i * BLK, (i + 1) * BLK)
+        dcum = acc_ref[rows, :]
+        drate = later + jnp.dot(upper, dcum, precision=HIGH, preferred_element_type=F32)
+        later = drate[0:1, :]
+        step = step_ref[rows, :]
+        dalog = dalog - jnp.sum(drate * step, axis=0, keepdims=True) * decay
+        dstep = pltpu.roll(dcum, BLK // 2, axis=1) - drate * decay
+        ddt = dstep * sigmoid(dt_ref[rows, :] + heads_ref[2:3, :])
+        dbias = dbias + jnp.sum(ddt, axis=0, keepdims=True)
+        dp_ref[rows, channels:] = jnp.where(iota((1, BLK), 1) < nheads, ddt, 0.0).astype(BF16)
+    dheads_ref[0:1, :] = dalog
+    dheads_ref[1:2, :] = dbias
 
 
 def grad_in_kernel(xn_ref, dp_ref, lo_ref, hi_ref):
@@ -480,6 +480,11 @@
     ig_ref[...] = cot_ref[...].astype(F32) + scale * (dunit - unit * inner)
 
 
+def stack_kernel(*refs):
+    rows = jnp.concatenate([ref[...].astype(F32) for ref in refs[:-1]], axis=0)
+    refs[-1][...] = rows.astype(BF16)
+
+
 def fold_kernel(count, *refs):
     total = refs[0][...].astype(F32)
     for ref in refs[1:count]:
@@ -509,7 +514,11 @@
     return jax.ShapeDtypeStruct(shape, dtype)
 
 
-PARAMS = dict(compiler_params=pltpu.CompilerParams(vmem_limit_bytes=60 * 1024 * 1024))
+def held(shape, dtype):
+    return pltpu.VMEM(shape, dtype)
+
+
+PARAMS = dict(compiler_params=pltpu.CompilerParams(vmem_limit_bytes=20 * 1024 * 1024))
 
 
 def head_scratch(length, inner):
@@ -517,57 +526,41 @@
     return [pltpu.VMEM((length, BLK), F32)] * 5 + [pltpu.VMEM((nheads, length), F32)]
 
 
-def full(shape):
-    return pl.BlockSpec(shape, lambda t: (0,) * len(shape))
-
-
-def tile(rows):
-    return pl.BlockSpec((rows, BLK), lambda t: (0, t))
-
-
-def scan_fwd(weights, xn, taps, segc, segr, heads, skip_row):
+def scan_scratch(length, inner, taps):
+    return head_scratch(length, inner) + [pltpu.VMEM((taps - 1, length, BLK), F32)]
+
+
+def scan_fwd(weights, taps_n, xn, taps, segc, segr, heads, skip_row):
     length = xn.shape[0]
     channels, inner = taps.shape[1], skip_row.shape[1]
-    kernel = 4
     blocks = length // BLK
-    ins = tuple(weights) + (xn, taps, segc, segr, heads, skip_row)
     count = len(weights)
-    return pl.pallas_call(
+    return call(
         lambda *refs: scan_fwd_kernel(count, *refs),
-        grid=(inner // BLK,),
-        in_specs=[full(a.shape) for a in ins[:-1]] + [tile(1)],
-        out_specs=[full((length, channels)), full((length, BLK)), tile(length), tile(length)],
-        out_shape=[
-            sds((length, channels), F32), sds((length, BLK), F32),
-            sds((length, inner), F32), sds((length, inner), F32),
-        ],
-        scratch_shapes=head_scratch(length, inner) + [
-            pltpu.VMEM((kernel - 1, length, BLK), F32),
+        (
+            held((length, channels), F32), held((length, BLK), F32),
+            held((length, inner), F32), held((length, inner), F32),
+        ),
+        *weights, xn, taps, segc, segr, heads, skip_row,
+        scratch=scan_scratch(length, inner, taps_n - 1) + [
             pltpu.VMEM((blocks, BLK, BLK), F32),
             pltpu.VMEM((blocks, BLK, BLK), BF16),
         ],
-        name="scan_fwd",
-        **PARAMS,
-    )(*ins)
-
-
-def scan_bwd(g, yd, ci, dt, taps, segc, segr, heads, skip_row):
+    )
+
+
+def scan_bwd(taps_n, g, yd, ci, dt, taps, segc, segr, heads, skip_row):
     length, channels = ci.shape
     inner = skip_row.shape[1]
-    kernel = 4
-    blocks = length // BLK
-    ins = (g, yd, ci, dt, taps, segc, segr, heads, skip_row)
-    score = (blocks, BLK, BLK)
-    return pl.pallas_call(
+    score = (length // BLK, BLK, BLK)
+    return call(
         scan_bwd_kernel,
-        grid=(inner // BLK,),
-        in_specs=[tile(length), tile(length)] + [full(a.shape) for a in ins[2:8]] + [tile(1)],
-        out_specs=[full((length, channels + BLK)), full(taps.shape), tile(1), full((8, BLK))],
-        out_shape=[
-            sds((length, channels + BLK), BF16), sds(taps.shape, F32), sds((1, inner), F32), sds((8, BLK), F32),
-        ],
-        scratch_shapes=head_scratch(length, inner) + [
-            pltpu.VMEM((kernel - 1, length, BLK), F32),
+        (
+            held((length, channels + BLK), BF16), held(taps.shape, F32), held((1, inner), F32),
+            held((8, BLK), F32),
+        ),
+        g, yd, ci, dt, taps, segc, segr, heads, skip_row,
+        scratch=scan_scratch(length, inner, taps_n - 1) + [
             pltpu.VMEM(score, F32),
             pltpu.VMEM(score, BF16),
             pltpu.VMEM(score, BF16),
@@ -576,34 +569,27 @@
             pltpu.VMEM((length, BLK), F32),
             pltpu.VMEM((length, BLK), F32),
         ],
-        name="scan_bwd",
-        **PARAMS,
-    )(*ins)
+    )
 
 
 def prep(at, taps_n, hidden, dvec, owner, where, pieces, channels, width):
-    ins = (hidden, dvec, owner, where) + tuple(pieces)
-    last = pieces[0].shape[1] // BLK - 1
-    outs = (sds(hidden.shape, BF16), sds((8, channels), F32), sds((1, width), F32))
-    return pl.pallas_call(
+    return call(
         lambda *refs: prep_kernel(at, taps_n, *refs),
-        grid=(1,),
-        in_specs=[full(a.shape) for a in ins[:4]]
-        + [pl.BlockSpec((a.shape[0], BLK), lambda t: (0, last)) for a in pieces],
-        out_specs=[full(a.shape) for a in outs],
-        out_shape=outs,
-        name="prep",
-        **PARAMS,
-    )(*ins)
+        (held(hidden.shape, BF16), held((8, channels), F32), held((1, width), F32)),
+        hidden, dvec, owner, where, *pieces,
+    )
 
 
 def call(kernel, outs, *ins, scratch=(), scalar=None):
     specs = [
         pl.BlockSpec(memory_space=pltpu.SMEM if k == scalar else pltpu.VMEM) for k in range(len(ins))
     ]
+    near = [a if k == scalar else pltpu.with_memory_space_constraint(a, pltpu.VMEM) for k, a in enumerate(ins)]
+    many = isinstance(outs, (tuple, list))
+    out_specs = [pl.BlockSpec(memory_space=pltpu.VMEM) for _ in outs] if many else pl.BlockSpec(memory_space=pltpu.VMEM)
     return pl.pallas_call(
-        kernel, out_shape=outs, in_specs=specs, scratch_shapes=list(scratch), **PARAMS
-    )(*ins)
+        kernel, out_shape=outs, in_specs=specs, out_specs=out_specs, scratch_shapes=list(scratch), **PARAMS
+    )(*near)
 
 
 def stages(devices):
@@ -630,12 +616,19 @@
     return [send(part, devices, m) for part, m in zip(parts, stages(devices)[stage])]
 
 
+def stack(pieces):
+    size, rest = pieces[0].shape[0], pieces[0].shape[1:]
+    if size % 8 or len(rest) != 1:
+        return jnp.concatenate(pieces, axis=0)
+    return call(stack_kernel, held((len(pieces) * size,) + rest, BF16), *pieces)
+
+
 def gather(x, devices):
     groups = stages(devices)
     core = len(groups) - 1
     pieces = [x]
     for stage in range(core):
-        x = pieces[0] if len(pieces) == 1 else jnp.concatenate(pieces, axis=0)
+        x = pieces[0] if len(pieces) == 1 else stack(pieces)
         pieces = [x] + send_all([x] * len(groups[stage]), devices, stage)
     return pieces + [send(a, devices, 1) for a in pieces]
 
@@ -647,9 +640,7 @@
         total = sum(part.astype(F32) for part in parts).astype(dtype)
         return [total[k * size : (k + 1) * size] for k in range(fan)]
     count = len(parts)
-    return call(
-        lambda *refs: fold_kernel(count, *refs), tuple(sds((size, cols), dtype) for _ in range(fan)), *parts
-    )
+    return call(lambda *refs: fold_kernel(count, *refs), tuple(held((size, cols), dtype) for _ in range(fan)), *parts)
 
 
 def reduce_shares(lo, hi, devices):
@@ -723,20 +714,20 @@
         taps = jnp.moveaxis(rows[:, :, :tap_share], 0, 1).reshape(8, channels)
         gains_all = rows[:, taps_n, :gain_share].reshape(1, width + inner)
         xn = call(norm_kernel, sds((length, width), BF16), hidden, gains_all, dvec)
-    ci, dt, sc, yd = scan_fwd(cw, xn, taps, segc, segment_ids, heads, skip_row)
+    ci, dt, sc, yd = scan_fwd(cw, taps_n, xn, taps, segc, segment_ids, heads, skip_row)
     if rows_out % 16:
         wo_all = jnp.concatenate(ow, axis=0).reshape(devices, rows_out, width)[place].reshape(inner, width)
         ow = [wo_all[k * (inner // count) : (k + 1) * (inner // count)] for k in range(count)]
     aligned = rows_in % 8 == 0
     if aligned:
-        halves = (sds((width // 2, inner + 2 * width), BF16), sds((width // 2, inner + 2 * width), BF16))
+        halves = (held((width // 2, inner + 2 * width), BF16), held((width // 2, inner + 2 * width), BF16))
     else:
         halves = (sds((width, inner), BF16), sds((inner, width), BF16))
     lo, hi, g, dgate, mixed, ginner, wo = call(
         lambda *refs: mid_kernel(count, *refs),
         halves + (
-            sds((length, inner), F32), sds((length, inner), BF16), sds((length, inner), BF16),
-            sds((8, inner), F32), sds((inner, width), BF16),
+            held((length, inner), F32), held((length, inner), BF16), held((length, inner), BF16),
+            held((8, inner), F32), held((inner, width), BF16),
         ),
         *gw, *ow, order, xn, sc, gains_all, cot,
         scratch=(
@@ -751,8 +742,8 @@
         lo, hi = both[: width // 2], both[width // 2 :]
     mid_parts = reduce_shares(lo, hi, devices)
     output = call(branch_kernel, sds((length, width), BF16), mixed, wo, hidden)
-    dp, dtaps, dskip, dheads = scan_bwd(g, yd, ci, dt, taps, segc, segment_ids, heads, skip_row)
-    half = sds((width // 2, dp.shape[1]), BF16)
+    dp, dtaps, dskip, dheads = scan_bwd(taps_n, g, yd, ci, dt, taps, segc, segment_ids, heads, skip_row)
+    half = held((width // 2, dp.shape[1]), BF16)
     clo, chi = call(grad_in_kernel, (half, half), xn, dp)
     conv_parts_in = reduce_shares(clo, chi, devices)
     input_grad, sums = call(

time: 268 us -> 223 us (0.83)
  Pallas kernels: 110 us -> 79.6 us
  waiting for transfers between devices: 79.4 us -> 69.1 us
  local copies, waits for them, and re-layouts: 18.4 us -> 13.4 us
  starting transfers between devices: 55.1 us -> 58 us
    pallas_call x13 -> x16, Pallas kernels: 110 us -> 79.6 us  [call(): pl.pallas_call(kernel, out_shape=outs, in_specs=specs, out_specs=out_spec...]
    ppermute x51, waiting for transfers between devices: 79.4 us -> 69.1 us  [send(): return lax.ppermute(x, 'fsdp', [(i, i ^ mask) for i in range(devices)])]
    ppermute x51, starting transfers between devices: 55.1 us -> 58 us  [send(): return lax.ppermute(x, 'fsdp', [(i, i ^ mask) for i in range(devices)])]
    unnamed x65 -> x72, local copies, waits for them, and re-layouts: 6.13 us -> 6.64 us
  transfers between devices with their start and end apart: 51 -> 51, of which waited for: 16 -> 16; matrix products, arithmetic and copies ran while one was open for 5% -> 3% of each run, Pallas kernels for 34% -> 30%
where the time goes in v1:
time: 223 us; the launch traced here: 222 us
  Pallas kernels  79.6 us (36%)
  waiting for transfers between devices  69.1 us (31%)
  starting transfers between devices  58 us (26%)
  local copies, waits for them, and re-layouts  13.4 us (6%)
    pallas_call x16, Pallas kernels, call(): pl.pallas_call(kernel, out_shape=outs, in_specs=specs, out_specs=out_spec...  79.6 us
    ppermute x51, waiting for transfers between devices, send(): return lax.ppermute(x, 'fsdp', [(i, i ^ mask) for i in range(devices)])  69.1 us
    ppermute x51, starting transfers between devices, send(): return lax.ppermute(x, 'fsdp', [(i, i ^ mask) for i in range(devices)])  58 us
    unnamed x72, local copies, waits for them, and re-layouts  6.64 us
  transfers between devices with their start and end apart: 51, of which 16 were waited for; matrix products, arithmetic and copies ran while one was open for 3% of the time, Pallas kernels for 30%

profile of v1, /device:TPU:0, one launch (start us, length us, event | category | flops | bytes accessed | tf_op | source)
XLA Modules:
  0.0 222.2 jit_solution(11632531732240618710)
XLA Ops:
  1.7 3.1 %collective-permute-start = (bf16[24,1536]{1,0:T(8,128)(2,1)S(1)}, bf16[24,1536]{1,0:T(8,128)(2,1)S(1)}, u32[]{:S(2)}, u32[]{:S(2)}) collective-permute-start(bf16[24,1536]{1,0:T(8,128)(2,1)S(1)} %slice.114.refs_0_), channel_id=1, source_target_pairs={{0,8},{1,9},{2,10},{3,11},{4,12},{5,13},{6,14},{7,15},{8,0},{9,1},... | collective-permute-start | bytes 221192 | tf_op jit(solution)/shard_map/ppermute | solution.py:612
  4.7 2.6 %collective-permute-start.1 = (bf16[24,1536]{1,0:T(8,128)(2,1)S(1)}, bf16[24,1536]{1,0:T(8,128)(2,1)S(1)}, u32[]{:S(2)}, u32[]{:S(2)}) collective-permute-start(bf16[24,1536]{1,0:T(8,128)(2,1)S(1)} %slice.114.refs_0_), channel_id=1, source_target_pairs={{0,16},{1,17},{2,18},{3,19},{4,20},{5,21},{6,22},{7,23},{8,24},{9,... | collective-permute-start | bytes 221192 | tf_op jit(solution)/shard_map/ppermute | solution.py:612
  8.2 3.5 %collective-permute-start.11 = (bf16[48,768]{1,0:T(8,128)(2,1)}, bf16[48,768]{1,0:T(8,128)(2,1)S(1)}, u32[]{:S(2)}, u32[]{:S(2)}) collective-permute-start(bf16[48,768]{1,0:T(8,128)(2,1)} %refs_0_.2), channel_id=1, source_target_pairs={{0,16},{1,17},{2,18},{3,19},{4,20},{5,21},{6,22},{7,23},{8,24},{9,... | collective-permute-start | bytes 221192 | tf_op jit(solution)/shard_map/ppermute | solution.py:612
  14.3 1.6 collective-permute-start.3
  15.9 2.8 %collective-permute-start.20 = (bf16[24,1920]{1,0:T(8,128)(2,1)S(1)}, bf16[24,1920]{1,0:T(8,128)(2,1)S(1)}, u32[]{:S(2)}, u32[]{:S(2)}) collective-permute-start(bf16[24,1920]{1,0:T(8,128)(2,1)S(1)} %pad_maximum_fusion.refs_0_), channel_id=1, source_target_pairs={{0,8},{1,9},{2,10},{3,11},{4,12},{5,13},{6,14},{7,15},{8,0},{9,1},... | collective-permute-start | bytes 276488 | tf_op jit(solution)/shard_map/ppermute | solution.py:612
  21.2 2.4 %collective-permute-start.22 = (bf16[24,1920]{1,0:T(8,128)(2,1)S(1)}, bf16[24,1920]{1,0:T(8,128)(2,1)S(1)}, u32[]{:S(2)}, u32[]{:S(2)}) collective-permute-start(bf16[24,1920]{1,0:T(8,128)(2,1)S(1)} %pad_maximum_fusion.refs_0_), channel_id=1, source_target_pairs={{0,24},{1,25},{2,26},{3,27},{4,28},{5,29},{6,30},{7,31},{8,16},{9,... | collective-permute-start | bytes 276488 | tf_op jit(solution)/shard_map/ppermute | solution.py:612
  23.6 2.5 %collective-permute-done.12.refs_3_ = bf16[48,768]{1,0:T(8,128)(2,1)S(1)} collective-permute-done((bf16[48,768]{1,0:T(8,128)(2,1)}, bf16[48,768]{1,0:T(8,128)(2,1)S(1)}, u32[]{:S(2)}, u32[]{:S(2)}) %collective-permute-start.12) | collective-permute-done | bytes 73760 | tf_op jit(solution)/shard_map/ppermute | solution.py:612
  29.1 1.6 collective-permute-start.13
  32.2 6.0 %collective-permute-done.4.refs_2_.refs_10_ = bf16[96,1536]{1,0:T(8,128)(2,1)S(1)} collective-permute-done((bf16[96,1536]{1,0:T(8,128)(2,1)S(1)}, bf16[96,1536]{1,0:T(8,128)(2,1)S(1)}, u32[]{:S(2)}, u32[]{:S(2)}) %collective-permute-start.4) | collective-permute-done | bytes 294944 | tf_op jit(solution)/shard_map/ppermute | solution.py:612
  38.8 2.4 %collective-permute-start.24 = (bf16[96,1920]{1,0:T(8,128)(2,1)S(1)}, bf16[96,1920]{1,0:T(8,128)(2,1)S(1)}, u32[]{:S(2)}, u32[]{:S(2)}) collective-permute-start(bf16[96,1920]{1,0:T(8,128)(2,1)S(1)} %shard_map.189.refs_4_.refs_0_), channel_id=1, source_target_pairs={{0,4},{1,5},{2,6},{3,7},{4,0},{5,1},{6,2},{7,3},{8,12},{9,13},{10,... | collective-permute-start | bytes 1105928 | tf_op jit(solution)/shard_map/ppermute | solution.py:612
  42.9 2.1 collective-permute-start.15
  44.9 19.0 %collective-permute-done.15.refs_11_ = bf16[192,768]{1,0:T(8,128)(2,1)S(1)} collective-permute-done((bf16[192,768]{1,0:T(8,128)(2,1)S(1)}, bf16[192,768]{1,0:T(8,128)(2,1)S(1)}, u32[]{:S(2)}, u32[]{:S(2)}) %collective-permute-start.15) | collective-permute-done | bytes 294944 | tf_op jit(solution)/shard_map/ppermute | solution.py:612
  71.2 2.9 %shard_map.190 = (bf16[512,768]{1,0:T(8,128)(2,1)S(1)}, f32[8,1792]{1,0:T(8,128)S(1)}, f32[1,2304]{1,0:T(1,128)S(1)}) custom-call(bf16[512,768]{1,0:T(8,128)(2,1)S(1)} %copy-done, s32[1,768]{1,0:T(1,128)S(1)} %add.67.refs_1_.refs_18_, s32[32,1]{1,0:T(8,128)S(1)} %copy.22.refs_2_, s32[8,2304]{1,0:T(8,128)S(1)} %copy-done.30, ...), custom_call_target="tpu_custom_call" | custom-call | tf_op jit(solution)/shard_map/pallas_call | solution.py:590
  74.3 17.7 %shard_map.191 = (f32[512,1792]{1,0:T(8,128)S(1)}, f32[512,128]{1,0:T(8,128)S(1)}, f32[512,1536]{1,0:T(8,128)S(1)}, f32[512,1536]{1,0:T(8,128)S(1)}) custom-call(bf16[96,1920]{1,0:T(8,128)(2,1)S(1)} %shard_map.189.refs_4_.refs_0_, bf16[96,1920]{1,0:T(8,128)(2,1)S(1)} %collective-permute-done.23.refs_5_.refs_1_, ...), custom_call_target="tpu_custom_call" | custom-call | tf_op jit(solution)/shard_map/pallas_call | solution.py:590
  92.1 13.0 %shard_map.192 = (bf16[384,3072]{1,0:T(8,128)(2,1)S(1)}, bf16[384,3072]{1,0:T(8,128)(2,1)}, f32[512,1536]{1,0:T(8,128)S(1)}, bf16[512,1536]{1,0:T(8,128)(2,1)S(1...) custom-call(bf16[96,1536]{1,0:T(8,128)(2,1)S(1)} %copy-done.3, ...), custom_call_target="tpu_custom_call" | custom-call | tf_op jit(solution)/shard_map/pallas_call | solution.py:590
  105.3 25.3 %shard_map.194 = (bf16[512,1920]{1,0:T(8,128)(2,1)S(1)}, f32[8,1792]{1,0:T(8,128)S(1)}, f32[1,1536]{1,0:T(1,128)S(1)}, f32[8,128]{1,0:T(8,128)S(1)}) custom-call(f32[512,1536]{1,0:T(8,128)S(1)} %get-tuple-element.115.g_ref, f32[512,1536]{1,0:T(8,128)S(1)} %get-tuple-element.116.yd_ref, f32[512,1792]{1,0:T(8,128)S(1)} %get-tuple-element.117.ci_ref, ...), custom_call_target="tpu_custom_call" | custom-call | tf_op jit(solution)/shard_map/pallas_call | solution.py:590
  130.7 3.0 %shard_map.196 = (bf16[384,1920]{1,0:T(8,128)(2,1)S(1)}, bf16[384,1920]{1,0:T(8,128)(2,1)}) custom-call(bf16[512,768]{1,0:T(8,128)(2,1)S(1)} %get-tuple-element.109.refs_8_.refs_17_.xn_ref, bf16[512,1920]{1,0:T(8,128)(2,1)S(1)} %get-tuple-element.119.refs_16_.dp_ref), custom_call_target="tpu_custom_call" | custom-call | tf_op jit(solution)/shard_map/pallas_call | solution.py:590
  135.2 9.2 %shard_map.195 = (f32[512,768]{1,0:T(8,128)}, f32[8,2304]{1,0:T(8,128)S(1)}) custom-call(bf16[96,1920]{1,0:T(8,128)(2,1)S(1)} %shard_map.189.refs_4_.refs_0_, bf16[96,1920]{1,0:T(8,128)(2,1)S(1)} %collective-permute-done.23.refs_5_.refs_1_, bf16[96,1920]{1,0:T(8,128)(2,1)S(1)} %collective-permute-done.24.refs_6_.refs_2_, ...), custom_call_target="tpu_custom_call" | custom-call | tf_op jit(solution)/shard_map/pallas_call | solution.py:590
  151.3 1.8 collective-permute-done.47
  153.1 2.3 %collective-permute-start.48 = (f32[8,2304]{1,0:T(8,128)S(1)}, f32[8,2304]{1,0:T(8,128)S(1)}, u32[]{:S(2)}, u32[]{:S(2)}) collective-permute-start(f32[8,2304]{1,0:T(8,128)S(1)} %add_add_fusion.1), channel_id=1, source_target_pairs={{0,8},{1,9},{2,10},{3,11},{4,12},{5,13},{6,14},{7,15},{8,0},{9,1},... | collective-permute-start | bytes 221192 | tf_op jit(solution)/shard_map/ppermute | solution.py:612
  157.9 1.7 copy-done.8
  161.0 2.3 %shard_map.193 = bf16[512,768]{1,0:T(8,128)(2,1)} custom-call(bf16[512,1536]{1,0:T(8,128)(2,1)S(1)} %copy-done.10, bf16[1536,768]{1,0:T(8,128)(2,1)S(1)} %copy-done.8, bf16[512,768]{1,0:T(8,128)(2,1)S(1)} %copy-done), custom_call_target="tpu_custom_call" | custom-call | tf_op jit(solution)/shard_map/pallas_call | solution.py:590
  163.2 1.9 shard_map.197
  166.6 2.2 shard_map.199
  170.2 2.3 %collective-permute-start.40 = (bf16[96,3072]{1,0:T(8,128)(2,1)S(1)}, bf16[96,3072]{1,0:T(8,128)(2,1)S(1)}, u32[]{:S(2)}, u32[]{:S(2)}) collective-permute-start(bf16[96,3072]{1,0:T(8,128)(2,1)S(1)} %get-tuple-element.141), channel_id=1, source_target_pairs={{0,6},{1,7},{2,4},{3,5},{4,2},{5,3},{6,0},{7,1},{8,14},{9,15},{10,... | collective-permute-start | bytes 1769480 | tf_op jit(solution)/shard_map/ppermute | solution.py:612
  173.2 16.1 %collective-permute-done.38.refs_1_ = bf16[96,3072]{1,0:T(8,128)(2,1)S(1)} collective-permute-done((bf16[96,3072]{1,0:T(8,128)(2,1)S(1)}, bf16[96,3072]{1,0:T(8,128)(2,1)S(1)}, u32[]{:S(2)}, u32[]{:S(2)}) %collective-permute-start.38) | collective-permute-done | bytes 589856 | tf_op jit(solution)/shard_map/ppermute | solution.py:612
  189.3 1.6 collective-permute-start.33
  191.4 10.7 %collective-permute-done.40.refs_3_ = bf16[96,3072]{1,0:T(8,128)(2,1)S(1)} collective-permute-done((bf16[96,3072]{1,0:T(8,128)(2,1)S(1)}, bf16[96,3072]{1,0:T(8,128)(2,1)S(1)}, u32[]{:S(2)}, u32[]{:S(2)}) %collective-permute-start.40) | collective-permute-done | bytes 589856 | tf_op jit(solution)/shard_map/ppermute | solution.py:612
  203.6 2.0 collective-permute-start.42
  208.4 2.3 %collective-permute-done.32.refs_2_ = bf16[96,1920]{1,0:T(8,128)(2,1)S(1)} collective-permute-done((bf16[96,1920]{1,0:T(8,128)(2,1)S(1)}, bf16[96,1920]{1,0:T(8,128)(2,1)S(1)}, u32[]{:S(2)}, u32[]{:S(2)}) %collective-permute-start.32) | collective-permute-done | bytes 368672 | tf_op jit(solution)/shard_map/ppermute | solution.py:612
  211.6 2.2 collective-permute-start.35
  216.9 4.5 %collective-permute-done.35.c_ref = bf16[24,1920]{1,0:T(8,128)(2,1)S(1)} collective-permute-done((bf16[24,1920]{1,0:T(8,128)(2,1)S(1)}, bf16[24,1920]{1,0:T(8,128)(2,1)S(1)}, u32[]{:S(2)}, u32[]{:S(2)}) %collective-permute-start.35) | collective-permute-done | bytes 92192 | tf_op jit(solution)/shard_map/ppermute | solution.py:612
  (184 shorter events, 46.7 us)
Async XLA Ops:
  1.7 12.4 %collective-permute-start = (bf16[24,1536]{1,0:T(8,128)(2,1)S(1)}, bf16[24,1536]{1,0:T(8,128)(2,1)S(1)}, u32[]{:S(2)}, u32[]{:S(2)}) collective-permute-start(bf16[24,1536]{1,0:T(8,128)(2,1)S(1)} %slice.114.refs_0_), channel_id=1, source_target_pairs={{0,8},{1,9},{2,10},{3,11},{4,12},{5,13},{6,14},{7,15},{8,0},{9,1},... | collective-permute-start | bytes 221192 | tf_op jit(solution)/shard_map/ppermute | solution.py:612
  7.3 12.5 %collective-permute-start.10 = (bf16[48,768]{1,0:T(8,128)(2,1)}, bf16[48,768]{1,0:T(8,128)(2,1)S(1)}, u32[]{:S(2)}, u32[]{:S(2)}) collective-permute-start(bf16[48,768]{1,0:T(8,128)(2,1)} %refs_0_.2), channel_id=1, source_target_pairs={{0,8},{1,9},{2,10},{3,11},{4,12},{5,13},{6,14},{7,15},{8,0},{9,1},... | collective-permute-start | bytes 221192 | tf_op jit(solution)/shard_map/ppermute | solution.py:612
  8.2 13.0 %collective-permute-start.11 = (bf16[48,768]{1,0:T(8,128)(2,1)}, bf16[48,768]{1,0:T(8,128)(2,1)S(1)}, u32[]{:S(2)}, u32[]{:S(2)}) collective-permute-start(bf16[48,768]{1,0:T(8,128)(2,1)} %refs_0_.2), channel_id=1, source_target_pairs={{0,16},{1,17},{2,18},{3,19},{4,20},{5,21},{6,22},{7,23},{8,24},{9,... | collective-permute-start | bytes 221192 | tf_op jit(solution)/shard_map/ppermute | solution.py:612
  14.3 16.4 %collective-permute-start.3 = (bf16[96,1536]{1,0:T(8,128)(2,1)S(1)}, bf16[96,1536]{1,0:T(8,128)(2,1)}, u32[]{:S(2)}, u32[]{:S(2)}) collective-permute-start(bf16[96,1536]{1,0:T(8,128)(2,1)S(1)} %shard_map.187.refs_0_.refs_8_), channel_id=1, source_target_pairs={{0,2},{1,3},{2,0},{3,1},{4,6},{5,7},{6,4},{7,5},{8,10},{9,11},{10,... | collective-permute-start | bytes 884744 | tf_op jit(solution)/shard_map/ppermute | solution.py:612
  15.9 11.8 %collective-permute-start.20 = (bf16[24,1920]{1,0:T(8,128)(2,1)S(1)}, bf16[24,1920]{1,0:T(8,128)(2,1)S(1)}, u32[]{:S(2)}, u32[]{:S(2)}) collective-permute-start(bf16[24,1920]{1,0:T(8,128)(2,1)S(1)} %pad_maximum_fusion.refs_0_), channel_id=1, source_target_pairs={{0,8},{1,9},{2,10},{3,11},{4,12},{5,13},{6,14},{7,15},{8,0},{9,1},... | collective-permute-start | bytes 276488 | tf_op jit(solution)/shard_map/ppermute | solution.py:612
  26.2 12.0 %collective-permute-start.4 = (bf16[96,1536]{1,0:T(8,128)(2,1)S(1)}, bf16[96,1536]{1,0:T(8,128)(2,1)S(1)}, u32[]{:S(2)}, u32[]{:S(2)}) collective-permute-start(bf16[96,1536]{1,0:T(8,128)(2,1)S(1)} %shard_map.187.refs_0_.refs_8_), channel_id=1, source_target_pairs={{0,4},{1,5},{2,6},{3,7},{4,0},{5,1},{6,2},{7,3},{8,12},{9,13},{10,... | collective-permute-start | bytes 884744 | tf_op jit(solution)/shard_map/ppermute | solution.py:612
  28.2 13.1 %collective-permute-start.6 = (bf16[96,1536]{1,0:T(8,128)(2,1)S(1)}, bf16[96,1536]{1,0:T(8,128)(2,1)S(1)}, u32[]{:S(2)}, u32[]{:S(2)}) collective-permute-start(bf16[96,1536]{1,0:T(8,128)(2,1)S(1)} %shard_map.187.refs_0_.refs_8_), channel_id=1, source_target_pairs={{0,1},{1,0},{2,3},{3,2},{4,5},{5,4},{6,7},{7,6},{8,9},{9,8},{10,11... | collective-permute-start | bytes 884744 | tf_op jit(solution)/shard_map/ppermute | solution.py:612
  29.1 13.7 %collective-permute-start.13 = (bf16[192,768]{1,0:T(8,128)(2,1)S(1)}, bf16[192,768]{1,0:T(8,128)(2,1)S(1)}, u32[]{:S(2)}, u32[]{:S(2)}) collective-permute-start(bf16[192,768]{1,0:T(8,128)(2,1)S(1)} %shard_map.188.refs_8_), channel_id=1, source_target_pairs={{0,2},{1,3},{2,0},{3,1},{4,6},{5,7},{6,4},{7,5},{8,10},{9,11},{10,... | collective-permute-start | bytes 884744 | tf_op jit(solution)/shard_map/ppermute | solution.py:612
  30.7 14.3 %collective-permute-start.14 = (bf16[192,768]{1,0:T(8,128)(2,1)S(1)}, bf16[192,768]{1,0:T(8,128)(2,1)S(1)}, u32[]{:S(2)}, u32[]{:S(2)}) collective-permute-start(bf16[192,768]{1,0:T(8,128)(2,1)S(1)} %shard_map.188.refs_8_), channel_id=1, source_target_pairs={{0,4},{1,5},{2,6},{3,7},{4,0},{5,1},{6,2},{7,3},{8,12},{9,13},{10,... | collective-permute-start | bytes 884744 | tf_op jit(solution)/shard_map/ppermute | solution.py:612
  38.2 25.7 %collective-permute-start.23 = (bf16[96,1920]{1,0:T(8,128)(2,1)S(1)}, bf16[96,1920]{1,0:T(8,128)(2,1)S(1)}, u32[]{:S(2)}, u32[]{:S(2)}) collective-permute-start(bf16[96,1920]{1,0:T(8,128)(2,1)S(1)} %shard_map.189.refs_4_.refs_0_), channel_id=1, source_target_pairs={{0,2},{1,3},{2,0},{3,1},{4,6},{5,7},{6,4},{7,5},{8,10},{9,11},{10,... | collective-permute-start | bytes 1105928 | tf_op jit(solution)/shard_map/ppermute | solution.py:612
  38.8 26.5 %collective-permute-start.24 = (bf16[96,1920]{1,0:T(8,128)(2,1)S(1)}, bf16[96,1920]{1,0:T(8,128)(2,1)S(1)}, u32[]{:S(2)}, u32[]{:S(2)}) collective-permute-start(bf16[96,1920]{1,0:T(8,128)(2,1)S(1)} %shard_map.189.refs_4_.refs_0_), channel_id=1, source_target_pairs={{0,4},{1,5},{2,6},{3,7},{4,0},{5,1},{6,2},{7,3},{8,12},{9,13},{10,... | collective-permute-start | bytes 1105928 | tf_op jit(solution)/shard_map/ppermute | solution.py:612
  42.0 23.3 %collective-permute-start.25 = (bf16[96,1920]{1,0:T(8,128)(2,1)S(1)}, bf16[96,1920]{1,0:T(8,128)(2,1)S(1)}, u32[]{:S(2)}, u32[]{:S(2)}) collective-permute-start(bf16[96,1920]{1,0:T(8,128)(2,1)S(1)} %shard_map.189.refs_4_.refs_0_), channel_id=1, source_target_pairs={{0,6},{1,7},{2,4},{3,5},{4,2},{5,3},{6,0},{7,1},{8,14},{9,15},{10,... | collective-permute-start | bytes 1105928 | tf_op jit(solution)/shard_map/ppermute | solution.py:612
  42.9 21.0 %collective-permute-start.15 = (bf16[192,768]{1,0:T(8,128)(2,1)S(1)}, bf16[192,768]{1,0:T(8,128)(2,1)S(1)}, u32[]{:S(2)}, u32[]{:S(2)}) collective-permute-start(bf16[192,768]{1,0:T(8,128)(2,1)S(1)} %shard_map.188.refs_8_), channel_id=1, source_target_pairs={{0,6},{1,7},{2,4},{3,5},{4,2},{5,3},{6,0},{7,1},{8,14},{9,15},{10,... | collective-permute-start | bytes 884744 | tf_op jit(solution)/shard_map/ppermute | solution.py:612
  44.9 20.9 %collective-permute-start.16 = (bf16[192,768]{1,0:T(8,128)(2,1)S(1)}, bf16[192,768]{1,0:T(8,128)(2,1)S(1)}, u32[]{:S(2)}, u32[]{:S(2)}) collective-permute-start(bf16[192,768]{1,0:T(8,128)(2,1)S(1)} %shard_map.188.refs_8_), channel_id=1, source_target_pairs={{0,1},{1,0},{2,3},{3,2},{4,5},{5,4},{6,7},{7,6},{8,9},{9,8},{10,11... | collective-permute-start | bytes 884744 | tf_op jit(solution)/shard_map/ppermute | solution.py:612
  66.6 25.3 %collective-permute-start.8 = (bf16[96,1536]{1,0:T(8,128)(2,1)}, bf16[96,1536]{1,0:T(8,128)(2,1)}, u32[]{:S(2)}, u32[]{:S(2)}) collective-permute-start(bf16[96,1536]{1,0:T(8,128)(2,1)} %copy-done.13), channel_id=1, source_target_pairs={{0,1},{1,0},{2,3},{3,2},{4,5},{5,4},{6,7},{7,6},{8,9},{9,8},{10,11... | collective-permute-start | bytes 884744 | tf_op jit(solution)/shard_map/ppermute | solution.py:612
  68.5 23.5 %collective-permute-start.9 = (bf16[96,1536]{1,0:T(8,128)(2,1)}, bf16[96,1536]{1,0:T(8,128)(2,1)}, u32[]{:S(2)}, u32[]{:S(2)}) collective-permute-start(bf16[96,1536]{1,0:T(8,128)(2,1)} %copy-done.15), channel_id=1, source_target_pairs={{0,1},{1,0},{2,3},{3,2},{4,5},{5,4},{6,7},{7,6},{8,9},{9,8},{10,11... | collective-permute-start | bytes 884744 | tf_op jit(solution)/shard_map/ppermute | solution.py:612
  68.6 23.4 %collective-permute-start.17 = (bf16[192,768]{1,0:T(8,128)(2,1)}, bf16[192,768]{1,0:T(8,128)(2,1)}, u32[]{:S(2)}, u32[]{:S(2)}) collective-permute-start(bf16[192,768]{1,0:T(8,128)(2,1)} %copy-done.21), channel_id=1, source_target_pairs={{0,1},{1,0},{2,3},{3,2},{4,5},{5,4},{6,7},{7,6},{8,9},{9,8},{10,11... | collective-permute-start | bytes 884744 | tf_op jit(solution)/shard_map/ppermute | solution.py:612
  69.0 23.0 %collective-permute-start.18 = (bf16[192,768]{1,0:T(8,128)(2,1)}, bf16[192,768]{1,0:T(8,128)(2,1)}, u32[]{:S(2)}, u32[]{:S(2)}) collective-permute-start(bf16[192,768]{1,0:T(8,128)(2,1)} %copy-done.23), channel_id=1, source_target_pairs={{0,1},{1,0},{2,3},{3,2},{4,5},{5,4},{6,7},{7,6},{8,9},{9,8},{10,11... | collective-permute-start | bytes 884744 | tf_op jit(solution)/shard_map/ppermute | solution.py:612
  69.1 22.9 %collective-permute-start.19 = (bf16[192,768]{1,0:T(8,128)(2,1)}, bf16[192,768]{1,0:T(8,128)(2,1)}, u32[]{:S(2)}, u32[]{:S(2)}) collective-permute-start(bf16[192,768]{1,0:T(8,128)(2,1)} %copy-done.25), channel_id=1, source_target_pairs={{0,1},{1,0},{2,3},{3,2},{4,5},{5,4},{6,7},{7,6},{8,9},{9,8},{10,11... | collective-permute-start | bytes 884744 | tf_op jit(solution)/shard_map/ppermute | solution.py:612
  105.1 61.5 %collective-permute-start.37 = (bf16[384,3072]{1,0:T(8,128)(2,1)}, bf16[384,3072]{1,0:T(8,128)(2,1)}, u32[]{:S(2)}, u32[]{:S(2)}) collective-permute-start(bf16[384,3072]{1,0:T(8,128)(2,1)} %get-tuple-element.137), channel_id=1, source_target_pairs={{0,1},{1,0},{2,3},{3,2},{4,5},{5,4},{6,7},{7,6},{8,9},{9,8},{10,11... | collective-permute-start | bytes 7077896 | tf_op jit(solution)/shard_map/ppermute | solution.py:612
  134.9 28.4 %collective-permute-start.30 = (bf16[384,1920]{1,0:T(8,128)(2,1)}, bf16[384,1920]{1,0:T(8,128)(2,1)}, u32[]{:S(2)}, u32[]{:S(2)}) collective-permute-start(bf16[384,1920]{1,0:T(8,128)(2,1)} %get-tuple-element.127), channel_id=1, source_target_pairs={{0,1},{1,0},{2,3},{3,2},{4,5},{5,4},{6,7},{7,6},{8,9},{9,8},{10,11... | collective-permute-start | bytes 4423688 | tf_op jit(solution)/shard_map/ppermute | solution.py:612
  153.1 16.3 %collective-permute-start.48 = (f32[8,2304]{1,0:T(8,128)S(1)}, f32[8,2304]{1,0:T(8,128)S(1)}, u32[]{:S(2)}, u32[]{:S(2)}) collective-permute-start(f32[8,2304]{1,0:T(8,128)S(1)} %add_add_fusion.1), channel_id=1, source_target_pairs={{0,8},{1,9},{2,10},{3,11},{4,12},{5,13},{6,14},{7,15},{8,0},{9,1},... | collective-permute-start | bytes 221192 | tf_op jit(solution)/shard_map/ppermute | solution.py:612
  155.4 14.7 %collective-permute-start.49 = (f32[8,2304]{1,0:T(8,128)S(1)}, f32[8,2304]{1,0:T(8,128)S(1)}, u32[]{:S(2)}, u32[]{:S(2)}) collective-permute-start(f32[8,2304]{1,0:T(8,128)S(1)} %add_add_fusion.1), channel_id=1, source_target_pairs={{0,16},{1,17},{2,18},{3,19},{4,20},{5,21},{6,22},{7,23},{8,24},{9,... | collective-permute-start | bytes 221192 | tf_op jit(solution)/shard_map/ppermute | solution.py:612
  156.5 16.0 %collective-permute-start.50 = (f32[8,2304]{1,0:T(8,128)S(1)}, f32[8,2304]{1,0:T(8,128)S(1)}, u32[]{:S(2)}, u32[]{:S(2)}) collective-permute-start(f32[8,2304]{1,0:T(8,128)S(1)} %add_add_fusion.1), channel_id=1, source_target_pairs={{0,24},{1,25},{2,26},{3,27},{4,28},{5,29},{6,30},{7,31},{8,16},{9,... | collective-permute-start | bytes 221192 | tf_op jit(solution)/shard_map/ppermute | solution.py:612
  165.1 40.5 %collective-permute-start.31 = (bf16[96,1920]{1,0:T(8,128)(2,1)S(1)}, bf16[96,1920]{1,0:T(8,128)(2,1)S(1)}, u32[]{:S(2)}, u32[]{:S(2)}) collective-permute-start(bf16[96,1920]{1,0:T(8,128)(2,1)S(1)} %get-tuple-element.129), channel_id=1, source_target_pairs={{0,2},{1,3},{2,0},{3,1},{4,6},{5,7},{6,4},{7,5},{8,10},{9,11},{10,... | collective-permute-start | bytes 1105928 | tf_op jit(solution)/shard_map/ppermute | solution.py:612
  168.8 20.4 %collective-permute-start.38 = (bf16[96,3072]{1,0:T(8,128)(2,1)S(1)}, bf16[96,3072]{1,0:T(8,128)(2,1)S(1)}, u32[]{:S(2)}, u32[]{:S(2)}) collective-permute-start(bf16[96,3072]{1,0:T(8,128)(2,1)S(1)} %get-tuple-element.139), channel_id=1, source_target_pairs={{0,2},{1,3},{2,0},{3,1},{4,6},{5,7},{6,4},{7,5},{8,10},{9,11},{10,... | collective-permute-start | bytes 1769480 | tf_op jit(solution)/shard_map/ppermute | solution.py:612
  169.5 21.9 %collective-permute-start.39 = (bf16[96,3072]{1,0:T(8,128)(2,1)S(1)}, bf16[96,3072]{1,0:T(8,128)(2,1)S(1)}, u32[]{:S(2)}, u32[]{:S(2)}) collective-permute-start(bf16[96,3072]{1,0:T(8,128)(2,1)S(1)} %get-tuple-element.140), channel_id=1, source_target_pairs={{0,4},{1,5},{2,6},{3,7},{4,0},{5,1},{6,2},{7,3},{8,12},{9,13},{10,... | collective-permute-start | bytes 1769480 | tf_op jit(solution)/shard_map/ppermute | solution.py:612
  170.2 32.0 %collective-permute-start.40 = (bf16[96,3072]{1,0:T(8,128)(2,1)S(1)}, bf16[96,3072]{1,0:T(8,128)(2,1)S(1)}, u32[]{:S(2)}, u32[]{:S(2)}) collective-permute-start(bf16[96,3072]{1,0:T(8,128)(2,1)S(1)} %get-tuple-element.141), channel_id=1, source_target_pairs={{0,6},{1,7},{2,4},{3,5},{4,2},{5,3},{6,0},{7,1},{8,14},{9,15},{10,... | collective-permute-start | bytes 1769480 | tf_op jit(solution)/shard_map/ppermute | solution.py:612
  172.4 38.2 %collective-permute-start.32 = (bf16[96,1920]{1,0:T(8,128)(2,1)S(1)}, bf16[96,1920]{1,0:T(8,128)(2,1)S(1)}, u32[]{:S(2)}, u32[]{:S(2)}) collective-permute-start(bf16[96,1920]{1,0:T(8,128)(2,1)S(1)} %get-tuple-element.130), channel_id=1, source_target_pairs={{0,4},{1,5},{2,6},{3,7},{4,0},{5,1},{6,2},{7,3},{8,12},{9,13},{10,... | collective-permute-start | bytes 1105928 | tf_op jit(solution)/shard_map/ppermute | solution.py:612
  189.3 21.4 %collective-permute-start.33 = (bf16[96,1920]{1,0:T(8,128)(2,1)S(1)}, bf16[96,1920]{1,0:T(8,128)(2,1)S(1)}, u32[]{:S(2)}, u32[]{:S(2)}) collective-permute-start(bf16[96,1920]{1,0:T(8,128)(2,1)S(1)} %get-tuple-element.131), channel_id=1, source_target_pairs={{0,6},{1,7},{2,4},{3,5},{4,2},{5,3},{6,0},{7,1},{8,14},{9,15},{10,... | collective-permute-start | bytes 1105928 | tf_op jit(solution)/shard_map/ppermute | solution.py:612
  202.4 11.4 %collective-permute-start.41 = (bf16[24,3072]{1,0:T(8,128)(2,1)S(1)}, bf16[24,3072]{1,0:T(8,128)(2,1)S(1)}, u32[]{:S(2)}, u32[]{:S(2)}) collective-permute-start(bf16[24,3072]{1,0:T(8,128)(2,1)S(1)} %get-tuple-element.143), channel_id=1, source_target_pairs={{0,8},{1,9},{2,10},{3,11},{4,12},{5,13},{6,14},{7,15},{8,0},{9,1},... | collective-permute-start | bytes 442376 | tf_op jit(solution)/shard_map/ppermute | solution.py:612
  203.6 12.3 %collective-permute-start.42 = (bf16[24,3072]{1,0:T(8,128)(2,1)S(1)}, bf16[24,3072]{1,0:T(8,128)(2,1)S(1)}, u32[]{:S(2)}, u32[]{:S(2)}) collective-permute-start(bf16[24,3072]{1,0:T(8,128)(2,1)S(1)} %get-tuple-element.144), channel_id=1, source_target_pairs={{0,16},{1,17},{2,18},{3,19},{4,20},{5,21},{6,22},{7,23},{8,24},{9,... | collective-permute-start | bytes 442376 | tf_op jit(solution)/shard_map/ppermute | solution.py:612
  (55 other events, 1069.0 us)

commit v2 on v1

--- a/solution.py
+++ b/solution.py
@@ -35,7 +35,8 @@
     return lax.broadcasted_iota(jnp.int32, shape, dim)
 
 
-def perm_matrix(dvec, width):
+def perm_matrix(me, tab_ref, width):
+    dvec = (tab_ref[0:1, :] ^ me) * tab_ref[2:3, 0:1] + tab_ref[1:2, :]
     return (iota((width, width), 0) == dvec).astype(F32).astype(BF16)
 
 
@@ -43,20 +44,35 @@
     return jnp.concatenate([ref[:, lanes] for ref in refs], axis=0)
 
 
-def normed_of(hid_ref, gain, dvec_ref, xn_ref):
+def normed_of(hid_ref, gain, me, tab_ref, xn_ref):
     tokens = hid_ref[...].astype(F32)
     scale = lax.rsqrt(jnp.mean(tokens * tokens, axis=-1, keepdims=True) + 1e-05)
     normed = (tokens * scale * gain).astype(BF16)
-    perm = perm_matrix(dvec_ref[...], tokens.shape[1])
+    perm = perm_matrix(me, tab_ref, tokens.shape[1])
     xn_ref[...] = mm(normed, perm).astype(BF16)
 
 
-def norm_kernel(hid_ref, gains_ref, dvec_ref, xn_ref):
-    normed_of(hid_ref, gains_ref[:, : hid_ref.shape[1]], dvec_ref, xn_ref)
-
-
-def prep_kernel(at, taps_n, hid_ref, dvec_ref, owner_ref, where_ref, *refs):
-    pieces, (xn_ref, taps_ref, gains_ref) = refs[:-3], refs[-3:]
+def pack_kernel(inner, w_ref, taps_in, gains_in, conv_ref, gate_ref):
+    gate_ref[...] = w_ref[:, :inner]
+    body = conv_ref.shape[1] - BLK
+    conv_ref[:, :body] = w_ref[:, inner : inner + body]
+    tail = w_ref[:, inner + body :]
+    spare = tail.shape[1]
+    rows, taps_n = w_ref.shape[0], taps_in.shape[0]
+
+    def onto(x, at):
+        return mm(x, (iota((x.shape[1], BLK), 1) == iota((x.shape[1], BLK), 0) + at).astype(F32).astype(BF16))
+
+    row = iota((rows, BLK), 0)
+    tile_of = onto(tail, 0)
+    taps_wide, gains_wide = onto(taps_in[...], spare), onto(gains_in[...], spare)
+    for j in range(taps_n):
+        tile_of = tile_of + jnp.where(row == j, taps_wide[j : j + 1, :], 0.0)
+    tile_of = tile_of + jnp.where(row == taps_n, gains_wide, 0.0)
+    conv_ref[:, body:] = tile_of.astype(BF16)
+
+
+def unpack(at, taps_n, pieces, me, owner_ref, where_ref, taps_ref, gains_ref):
     last = pieces[0].shape[1] - BLK
     tail = rows_of(pieces, slice(last, last + BLK))
     devices = owner_ref.shape[0]
@@ -71,18 +87,27 @@
         lane, owner = where_ref[line : line + 1, :width], where_ref[line + 1 : line + 2, :width]
         chosen = (iota((BLK, width), 0) == lane + at).astype(F32).astype(BF16)
         wide = mm(part, chosen)
-        return jnp.sum(jnp.where(owner_ref[...] == owner, wide, 0.0), axis=0, keepdims=True)
+        return jnp.sum(jnp.where((owner_ref[...] ^ me) == owner, wide, 0.0), axis=0, keepdims=True)
 
     channels, width = taps_ref.shape[1], gains_ref.shape[1]
     taps_ref[...] = jnp.zeros_like(taps_ref)
     for j in range(taps_n):
         taps_ref[j : j + 1, :] = spread(small[j * devices : (j + 1) * devices], 0, channels)
     gains_ref[...] = spread(small[taps_n * devices : (taps_n + 1) * devices], 2, width)
-    normed_of(hid_ref, gains_ref[:, : hid_ref.shape[1]], dvec_ref, xn_ref)
-
-
-def head_setup(dt_raw, heads_ref, step_ref, cc_ref, al_ref, ew_ref, wq_ref, cct_ref):
+
+
+def split3(x):
+    hi, rest = split2(x)
+    lo = (x - hi.astype(F32) - rest.astype(F32)).astype(BF16)
+    return hi, rest, lo
+
+
+def head_setup(dt_raw, rows_in, segr, heads_ref, step_ref, cc_ref, wide_ref, cct_ref, segb_ref):
     length = dt_raw.shape[0]
+    heads_ref[...] = jnp.zeros_like(heads_ref)
+    for k, ref in enumerate(rows_in):
+        heads_ref[k : k + 1, : ref.shape[1]] = ref[...]
+    segb_ref[...] = jnp.broadcast_to(segr, (BLK, length)).T
     biased = dt_raw + heads_ref[2:3, :]
     step = jnp.maximum(biased, 0.0) + jnp.log1p(jnp.exp(-jnp.abs(biased)))
     step_ref[...] = step
@@ -91,19 +116,16 @@
     for i in range(length // BLK):
         rows = slice(i * BLK, (i + 1) * BLK)
         cc = jnp.dot(lower, rate[rows], precision=HIGH, preferred_element_type=F32)
-        cc_ref[rows, :] = cc
-        al_ref[rows, :] = jnp.exp2(cc)
+        cc_ref[rows, :] = jnp.concatenate(split3(cc), axis=1)
         ew = jnp.exp2(jnp.minimum(cc[BLK - 1 : BLK, :] - cc, 0.0))
-        ew_ref[rows, :] = ew
-        wq_ref[rows, :] = ew * step[rows]
+        for k, x in enumerate((step[rows], ew * step[rows], jnp.exp2(cc), ew)):
+            wide_ref[k, rows, :] = jnp.concatenate(split2(x), axis=1)
         cct_ref[:, rows] = cc.T[: cct_ref.shape[0]]
 
 
-def mask_setup(segc_ref, mask_ref):
-    seg = segc_ref[...]
-    length = seg.shape[0]
-    pos = iota((length, BLK), 0)
-    segb = jnp.broadcast_to(seg, (length, BLK))
+def mask_setup(segb_ref, mask_ref):
+    segb = segb_ref[...]
+    pos = iota(segb.shape, 0)
     for j in range(1, mask_ref.shape[0] + 1):
         prev = pltpu.roll(segb, j, axis=0)
         mask_ref[j - 1] = ((prev == segb) & (pos >= j)).astype(F32)
@@ -122,30 +144,38 @@
     return 0.5 * jnp.tanh(0.5 * x) + 0.5
 
 
-def score_setup(bmat, cmat, segc_ref, segr_ref, sd_ref, so_ref, sdt_ref, sot_ref):
+def score_setup(bmat, cmat, segb_ref, segr, sd_ref, so_ref, sdt_ref, sot_ref):
     length = bmat.shape[0]
     bb, cb = bmat.astype(BF16), cmat.astype(BF16)
     causal = iota((BLK, BLK), 0) >= iota((BLK, BLK), 1)
     for i in range(length // BLK):
         rows = slice(i * BLK, (i + 1) * BLK)
         before = slice((i - 1) * BLK, i * BLK)
-        same = (segc_ref[rows, :] == segr_ref[:, rows]) & causal
+        same = (segb_ref[rows, :] == segr[:, rows]) & causal
         diag = jnp.where(same, mm_nt(cb[rows], bb[rows]), 0.0)
         if sd_ref is not None:
             sd_ref[i] = diag
         if sdt_ref is not None:
             sdt_ref[i] = diag.T
         if i > 0:
-            linked = segc_ref[rows, :] == segr_ref[:, before]
+            linked = segb_ref[rows, :] == segr[:, before]
             off = jnp.where(linked, mm_nt(cb[rows], bb[before]), 0.0)
             so_ref[i] = off.astype(BF16)
             if sot_ref is not None:
                 sot_ref[i] = off.T.astype(BF16)
 
 
-def pair_lanes(ref, shift, low):
-    both = pltpu.roll(ref[...], shift, axis=1)
-    return jnp.where(low, both[:, 0:1], both[:, 1:2])
+def pair_setup(t, heads_ref, wide_ref, cc_ref, cct_ref, count):
+    head = iota((2 * BLK, BLK), 0) & (BLK - 1)
+    pick = (head == 2 * t + jnp.where(iota((2 * BLK, BLK), 1) < BLK // 2, 0, 1)).astype(F32).astype(BF16)
+    spread = [mm(wide_ref[k], pick) for k in range(count)]
+    head = iota((3 * BLK, 2 * BLK), 0) & (BLK - 1)
+    each = (head == 2 * t + jnp.where(iota((3 * BLK, 2 * BLK), 1) < BLK, 0, 1)).astype(F32).astype(BF16)
+    c2 = mm(cc_ref[...], each)
+    r2 = pltpu.roll(cct_ref[...], lax.rem(cct_ref.shape[0] - 2 * t, cct_ref.shape[0]), axis=0)
+    h2 = pltpu.roll(heads_ref[...], lax.rem(BLK - 2 * t, BLK), axis=1)
+    skip = jnp.where(iota((1, BLK), 1) < BLK // 2, h2[1:2, 0:1], h2[1:2, 1:2])
+    return spread, c2, r2, skip
 
 
 def block_diag(x, low):
@@ -153,54 +183,63 @@
     return jnp.concatenate([jnp.where(low, x, zero), jnp.where(low, zero, x)], axis=0)
 
 
-def scan_fwd_kernel(pieces, *refs):
+def scan_fwd_kernel(pieces, packed, *refs):
     w_refs = refs[:pieces]
     (
-        xn_ref, taps_ref, segc_ref, segr_ref, heads_ref, skip_ref,
-        ci_ref, dt_ref, sc_ref, yd_ref,
-        step_ref, cc_ref, al_ref, ew_ref, wq_ref, cct_ref, mask_ref, sd_ref, so_ref,
+        me_ref, tab_ref, hid_ref, first_ref, second_ref, segr_ref, alog_ref, skip_ref, bias_ref,
+        xn_ref, taps_ref, gains_ref, wc_ref, ci_ref, dt_ref, sc_ref, yd_ref, v_ref, slope_ref,
+        heads_ref, step_ref, cc_ref, wide_ref, cct_ref, segb_ref, mask_ref, sd_ref, so_ref,
     ) = refs[pieces:]
+    me = me_ref[0]
+    segr = segr_ref[...].astype(F32)
     length = xn_ref.shape[0]
     channels = ci_ref.shape[1]
     states = BLK
     inner = channels - 2 * states
-
+    if packed:
+        unpack(packed[0], packed[1], w_refs, me, first_ref, second_ref, taps_ref, gains_ref)
+    else:
+        taps_ref[...] = first_ref[...]
+        gains_ref[...] = second_ref[...]
+    normed_of(hid_ref, gains_ref[:, : hid_ref.shape[1]], me, tab_ref, xn_ref)
     xn = xn_ref[...]
-    ci_ref[...] = mm(xn, rows_of(w_refs, slice(0, channels)))
-    dt_ref[...] = mm(xn, rows_of(w_refs, slice(channels, channels + BLK)))
-    head_setup(dt_ref[...], heads_ref, step_ref, cc_ref, al_ref, ew_ref, wq_ref, cct_ref)
-    mask_setup(segc_ref, mask_ref)
+    wc_ref[...] = rows_of(w_refs)
+    ci_ref[...] = mm(xn, wc_ref[:, :channels])
+    dt_ref[...] = mm(xn, wc_ref[:, channels:])
+    head_setup(
+        dt_ref[...], (alog_ref, skip_ref, bias_ref), segr, heads_ref, step_ref, cc_ref, wide_ref, cct_ref, segb_ref
+    )
+    mask_setup(segb_ref, mask_ref)
     lanes_b = slice(inner, inner + states)
     lanes_c = slice(inner + states, channels)
     _, pre_b = conv_parts(ci_ref[:, lanes_b], taps_ref, lanes_b, mask_ref)
     _, pre_c = conv_parts(ci_ref[:, lanes_c], taps_ref, lanes_c, mask_ref)
     score_setup(
         pre_b * sigmoid(pre_b), pre_c * sigmoid(pre_c),
-        segc_ref, segr_ref, sd_ref, so_ref, None, None,
+        segb_ref, segr, sd_ref, so_ref, None, None,
     )
 
     def body(t, carry):
         lanes = pl.ds(pl.multiple_of(t * BLK, BLK), BLK)
         _, pre = conv_parts(ci_ref[:, lanes], taps_ref, lanes, mask_ref)
-        v = pre * sigmoid(pre)
+        v, slope = silu_and_slope(pre)
+        v_ref[:, lanes] = v
+        slope_ref[:, lanes] = slope
         low = iota((1, BLK), 1) < BLK // 2
-        shift = lax.rem(BLK - 2 * t, BLK)
-        vt = (v * pair_lanes(step_ref, shift, low)).astype(BF16)
-        vp = (v * pair_lanes(wq_ref, shift, low)).astype(BF16)
-        al2 = pair_lanes(al_ref, shift, low)
-        c2 = pltpu.roll(cc_ref[...], shift, axis=1)
-        r2 = pltpu.roll(cct_ref[...], lax.rem(cct_ref.shape[0] - 2 * t, cct_ref.shape[0]), axis=0)
+        (st2, wq2, al2), c2, r2, skip = pair_setup(t, heads_ref, wide_ref, cc_ref, cct_ref, 3)
+        vt = (v * st2).astype(BF16)
+        vp = (v * wq2).astype(BF16)
         for i in range(length // BLK):
             rows = slice(i * BLK, (i + 1) * BLK)
             before = slice((i - 1) * BLK, i * BLK)
             ms = []
             for k in range(2):
                 row = r2[k : k + 1, rows]
-                d = jnp.exp2(jnp.minimum(c2[rows, k : k + 1] - row, 0.0))
+                d = jnp.exp2(jnp.minimum(c2[rows, k * BLK : (k + 1) * BLK] - row, 0.0))
                 ms.append((sd_ref[i] * d).astype(BF16))
             yd = mm(jnp.concatenate(ms, axis=1), block_diag(vt[rows], low))
             yd_ref[rows, lanes] = yd
-            y = yd + skip_ref[:, lanes] * v[rows]
+            y = yd + skip * v[rows]
             if i > 0:
                 y = y + al2[rows] * mm(so_ref[i], vp[before])
             sc_ref[rows, lanes] = y
@@ -209,14 +248,15 @@
     lax.fori_loop(0, inner // BLK, body, 0)
 
 
-def mid_kernel(pieces, *refs):
+def mid_kernel(pieces, table, *refs):
     gw_refs, ow_refs = refs[:pieces], refs[pieces : 2 * pieces]
     (
-        order_ref, xn_ref, sc_ref, gains_ref, cot_ref,
-        lo_ref, hi_ref, g_ref, dgate_ref, mixed_ref, ginner_ref, wo_ref,
-        gate_ref, dm_ref, nat_ref,
+        me_ref, xn_ref, sc_ref, gains_ref, cot_ref,
+        lo_ref, hi_ref, g_ref, dgate_ref, mixed_ref, ginner_ref, wo_ref, wg_ref,
+        dm_ref, nat_ref,
     ) = refs[2 * pieces :]
-    devices = order_ref.shape[0]
+    me = me_ref[0]
+    devices = len(table)
     share = wo_ref.shape[0] // devices
     per = ow_refs[0].shape[0] // share
     gain = slice(xn_ref.shape[1], gains_ref.shape[1])
@@ -224,12 +264,13 @@
     width = cot_ref.shape[1]
     rows_in = xn_ref.shape[1] // devices
     xn = xn_ref[...]
-    gate_ref[...] = mm(xn, rows_of(gw_refs))
+    wg_ref[...] = rows_of(gw_refs)
+    g_ref[...] = mm(xn, wg_ref[...])
     if share % 16:
         wo_ref[...] = rows_of(ow_refs)
     else:
         for p in range(devices):
-            at = pl.multiple_of(order_ref[p] * share, 16)
+            at = pl.multiple_of((me ^ int(table[p])) * share, 16)
             row = (p % per) * share
             wo_ref[pl.ds(at, share), :] = ow_refs[p // per][row : row + share, :]
     dm_ref[...] = mm_nt(cot_ref[...], wo_ref[...])
@@ -239,7 +280,7 @@
 
     def body(k, carry):
         rows = pl.ds(pl.multiple_of(k * sub, sub), sub)
-        gate = gate_ref[rows, :]
+        gate = g_ref[rows, :]
         sig = sigmoid(gate)
         silu = gate * sig
         scanned = sc_ref[rows, :]
@@ -271,15 +312,16 @@
         row = (p % (devices // 2)) * rows_in
         for k in range(2):
             both = [
-                nat_ref[pl.ds(pl.multiple_of(order_ref[q] * share + k * rows_in, 8), rows_in), :]
+                nat_ref[pl.ds(pl.multiple_of((me ^ int(table[q])) * share + k * rows_in, 8), rows_in), :]
                 for q in (p, p + 1)
             ]
             lanes = slice(inner + k * width, inner + (k + 1) * width)
             target[row : row + 2 * rows_in, lanes] = jnp.concatenate(both, axis=0).astype(BF16)
 
 
-def branch_kernel(mixed_ref, wo_ref, hid_ref, out_ref):
+def branch_kernel(mixed_ref, wo_ref, hid_ref, dgate_ref, wg_ref, out_ref, dn_ref):
     out_ref[...] = (hid_ref[...].astype(F32) + mm(mixed_ref[...], wo_ref[...])).astype(BF16)
+    dn_ref[...] = mm_nt(dgate_ref[...], wg_ref[...])
 
 
 def conv_back(dpre, x, taps_ref, lanes, mask_ref, dtaps_ref, dp_ref, to):
@@ -306,12 +348,13 @@
 
 
 def scan_bwd_kernel(
-    g_ref, yd_ref, ci_ref, dt_ref, taps_ref, segc_ref, segr_ref, heads_ref, skip_ref,
+    g_ref, yd_ref, v_ref, slope_ref, ci_ref, dt_ref, taps_ref, segr_ref, alog_ref, skip_ref, bias_ref,
     dp_ref, dtaps_ref, dskip_ref, dheads_ref,
-    step_ref, cc_ref, al_ref, ew_ref, wq_ref, cct_ref, mask_ref,
+    heads_ref, step_ref, cc_ref, wide_ref, cct_ref, segb_ref, mask_ref,
     sdt_ref, so_ref, sot_ref, dsdt_ref, dso_ref, acc_ref, dpre_ref,
 ):
     length = ci_ref.shape[0]
+    segr = segr_ref[...].astype(F32)
     blocks = length // BLK
     channels = ci_ref.shape[1]
     states = BLK
@@ -320,15 +363,17 @@
     lanes_b = slice(inner, inner + states)
     lanes_c = slice(inner + states, channels)
 
-    head_setup(dt_ref[...], heads_ref, step_ref, cc_ref, al_ref, ew_ref, wq_ref, cct_ref)
-    mask_setup(segc_ref, mask_ref)
+    head_setup(
+        dt_ref[...], (alog_ref, skip_ref, bias_ref), segr, heads_ref, step_ref, cc_ref, wide_ref, cct_ref, segb_ref
+    )
+    mask_setup(segb_ref, mask_ref)
     dheads_ref[...] = jnp.zeros_like(dheads_ref)
     dtaps_ref[...] = jnp.zeros_like(dtaps_ref)
     _, pre_b = conv_parts(ci_ref[:, lanes_b], taps_ref, lanes_b, mask_ref)
     _, pre_c = conv_parts(ci_ref[:, lanes_c], taps_ref, lanes_c, mask_ref)
     score_setup(
         pre_b * sigmoid(pre_b), pre_c * sigmoid(pre_c),
-        segc_ref, segr_ref, None, so_ref, sdt_ref, sot_ref,
+        segb_ref, segr, None, so_ref, sdt_ref, sot_ref,
     )
     dsdt_ref[...] = jnp.zeros_like(dsdt_ref)
     dso_ref[...] = jnp.zeros_like(dso_ref)
@@ -337,26 +382,19 @@
     def body(t, carry):
         lanes = pl.ds(pl.multiple_of(t * BLK, BLK), BLK)
         x = ci_ref[:, lanes]
-        _, pre = conv_parts(x, taps_ref, lanes, mask_ref)
-        v, slope = silu_and_slope(pre)
+        v = v_ref[:, lanes]
         low = iota((1, BLK), 1) < BLK // 2
-        shift = lax.rem(BLK - 2 * t, BLK)
-        st2 = pair_lanes(step_ref, shift, low)
-        wq2 = pair_lanes(wq_ref, shift, low)
-        ew2 = pair_lanes(ew_ref, shift, low)
-        al2 = pair_lanes(al_ref, shift, low)
-        c2 = pltpu.roll(cc_ref[...], shift, axis=1)
-        r2 = pltpu.roll(cct_ref[...], lax.rem(cct_ref.shape[0] - 2 * t, cct_ref.shape[0]), axis=0)
+        (st2, wq2, al2, ew2), c2, r2, skip = pair_setup(t, heads_ref, wide_ref, cc_ref, cct_ref, 4)
         vtb = (v * st2).astype(BF16)
         vpb = (v * wq2).astype(BF16)
         g = g_ref[:, lanes]
         gb = g.astype(BF16)
         gpb = (al2 * g).astype(BF16)
         dskip_ref[:, lanes] = jnp.sum(g * v, axis=0, keepdims=True)
-        k_row = iota((4 * BLK, BLK), 0)
+        k_row = iota((3 * BLK, BLK), 0)
         target = jnp.where(k_row >= 2 * BLK, BLK // 2, 0) + 2 * t
         target = target + jnp.where((k_row & (BLK - 1)) >= BLK // 2, 1, 0)
-        collect = (iota((4 * BLK, BLK), 1) == target).astype(F32).astype(BF16)
+        collect = (iota((3 * BLK, BLK), 1) == target).astype(F32).astype(BF16)
         for i in range(blocks):
             rows = slice(i * BLK, (i + 1) * BLK)
             before = slice((i - 1) * BLK, i * BLK)
@@ -367,13 +405,13 @@
             part = jnp.zeros((BLK, BLK), F32)
             for k in range(2):
                 row = r2[k : k + 1, rows]
-                d = jnp.exp2(jnp.minimum(row - c2[rows, k : k + 1], 0.0))
+                d = jnp.exp2(jnp.minimum(row - c2[rows, k * BLK : (k + 1) * BLK], 0.0))
                 ms.append((sdt_ref[i] * d).astype(BF16))
                 part = part + both[:, k * BLK : (k + 1) * BLK] * d
             dsdt_ref[i] += part
             dvt = mm(jnp.concatenate(ms, axis=1), gdiag)
             x1 = gb[rows].astype(F32) * yd_ref[rows, lanes] - dvt * vtb[rows].astype(F32)
-            dv = st2[rows] * dvt + skip_ref[:, lanes] * g[rows]
+            dv = st2[rows] * dvt + skip * g[rows]
             dstep = dvt
             if i > 0:
                 z = mm(so_ref[i], vpb[before])
@@ -385,9 +423,9 @@
                 dv = dv + wq2[rows] * dvp
                 dstep = dstep + ew2[rows] * dvp
             h1, l1 = split2(x1)
-            h2, l2 = split2(dstep * v[rows])
-            acc_ref[rows, :] += mm(jnp.concatenate([h1, l1, h2, l2], axis=1), collect)
-            dpre_ref[rows, :] = dv * slope[rows]
+            h2 = (dstep * v[rows]).astype(BF16)
+            acc_ref[rows, :] += mm(jnp.concatenate([h1, l1, h2], axis=1), collect)
+            dpre_ref[rows, :] = dv * slope_ref[rows, lanes]
         conv_back(dpre_ref[...], x, taps_ref, lanes, mask_ref, dtaps_ref, dp_ref, lanes)
         return carry
 
@@ -404,10 +442,10 @@
     for i in range(blocks):
         rows = slice(i * BLK, (i + 1) * BLK)
         before = slice((i - 1) * BLK, i * BLK)
-        same = (segc_ref[rows, :] == segr_ref[:, rows]) & causal_t
+        same = (segb_ref[rows, :] == segr[:, rows]) & causal_t
         dst.append(jnp.where(same, dsdt_ref[i], 0.0))
         if i > 0:
-            linked = segc_ref[rows, :] == segr_ref[:, before]
+            linked = segb_ref[rows, :] == segr[:, before]
             dso.append(jnp.where(linked, dso_ref[i], 0.0))
     for i in range(blocks):
         rows = slice(i * BLK, (i + 1) * BLK)
@@ -453,15 +491,13 @@
     hi_ref[...] = grad[half:]
 
 
-def input_kernel(pieces, *refs):
-    cw_refs, gw_refs = refs[:pieces], refs[pieces : 2 * pieces]
-    (
-        dp_ref, dgate_ref, dvec_ref, hid_ref, cot_ref, gains_ref,
-        dtaps_ref, ginner_ref, dskip_ref, dheads_ref,
-        ig_ref, sums_ref,
-    ) = refs[2 * pieces :]
-    dn = mm_nt(dp_ref[...], rows_of(cw_refs)) + mm_nt(dgate_ref[...], rows_of(gw_refs))
-    perm = perm_matrix(dvec_ref[...], dn.shape[1])
+def input_kernel(
+    wc_ref, dng_ref, dp_ref, me_ref, tab_ref, hid_ref, cot_ref, gains_ref,
+    dtaps_ref, ginner_ref, dskip_ref, dheads_ref,
+    ig_ref, sums_ref,
+):
+    dn = mm_nt(dp_ref[...], wc_ref[...]) + dng_ref[...]
+    perm = perm_matrix(me_ref[0], tab_ref, dn.shape[1])
     hi, lo = split2(dn)
     dn = mm_nt(hi, perm) + mm_nt(lo, perm)
     tokens = hid_ref[...].astype(F32)
@@ -518,30 +554,30 @@
     return pltpu.VMEM(shape, dtype)
 
 
-PARAMS = dict(compiler_params=pltpu.CompilerParams(vmem_limit_bytes=20 * 1024 * 1024))
-
-
-def head_scratch(length, inner):
+def scan_scratch(length, inner, taps):
     nheads = -(-2 * inner // (8 * BLK)) * 8
-    return [pltpu.VMEM((length, BLK), F32)] * 5 + [pltpu.VMEM((nheads, length), F32)]
-
-
-def scan_scratch(length, inner, taps):
-    return head_scratch(length, inner) + [pltpu.VMEM((taps - 1, length, BLK), F32)]
-
-
-def scan_fwd(weights, taps_n, xn, taps, segc, segr, heads, skip_row):
-    length = xn.shape[0]
-    channels, inner = taps.shape[1], skip_row.shape[1]
+    return [
+        pltpu.VMEM((8, BLK), F32), pltpu.VMEM((length, BLK), F32), pltpu.VMEM((length, 3 * BLK), BF16),
+        pltpu.VMEM((4, length, 2 * BLK), BF16), pltpu.VMEM((nheads, length), F32), pltpu.VMEM((length, BLK), F32),
+        pltpu.VMEM((taps - 1, length, BLK), F32),
+    ]
+
+
+def scan_fwd(weights, packed, taps_n, widths, mine, tab, hidden, first, second, segr, *heads):
+    length, width = hidden.shape
+    channels, inner = widths
     blocks = length // BLK
     count = len(weights)
+    rows = held((length, inner), F32)
     return call(
-        lambda *refs: scan_fwd_kernel(count, *refs),
+        lambda *refs: scan_fwd_kernel(count, packed, *refs),
         (
-            held((length, channels), F32), held((length, BLK), F32),
-            held((length, inner), F32), held((length, inner), F32),
+            held((length, width), BF16), held((8, channels), F32), held((1, width + inner), F32),
+            held((width, channels + BLK), BF16),
+            held((length, channels), F32), held((length, BLK), F32), rows, rows, rows, rows,
         ),
-        *weights, xn, taps, segc, segr, heads, skip_row,
+        *weights, mine, tab, hidden, first, second, segr, *heads, scalar=count,
+        leave=(tab, first, second, segr) + heads,
         scratch=scan_scratch(length, inner, taps_n - 1) + [
             pltpu.VMEM((blocks, BLK, BLK), F32),
             pltpu.VMEM((blocks, BLK, BLK), BF16),
@@ -549,9 +585,9 @@
     )
 
 
-def scan_bwd(taps_n, g, yd, ci, dt, taps, segc, segr, heads, skip_row):
+def scan_bwd(taps_n, g, yd, v, slope, ci, dt, taps, segr, *heads):
     length, channels = ci.shape
-    inner = skip_row.shape[1]
+    inner = g.shape[1]
     score = (length // BLK, BLK, BLK)
     return call(
         scan_bwd_kernel,
@@ -559,7 +595,7 @@
             held((length, channels + BLK), BF16), held(taps.shape, F32), held((1, inner), F32),
             held((8, BLK), F32),
         ),
-        g, yd, ci, dt, taps, segc, segr, heads, skip_row,
+        g, yd, v, slope, ci, dt, taps, segr, *heads, leave=(segr,) + heads,
         scratch=scan_scratch(length, inner, taps_n - 1) + [
             pltpu.VMEM(score, F32),
             pltpu.VMEM(score, BF16),
@@ -572,23 +608,19 @@
     )
 
 
-def prep(at, taps_n, hidden, dvec, owner, where, pieces, channels, width):
-    return call(
-        lambda *refs: prep_kernel(at, taps_n, *refs),
-        (held(hidden.shape, BF16), held((8, channels), F32), held((1, width), F32)),
-        hidden, dvec, owner, where, *pieces,
-    )
-
-
-def call(kernel, outs, *ins, scratch=(), scalar=None):
+def call(kernel, outs, *ins, scratch=(), scalar=None, leave=()):
     specs = [
         pl.BlockSpec(memory_space=pltpu.SMEM if k == scalar else pltpu.VMEM) for k in range(len(ins))
     ]
-    near = [a if k == scalar else pltpu.with_memory_space_constraint(a, pltpu.VMEM) for k, a in enumerate(ins)]
+    near = [
+        a if k == scalar else pltpu.with_memory_space_constraint(a, pltpu.HBM if any(a is b for b in leave) else pltpu.VMEM)
+        for k, a in enumerate(ins)
+    ]
     many = isinstance(outs, (tuple, list))
     out_specs = [pl.BlockSpec(memory_space=pltpu.VMEM) for _ in outs] if many else pl.BlockSpec(memory_space=pltpu.VMEM)
     return pl.pallas_call(
-        kernel, out_shape=outs, in_specs=specs, out_specs=out_specs, scratch_shapes=list(scratch), **PARAMS
+        kernel, out_shape=outs, in_specs=specs, out_specs=out_specs, scratch_shapes=list(scratch),
+        compiler_params=pltpu.CompilerParams(vmem_limit_bytes=(20 if scratch else 8) * 1024 * 1024),
     )(*near)
 
 
@@ -675,46 +707,53 @@
     inner = w_out.shape[0] * devices
     proj = w_in.shape[1]
     rows_in, rows_out = w_in.shape[0], w_out.shape[0]
+    pairs = inner // BLK
+    first = pairs // 2
 
     table = order_table(devices)
     inverse = np.argsort(table).astype(np.int32)
     order = jnp.asarray(table) ^ me
     place = jnp.asarray(inverse)[me ^ jnp.arange(devices)]
-    dvec = (order[:, None] * rows_in + jnp.arange(rows_in)[None, :]).reshape(1, width)
+    mine = me.reshape(1).astype(jnp.int32)
+    tab = np.zeros((8, width), np.int32)
+    tab[0], tab[1], tab[2] = np.repeat(table, rows_in), np.tile(np.arange(rows_in), devices), rows_in
+    tab = jnp.asarray(tab)
 
     spare = BLK - (proj - inner - channels)
     packed = rows_in > taps_n and max(tap_share, gain_share) <= spare
-    small = jnp.zeros((rows_in if packed else 8, BLK if not packed else spare), BF16)
-    small = small.at[:taps_n, :tap_share].set(conv_taps)
-    small = small.at[taps_n, :gain_share].set(gains)
     if packed:
-        w_conv = jnp.concatenate([w_in[:, inner:], small], axis=1)
+        gain_row = gains.reshape(1, gain_share)
+        w_conv, w_gate = call(
+            lambda *refs: pack_kernel(inner, *refs),
+            (held((rows_in, channels + BLK), BF16), held((rows_in, inner), BF16)),
+            w_in, conv_taps, gain_row, leave=(w_in, conv_taps, gain_row),
+        )
     else:
         w_conv = jnp.pad(w_in[:, inner:], ((0, 0), (0, spare)))
+        w_gate = w_in[:, :inner]
     cw = gather(w_conv, devices)
-    gw = gather(w_in[:, :inner], devices)
+    gw = gather(w_gate, devices)
     ow = gather(w_out, devices)
     count = len(cw)
 
-    heads = jnp.zeros((8, BLK), F32)
-    heads = heads.at[0, :nheads].set(a_log).at[1, :nheads].set(d_skip).at[2, :nheads].set(dt_bias)
-    skip_row = jnp.repeat(d_skip, inner // nheads)[None]
-    segc = segment_ids.reshape(length, 1)
+    heads = [x.reshape(1, nheads) for x in (a_log, d_skip, dt_bias)]
 
     if packed:
         at = np.arange(width + inner)
         where = np.stack([at % tap_share, at // tap_share, at % gain_share, at // gain_share])
-        where = jnp.asarray(np.pad(where, ((0, 4), (0, 0))).astype(np.int32))
-        xn, taps, gains_all = prep(
-            proj - inner - channels, taps_n, hidden, dvec, order.reshape(devices, 1), where, cw,
-            channels, width + inner,
-        )
+        second = jnp.asarray(np.pad(where, ((0, 4), (0, 0))).astype(np.int32))
+        first = jnp.asarray(table.reshape(devices, 1))
     else:
-        rows = jnp.concatenate(gather(small.astype(F32)[None], devices), axis=0)[place]
-        taps = jnp.moveaxis(rows[:, :, :tap_share], 0, 1).reshape(8, channels)
-        gains_all = rows[:, taps_n, :gain_share].reshape(1, width + inner)
-        xn = call(norm_kernel, sds((length, width), BF16), hidden, gains_all, dvec)
-    ci, dt, sc, yd = scan_fwd(cw, taps_n, xn, taps, segc, segment_ids, heads, skip_row)
+        small = jnp.zeros((8, BLK), F32)
+        small = small.at[:taps_n, :tap_share].set(conv_taps.astype(F32))
+        small = small.at[taps_n, :gain_share].set(gains.astype(F32))
+        rows = jnp.concatenate(gather(small[None], devices), axis=0)[place]
+        first = jnp.moveaxis(rows[:, :, :tap_share], 0, 1).reshape(8, channels)
+        second = rows[:, taps_n, :gain_share].reshape(1, width + inner)
+    xn, taps, gains_all, wc, ci, dt, sc, yd, v, slope = scan_fwd(
+        cw, (proj - inner - channels, taps_n) if packed else None, taps_n, (channels, inner),
+        mine, tab, hidden, first, second, segment_ids, *heads,
+    )
     if rows_out % 16:
         wo_all = jnp.concatenate(ow, axis=0).reshape(devices, rows_out, width)[place].reshape(inner, width)
         ow = [wo_all[k * (inner // count) : (k + 1) * (inner // count)] for k in range(count)]
@@ -723,16 +762,15 @@
         halves = (held((width // 2, inner + 2 * width), BF16), held((width // 2, inner + 2 * width), BF16))
     else:
         halves = (sds((width, inner), BF16), sds((inner, width), BF16))
-    lo, hi, g, dgate, mixed, ginner, wo = call(
-        lambda *refs: mid_kernel(count, *refs),
+    lo, hi, g, dgate, mixed, ginner, wo, wg = call(
+        lambda *refs: mid_kernel(count, table, *refs),
         halves + (
             held((length, inner), F32), held((length, inner), BF16), held((length, inner), BF16),
-            held((8, inner), F32), held((inner, width), BF16),
+            held((8, inner), F32), held((inner, width), BF16), held((width, inner), BF16),
         ),
-        *gw, *ow, order, xn, sc, gains_all, cot,
+        *gw, *ow, mine, xn, sc, gains_all, cot,
         scratch=(
-            pltpu.VMEM((length, inner), F32), pltpu.VMEM((length, inner), F32),
-            pltpu.VMEM((inner, width), F32),
+            pltpu.VMEM((length, inner), F32), pltpu.VMEM((inner, width), F32),
         ),
         scalar=2 * count,
     )
@@ -741,15 +779,18 @@
         both = jnp.concatenate([lo, gwo[:, 0].reshape(width, width), gwo[:, 1].reshape(width, width)], axis=1)
         lo, hi = both[: width // 2], both[width // 2 :]
     mid_parts = reduce_shares(lo, hi, devices)
-    output = call(branch_kernel, sds((length, width), BF16), mixed, wo, hidden)
-    dp, dtaps, dskip, dheads = scan_bwd(taps_n, g, yd, ci, dt, taps, segc, segment_ids, heads, skip_row)
+    output, dng = call(
+        branch_kernel, (sds((length, width), BF16), held((length, width), F32)),
+        mixed, wo, hidden, dgate, wg,
+    )
+    dp, dtaps, dskip, dheads = scan_bwd(taps_n, g, yd, v, slope, ci, dt, taps, segment_ids, *heads)
     half = held((width // 2, dp.shape[1]), BF16)
     clo, chi = call(grad_in_kernel, (half, half), xn, dp)
     conv_parts_in = reduce_shares(clo, chi, devices)
     input_grad, sums = call(
-        lambda *refs: input_kernel(count, *refs),
-        (sds((length, width), F32), sds((8, width + inner), F32)),
-        *cw, *gw, dp, dgate, dvec, hidden, cot, gains_all, dtaps, ginner, dskip, dheads,
+        input_kernel,
+        (sds((length, width), F32), held((8, width + inner), F32)),
+        wc, dng, dp, mine, tab, hidden, cot, gains_all, dtaps, ginner, dskip, dheads, scalar=3, leave=(tab,),
     )
     if aligned and len(mid_parts) == 4:
         gate_share, out_share = call(

time: 223 us -> 228 us (1.022)
  Pallas kernels: 79.6 us -> 74.8 us
  waiting for transfers between devices: 69.1 us -> 73 us
  local copies, waits for them, and re-layouts: 13.4 us -> 16.5 us
    unnamed x72 -> x54, local copies, waits for them, and re-layouts: 6.64 us -> 14.7 us
    pallas_call x16, Pallas kernels: 79.6 us -> 74.8 us  [call(): pl.pallas_call(kernel, out_shape=outs, in_specs=specs, out_specs=out_spec...]
    ppermute x51, waiting for transfers between devices: 69.1 us -> 73 us  [send(): return lax.ppermute(x, 'fsdp', [(i, i ^ mask) for i in range(devices)])]
  transfers between devices with their start and end apart: 51 -> 51, of which waited for: 16 -> 17; matrix products, arithmetic and copies ran while one was open for 3% -> 2% of each run, Pallas kernels for 30% -> 26%
where the time goes in v2:
time: 228 us; the launch traced here: 227 us
  Pallas kernels  74.8 us (33%)
  waiting for transfers between devices  73 us (32%)
  starting transfers between devices  60 us (26%)
  local copies, waits for them, and re-layouts  16.5 us (7%)
    pallas_call x16, Pallas kernels, call(): pl.pallas_call(kernel, out_shape=outs, in_specs=specs, out_specs=out_spec...  74.8 us
    ppermute x51, waiting for transfers between devices, send(): return lax.ppermute(x, 'fsdp', [(i, i ^ mask) for i in range(devices)])  73 us
    ppermute x51, starting transfers between devices, send(): return lax.ppermute(x, 'fsdp', [(i, i ^ mask) for i in range(devices)])  60 us
    unnamed x54, local copies, waits for them, and re-layouts  14.7 us
  transfers between devices with their start and end apart: 51, of which 17 were waited for; matrix products, arithmetic and copies ran while one was open for 2% of the time, Pallas kernels for 26%

profile of v2, /device:TPU:0, one launch (start us, length us, event | category | flops | bytes accessed | tf_op | source)
XLA Modules:
  0.0 226.8 jit_solution(4179509164460267577)
XLA Ops:
  1.8 3.1 %collective-permute-start = (bf16[24,1536]{1,0:T(8,128)(2,1)S(1)}, bf16[24,1536]{1,0:T(8,128)(2,1)S(1)}, u32[]{:S(2)}, u32[]{:S(2)}) collective-permute-start(bf16[24,1536]{1,0:T(8,128)(2,1)S(1)} %get-tuple-element.57.refs_0_), channel_id=1, source_target_pairs={{0,8},{1,9},{2,10},{3,11},{4,12},{5,13},{6,14},{7,15},{8,0},{9,1},... | collective-permute-start | bytes 221192 | tf_op jit(solution)/shard_map/ppermute | solution.py:644
  4.9 2.6 %collective-permute-start.1 = (bf16[24,1536]{1,0:T(8,128)(2,1)S(1)}, bf16[24,1536]{1,0:T(8,128)(2,1)S(1)}, u32[]{:S(2)}, u32[]{:S(2)}) collective-permute-start(bf16[24,1536]{1,0:T(8,128)(2,1)S(1)} %get-tuple-element.57.refs_0_), channel_id=1, source_target_pairs={{0,16},{1,17},{2,18},{3,19},{4,20},{5,21},{6,22},{7,23},{8,24},{9,... | collective-permute-start | bytes 221192 | tf_op jit(solution)/shard_map/ppermute | solution.py:644
  7.5 5.2 %collective-permute-done.1.refs_2_ = bf16[24,1536]{1,0:T(8,128)(2,1)S(1)} collective-permute-done((bf16[24,1536]{1,0:T(8,128)(2,1)S(1)}, bf16[24,1536]{1,0:T(8,128)(2,1)S(1)}, u32[]{:S(2)}, u32[]{:S(2)}) %collective-permute-start.1) | collective-permute-done | bytes 73760 | tf_op jit(solution)/shard_map/ppermute | solution.py:644
  16.4 1.7 collective-permute-start.11
  20.3 3.6 %collective-permute-start.12 = (bf16[48,768]{1,0:T(8,128)(2,1)}, bf16[48,768]{1,0:T(8,128)(2,1)S(1)}, u32[]{:S(2)}, u32[]{:S(2)}) collective-permute-start(bf16[48,768]{1,0:T(8,128)(2,1)} %refs_0_.3), channel_id=1, source_target_pairs={{0,24},{1,25},{2,26},{3,27},{4,28},{5,29},{6,30},{7,31},{8,16},{9,... | collective-permute-start | bytes 221192 | tf_op jit(solution)/shard_map/ppermute | solution.py:644
  23.9 1.9 collective-permute-done.11.refs_2_
  25.8 4.6 %collective-permute-start.22 = (bf16[24,1920]{1,0:T(8,128)(2,1)S(1)}, bf16[24,1920]{1,0:T(8,128)(2,1)S(1)}, u32[]{:S(2)}, u32[]{:S(2)}) collective-permute-start(bf16[24,1920]{1,0:T(8,128)(2,1)S(1)} %get-tuple-element.58.refs_0_), channel_id=1, source_target_pairs={{0,24},{1,25},{2,26},{3,27},{4,28},{5,29},{6,30},{7,31},{8,16},{9,... | collective-permute-start | bytes 276488 | tf_op jit(solution)/shard_map/ppermute | solution.py:644
  33.4 1.6 collective-permute-start.13
  36.5 3.8 %collective-permute-done.4.refs_2_ = bf16[96,1536]{1,0:T(8,128)(2,1)} collective-permute-done((bf16[96,1536]{1,0:T(8,128)(2,1)S(1)}, bf16[96,1536]{1,0:T(8,128)(2,1)}, u32[]{:S(2)}, u32[]{:S(2)}) %collective-permute-start.4) | collective-permute-done | bytes 294944 | tf_op jit(solution)/shard_map/ppermute | solution.py:644
  41.8 2.2 collective-permute-start.24
  45.2 2.0 collective-permute-done.13.refs_9_
  47.7 20.5 %collective-permute-done.15.refs_11_ = bf16[192,768]{1,0:T(8,128)(2,1)} collective-permute-done((bf16[192,768]{1,0:T(8,128)(2,1)S(1)}, bf16[192,768]{1,0:T(8,128)(2,1)}, u32[]{:S(2)}, u32[]{:S(2)}) %collective-permute-start.15) | collective-permute-done | bytes 294944 | tf_op jit(solution)/shard_map/ppermute | solution.py:644
  81.3 14.8 %shard_map.200 = (bf16[512,768]{1,0:T(8,128)(2,1)S(1)}, f32[8,1792]{1,0:T(8,128)S(1)}, f32[1,2304]{1,0:T(1,128)S(1)}, bf16[768,1920]{1,0:T(8,128)(2,1)S(1)}, f32...) custom-call(bf16[96,1920]{1,0:T(8,128)(2,1)S(1)} %shard_map.199.refs, ...), custom_call_target="tpu_custom_call" | custom-call | tf_op jit(solution)/shard_map/pallas_call | solution.py:621
  96.1 1.6 copy-done.2
  97.7 13.2 %shard_map.201 = (bf16[384,3072]{1,0:T(8,128)(2,1)S(1)}, bf16[384,3072]{1,0:T(8,128)(2,1)}, f32[512,1536]{1,0:T(8,128)S(1)}, bf16[512,1536]{1,0:T(8,128)(2,1)S(1...) custom-call(bf16[96,1536]{1,0:T(8,128)(2,1)S(1)} %shard_map.197.refs, ...), custom_call_target="tpu_custom_call" | custom-call | tf_op jit(solution)/shard_map/pallas_call | solution.py:621
  111.0 26.2 %shard_map.203 = (bf16[512,1920]{1,0:T(8,128)(2,1)S(1)}, f32[8,1792]{1,0:T(8,128)S(1)}, f32[1,1536]{1,0:T(1,128)S(1)}, f32[8,128]{1,0:T(8,128)S(1)}) custom-call(f32[512,1536]{1,0:T(8,128)S(1)} %get-tuple-element.69.g_ref, f32[512,1536]{1,0:T(8,128)S(1)} %get-tuple-element.70.yd_ref, f32[512,1536]{1,0:T(8,128)S(1)} %get-tuple-element.71.v_ref, ...), custom_call_target="tpu_custom_call" | custom-call | tf_op jit(solution)/shard_map/pallas_call | solution.py:621
  137.2 3.0 %shard_map.205 = (bf16[384,1920]{1,0:T(8,128)(2,1)S(1)}, bf16[384,1920]{1,0:T(8,128)(2,1)}) custom-call(bf16[512,768]{1,0:T(8,128)(2,1)S(1)} %get-tuple-element.59.refs_17_.xn_ref, bf16[512,1920]{1,0:T(8,128)(2,1)S(1)} %get-tuple-element.76.dp_ref), custom_call_target="tpu_custom_call" | custom-call | tf_op jit(solution)/shard_map/pallas_call | solution.py:621
  140.5 2.7 %shard_map.202 = (bf16[512,768]{1,0:T(8,128)(2,1)}, f32[512,768]{1,0:T(8,128)S(1)}) custom-call(bf16[512,1536]{1,0:T(8,128)(2,1)S(1)} %get-tuple-element.62.mixed_ref, bf16[1536,768]{1,0:T(8,128)(2,1)S(1)} %get-tuple-element.63.wo_ref, bf16[512,768]{1,0:T(8,128)(2,1)S(1)} %copy-done, bf16[512,1536]{1,0:T(8,128)(2,1)S(1)} %get-tuple-element.64.dgate_ref, ...), custom_call_target="tpu_custom_call" | custom-call | tf_op jit(solution)/shard_map/pallas_call | solution.py:621
  143.2 7.5 %shard_map.204 = (f32[512,768]{1,0:T(8,128)}, f32[8,2304]{1,0:T(8,128)S(1)}) custom-call(bf16[768,1920]{1,0:T(8,128)(2,1)S(1)} %copy-done.3, f32[512,768]{1,0:T(8,128)S(1)} %get-tuple-element.68.dng_ref, bf16[512,1920]{1,0:T(8,128)(2,1)S(1)} %get-tuple-element.76.dp_ref, s32[1]{0:T(128)} %bitcast.1.refs_8_.refs_16_.me_ref, ...), custom_call_target="tpu_custom_call" | custom-call | tf_op jit(solution)/shard_map/pallas_call | solution.py:621
  156.9 2.4 %collective-permute-done.47 = f32[8,2304]{1,0:T(8,128)S(1)} collective-permute-done((f32[8,2304]{1,0:T(8,128)S(1)}, f32[8,2304]{1,0:T(8,128)S(1)}, u32[]{:S(2)}, u32[]{:S(2)}) %collective-permute-start.47) | collective-permute-done | bytes 73760 | tf_op jit(solution)/shard_map/ppermute | solution.py:644
  159.4 4.5 %collective-permute-start.48 = (f32[8,2304]{1,0:T(8,128)S(1)}, f32[8,2304]{1,0:T(8,128)}, u32[]{:S(2)}, u32[]{:S(2)}) collective-permute-start(f32[8,2304]{1,0:T(8,128)S(1)} %add_add_fusion.1), channel_id=1, source_target_pairs={{0,8},{1,9},{2,10},{3,11},{4,12},{5,13},{6,14},{7,15},{8,0},{9,1},... | collective-permute-start | bytes 221192 | tf_op jit(solution)/shard_map/ppermute | solution.py:644
  163.8 2.4 %collective-permute-start.50 = (f32[8,2304]{1,0:T(8,128)S(1)}, f32[8,2304]{1,0:T(8,128)}, u32[]{:S(2)}, u32[]{:S(2)}) collective-permute-start(f32[8,2304]{1,0:T(8,128)S(1)} %add_add_fusion.1), channel_id=1, source_target_pairs={{0,24},{1,25},{2,26},{3,27},{4,28},{5,29},{6,30},{7,31},{8,16},{9,... | collective-permute-start | bytes 221192 | tf_op jit(solution)/shard_map/ppermute | solution.py:644
  167.6 2.2 shard_map.206
  171.3 2.2 shard_map.208
  174.8 2.3 collective-permute-start.40
  178.8 15.1 %collective-permute-done.38.refs_1_ = bf16[96,3072]{1,0:T(8,128)(2,1)S(1)} collective-permute-done((bf16[96,3072]{1,0:T(8,128)(2,1)S(1)}, bf16[96,3072]{1,0:T(8,128)(2,1)S(1)}, u32[]{:S(2)}, u32[]{:S(2)}) %collective-permute-start.38) | collective-permute-done | bytes 589856 | tf_op jit(solution)/shard_map/ppermute | solution.py:644
  193.9 1.6 collective-permute-start.33
  196.1 10.7 %collective-permute-done.40.refs_3_ = bf16[96,3072]{1,0:T(8,128)(2,1)S(1)} collective-permute-done((bf16[96,3072]{1,0:T(8,128)(2,1)S(1)}, bf16[96,3072]{1,0:T(8,128)(2,1)S(1)}, u32[]{:S(2)}, u32[]{:S(2)}) %collective-permute-start.40) | collective-permute-done | bytes 589856 | tf_op jit(solution)/shard_map/ppermute | solution.py:644
  209.2 2.4 %collective-permute-start.43 = (bf16[24,3072]{1,0:T(8,128)(2,1)S(1)}, bf16[24,3072]{1,0:T(8,128)(2,1)S(1)}, u32[]{:S(2)}, u32[]{:S(2)}) collective-permute-start(bf16[24,3072]{1,0:T(8,128)(2,1)S(1)} %get-tuple-element.101), channel_id=1, source_target_pairs={{0,24},{1,25},{2,26},{3,27},{4,28},{5,29},{6,30},{7,31},{8,16},{9,... | collective-permute-start | bytes 442376 | tf_op jit(solution)/shard_map/ppermute | solution.py:644
  213.0 2.3 collective-permute-done.32.refs_2_
  217.5 2.4 %collective-permute-start.36 = (bf16[24,1920]{1,0:T(8,128)(2,1)S(1)}, bf16[24,1920]{1,0:T(8,128)(2,1)S(1)}, u32[]{:S(2)}, u32[]{:S(2)}) collective-permute-start(bf16[24,1920]{1,0:T(8,128)(2,1)S(1)} %get-tuple-element.91), channel_id=1, source_target_pairs={{0,24},{1,25},{2,26},{3,27},{4,28},{5,29},{6,30},{7,31},{8,16},{9,... | collective-permute-start | bytes 276488 | tf_op jit(solution)/shard_map/ppermute | solution.py:644
  221.5 4.5 %collective-permute-done.35.c_ref = bf16[24,1920]{1,0:T(8,128)(2,1)S(1)} collective-permute-done((bf16[24,1920]{1,0:T(8,128)(2,1)S(1)}, bf16[24,1920]{1,0:T(8,128)(2,1)S(1)}, u32[]{:S(2)}, u32[]{:S(2)}) %collective-permute-start.35) | collective-permute-done | bytes 92192 | tf_op jit(solution)/shard_map/ppermute | solution.py:644
  (151 shorter events, 49.3 us)
Async XLA Ops:
  13.8 21.1 %collective-permute-start.3 = (bf16[96,1536]{1,0:T(8,128)(2,1)S(1)}, bf16[96,1536]{1,0:T(8,128)(2,1)S(1)}, u32[]{:S(2)}, u32[]{:S(2)}) collective-permute-start(bf16[96,1536]{1,0:T(8,128)(2,1)S(1)} %shard_map.197.refs_0_), channel_id=1, source_target_pairs={{0,2},{1,3},{2,0},{3,1},{4,6},{5,7},{6,4},{7,5},{8,10},{9,11},{10,... | collective-permute-start | bytes 884744 | tf_op jit(solution)/shard_map/ppermute | solution.py:644
  18.1 13.8 %collective-permute-start.20 = (bf16[24,1920]{1,0:T(8,128)(2,1)S(1)}, bf16[24,1920]{1,0:T(8,128)(2,1)S(1)}, u32[]{:S(2)}, u32[]{:S(2)}) collective-permute-start(bf16[24,1920]{1,0:T(8,128)(2,1)S(1)} %get-tuple-element.58.refs_0_), channel_id=1, source_target_pairs={{0,8},{1,9},{2,10},{3,11},{4,12},{5,13},{6,14},{7,15},{8,0},{9,1},... | collective-permute-start | bytes 276488 | tf_op jit(solution)/shard_map/ppermute | solution.py:644
  19.5 12.9 %collective-permute-start.21 = (bf16[24,1920]{1,0:T(8,128)(2,1)S(1)}, bf16[24,1920]{1,0:T(8,128)(2,1)S(1)}, u32[]{:S(2)}, u32[]{:S(2)}) collective-permute-start(bf16[24,1920]{1,0:T(8,128)(2,1)S(1)} %get-tuple-element.58.refs_0_), channel_id=1, source_target_pairs={{0,16},{1,17},{2,18},{3,19},{4,20},{5,21},{6,22},{7,23},{8,24},{9,... | collective-permute-start | bytes 276488 | tf_op jit(solution)/shard_map/ppermute | solution.py:644
  20.3 10.1 %collective-permute-start.12 = (bf16[48,768]{1,0:T(8,128)(2,1)}, bf16[48,768]{1,0:T(8,128)(2,1)S(1)}, u32[]{:S(2)}, u32[]{:S(2)}) collective-permute-start(bf16[48,768]{1,0:T(8,128)(2,1)} %refs_0_.3), channel_id=1, source_target_pairs={{0,24},{1,25},{2,26},{3,27},{4,28},{5,29},{6,30},{7,31},{8,16},{9,... | collective-permute-start | bytes 221192 | tf_op jit(solution)/shard_map/ppermute | solution.py:644
  31.9 9.9 %collective-permute-start.5 = (bf16[96,1536]{1,0:T(8,128)(2,1)S(1)}, bf16[96,1536]{1,0:T(8,128)(2,1)}, u32[]{:S(2)}, u32[]{:S(2)}) collective-permute-start(bf16[96,1536]{1,0:T(8,128)(2,1)S(1)} %shard_map.197.refs_0_), channel_id=1, source_target_pairs={{0,6},{1,7},{2,4},{3,5},{4,2},{5,3},{6,0},{7,1},{8,14},{9,15},{10,... | collective-permute-start | bytes 884744 | tf_op jit(solution)/shard_map/ppermute | solution.py:644
  32.4 11.6 %collective-permute-start.6 = (bf16[96,1536]{1,0:T(8,128)(2,1)S(1)}, bf16[96,1536]{1,0:T(8,128)(2,1)S(1)}, u32[]{:S(2)}, u32[]{:S(2)}) collective-permute-start(bf16[96,1536]{1,0:T(8,128)(2,1)S(1)} %shard_map.197.refs_0_), channel_id=1, source_target_pairs={{0,1},{1,0},{2,3},{3,2},{4,5},{5,4},{6,7},{7,6},{8,9},{9,8},{10,11... | collective-permute-start | bytes 884744 | tf_op jit(solution)/shard_map/ppermute | solution.py:644
  33.4 13.8 %collective-permute-start.13 = (bf16[192,768]{1,0:T(8,128)(2,1)S(1)}, bf16[192,768]{1,0:T(8,128)(2,1)}, u32[]{:S(2)}, u32[]{:S(2)}) collective-permute-start(bf16[192,768]{1,0:T(8,128)(2,1)S(1)} %shard_map.198.refs_8_), channel_id=1, source_target_pairs={{0,2},{1,3},{2,0},{3,1},{4,6},{5,7},{6,4},{7,5},{8,10},{9,11},{10,... | collective-permute-start | bytes 884744 | tf_op jit(solution)/shard_map/ppermute | solution.py:644
  34.9 12.8 %collective-permute-start.14 = (bf16[192,768]{1,0:T(8,128)(2,1)S(1)}, bf16[192,768]{1,0:T(8,128)(2,1)}, u32[]{:S(2)}, u32[]{:S(2)}) collective-permute-start(bf16[192,768]{1,0:T(8,128)(2,1)S(1)} %shard_map.198.refs_8_), channel_id=1, source_target_pairs={{0,4},{1,5},{2,6},{3,7},{4,0},{5,1},{6,2},{7,3},{8,12},{9,13},{10,... | collective-permute-start | bytes 884744 | tf_op jit(solution)/shard_map/ppermute | solution.py:644
  40.3 28.0 %collective-permute-start.23 = (bf16[96,1920]{1,0:T(8,128)(2,1)S(1)}, bf16[96,1920]{1,0:T(8,128)(2,1)S(1)}, u32[]{:S(2)}, u32[]{:S(2)}) collective-permute-start(bf16[96,1920]{1,0:T(8,128)(2,1)S(1)} %shard_map.199.refs_0_), channel_id=1, source_target_pairs={{0,2},{1,3},{2,0},{3,1},{4,6},{5,7},{6,4},{7,5},{8,10},{9,11},{10,... | collective-permute-start | bytes 1105928 | tf_op jit(solution)/shard_map/ppermute | solution.py:644
  41.8 26.9 %collective-permute-start.24 = (bf16[96,1920]{1,0:T(8,128)(2,1)S(1)}, bf16[96,1920]{1,0:T(8,128)(2,1)S(1)}, u32[]{:S(2)}, u32[]{:S(2)}) collective-permute-start(bf16[96,1920]{1,0:T(8,128)(2,1)S(1)} %shard_map.199.refs_0_), channel_id=1, source_target_pairs={{0,4},{1,5},{2,6},{3,7},{4,0},{5,1},{6,2},{7,3},{8,12},{9,13},{10,... | collective-permute-start | bytes 1105928 | tf_op jit(solution)/shard_map/ppermute | solution.py:644
  44.7 24.1 %collective-permute-start.25 = (bf16[96,1920]{1,0:T(8,128)(2,1)S(1)}, bf16[96,1920]{1,0:T(8,128)(2,1)S(1)}, u32[]{:S(2)}, u32[]{:S(2)}) collective-permute-start(bf16[96,1920]{1,0:T(8,128)(2,1)S(1)} %shard_map.199.refs_0_), channel_id=1, source_target_pairs={{0,6},{1,7},{2,4},{3,5},{4,2},{5,3},{6,0},{7,1},{8,14},{9,15},{10,... | collective-permute-start | bytes 1105928 | tf_op jit(solution)/shard_map/ppermute | solution.py:644
  47.2 21.0 %collective-permute-start.15 = (bf16[192,768]{1,0:T(8,128)(2,1)S(1)}, bf16[192,768]{1,0:T(8,128)(2,1)}, u32[]{:S(2)}, u32[]{:S(2)}) collective-permute-start(bf16[192,768]{1,0:T(8,128)(2,1)S(1)} %shard_map.198.refs_8_), channel_id=1, source_target_pairs={{0,6},{1,7},{2,4},{3,5},{4,2},{5,3},{6,0},{7,1},{8,14},{9,15},{10,... | collective-permute-start | bytes 884744 | tf_op jit(solution)/shard_map/ppermute | solution.py:644
  47.7 22.3 %collective-permute-start.16 = (bf16[192,768]{1,0:T(8,128)(2,1)S(1)}, bf16[192,768]{1,0:T(8,128)(2,1)S(1)}, u32[]{:S(2)}, u32[]{:S(2)}) collective-permute-start(bf16[192,768]{1,0:T(8,128)(2,1)S(1)} %shard_map.198.refs_8_), channel_id=1, source_target_pairs={{0,1},{1,0},{2,3},{3,2},{4,5},{5,4},{6,7},{7,6},{8,9},{9,8},{10,11... | collective-permute-start | bytes 884744 | tf_op jit(solution)/shard_map/ppermute | solution.py:644
  71.5 26.1 %collective-permute-start.8 = (bf16[96,1536]{1,0:T(8,128)(2,1)}, bf16[96,1536]{1,0:T(8,128)(2,1)}, u32[]{:S(2)}, u32[]{:S(2)}) collective-permute-start(bf16[96,1536]{1,0:T(8,128)(2,1)} %collective-permute-done.4.refs_2_), channel_id=1, source_target_pairs={{0,1},{1,0},{2,3},{3,2},{4,5},{5,4},{6,7},{7,6},{8,9},{9,8},{10,11... | collective-permute-start | bytes 884744 | tf_op jit(solution)/shard_map/ppermute | solution.py:644
  73.1 24.6 %collective-permute-start.9 = (bf16[96,1536]{1,0:T(8,128)(2,1)}, bf16[96,1536]{1,0:T(8,128)(2,1)}, u32[]{:S(2)}, u32[]{:S(2)}) collective-permute-start(bf16[96,1536]{1,0:T(8,128)(2,1)} %collective-permute-done.5.refs_3_), channel_id=1, source_target_pairs={{0,1},{1,0},{2,3},{3,2},{4,5},{5,4},{6,7},{7,6},{8,9},{9,8},{10,11... | collective-permute-start | bytes 884744 | tf_op jit(solution)/shard_map/ppermute | solution.py:644
  73.9 23.7 %collective-permute-start.17 = (bf16[192,768]{1,0:T(8,128)(2,1)}, bf16[192,768]{1,0:T(8,128)(2,1)}, u32[]{:S(2)}, u32[]{:S(2)}) collective-permute-start(bf16[192,768]{1,0:T(8,128)(2,1)} %collective-permute-done.13.refs_9_), channel_id=1, source_target_pairs={{0,1},{1,0},{2,3},{3,2},{4,5},{5,4},{6,7},{7,6},{8,9},{9,8},{10,11... | collective-permute-start | bytes 884744 | tf_op jit(solution)/shard_map/ppermute | solution.py:644
  75.0 22.6 %collective-permute-start.18 = (bf16[192,768]{1,0:T(8,128)(2,1)}, bf16[192,768]{1,0:T(8,128)(2,1)}, u32[]{:S(2)}, u32[]{:S(2)}) collective-permute-start(bf16[192,768]{1,0:T(8,128)(2,1)} %collective-permute-done.14.refs_10_), channel_id=1, source_target_pairs={{0,1},{1,0},{2,3},{3,2},{4,5},{5,4},{6,7},{7,6},{8,9},{9,8},{10,11... | collective-permute-start | bytes 884744 | tf_op jit(solution)/shard_map/ppermute | solution.py:644
  75.9 21.7 %collective-permute-start.19 = (bf16[192,768]{1,0:T(8,128)(2,1)}, bf16[192,768]{1,0:T(8,128)(2,1)}, u32[]{:S(2)}, u32[]{:S(2)}) collective-permute-start(bf16[192,768]{1,0:T(8,128)(2,1)} %collective-permute-done.15.refs_11_), channel_id=1, source_target_pairs={{0,1},{1,0},{2,3},{3,2},{4,5},{5,4},{6,7},{7,6},{8,9},{9,8},{10,11... | collective-permute-start | bytes 884744 | tf_op jit(solution)/shard_map/ppermute | solution.py:644
  110.9 60.5 %collective-permute-start.37 = (bf16[384,3072]{1,0:T(8,128)(2,1)}, bf16[384,3072]{1,0:T(8,128)(2,1)}, u32[]{:S(2)}, u32[]{:S(2)}) collective-permute-start(bf16[384,3072]{1,0:T(8,128)(2,1)} %get-tuple-element.93), channel_id=1, source_target_pairs={{0,1},{1,0},{2,3},{3,2},{4,5},{5,4},{6,7},{7,6},{8,9},{9,8},{10,11... | collective-permute-start | bytes 7077896 | tf_op jit(solution)/shard_map/ppermute | solution.py:644
  140.2 26.1 %collective-permute-start.30 = (bf16[384,1920]{1,0:T(8,128)(2,1)}, bf16[384,1920]{1,0:T(8,128)(2,1)}, u32[]{:S(2)}, u32[]{:S(2)}) collective-permute-start(bf16[384,1920]{1,0:T(8,128)(2,1)} %get-tuple-element.83), channel_id=1, source_target_pairs={{0,1},{1,0},{2,3},{3,2},{4,5},{5,4},{6,7},{7,6},{8,9},{9,8},{10,11... | collective-permute-start | bytes 4423688 | tf_op jit(solution)/shard_map/ppermute | solution.py:644
  159.4 14.8 %collective-permute-start.48 = (f32[8,2304]{1,0:T(8,128)S(1)}, f32[8,2304]{1,0:T(8,128)}, u32[]{:S(2)}, u32[]{:S(2)}) collective-permute-start(f32[8,2304]{1,0:T(8,128)S(1)} %add_add_fusion.1), channel_id=1, source_target_pairs={{0,8},{1,9},{2,10},{3,11},{4,12},{5,13},{6,14},{7,15},{8,0},{9,1},... | collective-permute-start | bytes 221192 | tf_op jit(solution)/shard_map/ppermute | solution.py:644
  163.8 11.0 %collective-permute-start.49 = (f32[8,2304]{1,0:T(8,128)S(1)}, f32[8,2304]{1,0:T(8,128)}, u32[]{:S(2)}, u32[]{:S(2)}) collective-permute-start(f32[8,2304]{1,0:T(8,128)S(1)} %add_add_fusion.1), channel_id=1, source_target_pairs={{0,16},{1,17},{2,18},{3,19},{4,20},{5,21},{6,22},{7,23},{8,24},{9,... | collective-permute-start | bytes 221192 | tf_op jit(solution)/shard_map/ppermute | solution.py:644
  163.8 13.3 %collective-permute-start.50 = (f32[8,2304]{1,0:T(8,128)S(1)}, f32[8,2304]{1,0:T(8,128)}, u32[]{:S(2)}, u32[]{:S(2)}) collective-permute-start(f32[8,2304]{1,0:T(8,128)S(1)} %add_add_fusion.1), channel_id=1, source_target_pairs={{0,24},{1,25},{2,26},{3,27},{4,28},{5,29},{6,30},{7,31},{8,16},{9,... | collective-permute-start | bytes 221192 | tf_op jit(solution)/shard_map/ppermute | solution.py:644
  169.8 39.4 %collective-permute-start.31 = (bf16[96,1920]{1,0:T(8,128)(2,1)S(1)}, bf16[96,1920]{1,0:T(8,128)(2,1)S(1)}, u32[]{:S(2)}, u32[]{:S(2)}) collective-permute-start(bf16[96,1920]{1,0:T(8,128)(2,1)S(1)} %get-tuple-element.85), channel_id=1, source_target_pairs={{0,2},{1,3},{2,0},{3,1},{4,6},{5,7},{6,4},{7,5},{8,10},{9,11},{10,... | collective-permute-start | bytes 1105928 | tf_op jit(solution)/shard_map/ppermute | solution.py:644
  173.5 20.4 %collective-permute-start.38 = (bf16[96,3072]{1,0:T(8,128)(2,1)S(1)}, bf16[96,3072]{1,0:T(8,128)(2,1)S(1)}, u32[]{:S(2)}, u32[]{:S(2)}) collective-permute-start(bf16[96,3072]{1,0:T(8,128)(2,1)S(1)} %get-tuple-element.95), channel_id=1, source_target_pairs={{0,2},{1,3},{2,0},{3,1},{4,6},{5,7},{6,4},{7,5},{8,10},{9,11},{10,... | collective-permute-start | bytes 1769480 | tf_op jit(solution)/shard_map/ppermute | solution.py:644
  174.1 21.9 %collective-permute-start.39 = (bf16[96,3072]{1,0:T(8,128)(2,1)S(1)}, bf16[96,3072]{1,0:T(8,128)(2,1)S(1)}, u32[]{:S(2)}, u32[]{:S(2)}) collective-permute-start(bf16[96,3072]{1,0:T(8,128)(2,1)S(1)} %get-tuple-element.96), channel_id=1, source_target_pairs={{0,4},{1,5},{2,6},{3,7},{4,0},{5,1},{6,2},{7,3},{8,12},{9,13},{10,... | collective-permute-start | bytes 1769480 | tf_op jit(solution)/shard_map/ppermute | solution.py:644
  174.8 32.0 %collective-permute-start.40 = (bf16[96,3072]{1,0:T(8,128)(2,1)S(1)}, bf16[96,3072]{1,0:T(8,128)(2,1)S(1)}, u32[]{:S(2)}, u32[]{:S(2)}) collective-permute-start(bf16[96,3072]{1,0:T(8,128)(2,1)S(1)} %get-tuple-element.97), channel_id=1, source_target_pairs={{0,6},{1,7},{2,4},{3,5},{4,2},{5,3},{6,0},{7,1},{8,14},{9,15},{10,... | collective-permute-start | bytes 1769480 | tf_op jit(solution)/shard_map/ppermute | solution.py:644
  178.1 37.2 %collective-permute-start.32 = (bf16[96,1920]{1,0:T(8,128)(2,1)}, bf16[96,1920]{1,0:T(8,128)(2,1)S(1)}, u32[]{:S(2)}, u32[]{:S(2)}) collective-permute-start(bf16[96,1920]{1,0:T(8,128)(2,1)} %get-tuple-element.86), channel_id=1, source_target_pairs={{0,4},{1,5},{2,6},{3,7},{4,0},{5,1},{6,2},{7,3},{8,12},{9,13},{10,... | collective-permute-start | bytes 1105928 | tf_op jit(solution)/shard_map/ppermute | solution.py:644
  193.9 21.4 %collective-permute-start.33 = (bf16[96,1920]{1,0:T(8,128)(2,1)S(1)}, bf16[96,1920]{1,0:T(8,128)(2,1)S(1)}, u32[]{:S(2)}, u32[]{:S(2)}) collective-permute-start(bf16[96,1920]{1,0:T(8,128)(2,1)S(1)} %get-tuple-element.87), channel_id=1, source_target_pairs={{0,6},{1,7},{2,4},{3,5},{4,2},{5,3},{6,0},{7,1},{8,14},{9,15},{10,... | collective-permute-start | bytes 1105928 | tf_op jit(solution)/shard_map/ppermute | solution.py:644
  207.1 10.4 %collective-permute-start.41 = (bf16[24,3072]{1,0:T(8,128)(2,1)S(1)}, bf16[24,3072]{1,0:T(8,128)(2,1)S(1)}, u32[]{:S(2)}, u32[]{:S(2)}) collective-permute-start(bf16[24,3072]{1,0:T(8,128)(2,1)S(1)} %get-tuple-element.99), channel_id=1, source_target_pairs={{0,8},{1,9},{2,10},{3,11},{4,12},{5,13},{6,14},{7,15},{8,0},{9,1},... | collective-permute-start | bytes 442376 | tf_op jit(solution)/shard_map/ppermute | solution.py:644
  208.3 12.3 %collective-permute-start.42 = (bf16[24,3072]{1,0:T(8,128)(2,1)S(1)}, bf16[24,3072]{1,0:T(8,128)(2,1)S(1)}, u32[]{:S(2)}, u32[]{:S(2)}) collective-permute-start(bf16[24,3072]{1,0:T(8,128)(2,1)S(1)} %get-tuple-element.100), channel_id=1, source_target_pairs={{0,16},{1,17},{2,18},{3,19},{4,20},{5,21},{6,22},{7,23},{8,24},{9,... | collective-permute-start | bytes 442376 | tf_op jit(solution)/shard_map/ppermute | solution.py:644
  209.2 11.3 %collective-permute-start.43 = (bf16[24,3072]{1,0:T(8,128)(2,1)S(1)}, bf16[24,3072]{1,0:T(8,128)(2,1)S(1)}, u32[]{:S(2)}, u32[]{:S(2)}) collective-permute-start(bf16[24,3072]{1,0:T(8,128)(2,1)S(1)} %get-tuple-element.101), channel_id=1, source_target_pairs={{0,24},{1,25},{2,26},{3,27},{4,28},{5,29},{6,30},{7,31},{8,16},{9,... | collective-permute-start | bytes 442376 | tf_op jit(solution)/shard_map/ppermute | solution.py:644
  (46 other events, 425.6 us)

commit v3 on v2

--- a/solution.py
+++ b/solution.py
@@ -94,12 +94,6 @@
     for j in range(taps_n):
         taps_ref[j : j + 1, :] = spread(small[j * devices : (j + 1) * devices], 0, channels)
     gains_ref[...] = spread(small[taps_n * devices : (taps_n + 1) * devices], 2, width)
-
-
-def split3(x):
-    hi, rest = split2(x)
-    lo = (x - hi.astype(F32) - rest.astype(F32)).astype(BF16)
-    return hi, rest, lo
 
 
 def head_setup(dt_raw, rows_in, segr, heads_ref, step_ref, cc_ref, wide_ref, cct_ref, segb_ref):
@@ -116,9 +110,9 @@
     for i in range(length // BLK):
         rows = slice(i * BLK, (i + 1) * BLK)
         cc = jnp.dot(lower, rate[rows], precision=HIGH, preferred_element_type=F32)
-        cc_ref[rows, :] = jnp.concatenate(split3(cc), axis=1)
+        cc_ref[rows, :] = cc
         ew = jnp.exp2(jnp.minimum(cc[BLK - 1 : BLK, :] - cc, 0.0))
-        for k, x in enumerate((step[rows], ew * step[rows], jnp.exp2(cc), ew)):
+        for k, x in enumerate((step[rows], ew, jnp.exp2(cc))):
             wide_ref[k, rows, :] = jnp.concatenate(split2(x), axis=1)
         cct_ref[:, rows] = cc.T[: cct_ref.shape[0]]
 
@@ -165,17 +159,15 @@
                 sot_ref[i] = off.T.astype(BF16)
 
 
-def pair_setup(t, heads_ref, wide_ref, cc_ref, cct_ref, count):
+def pair_setup(t, heads_ref, wide_ref, cc_ref, cct_ref):
     head = iota((2 * BLK, BLK), 0) & (BLK - 1)
     pick = (head == 2 * t + jnp.where(iota((2 * BLK, BLK), 1) < BLK // 2, 0, 1)).astype(F32).astype(BF16)
-    spread = [mm(wide_ref[k], pick) for k in range(count)]
-    head = iota((3 * BLK, 2 * BLK), 0) & (BLK - 1)
-    each = (head == 2 * t + jnp.where(iota((3 * BLK, 2 * BLK), 1) < BLK, 0, 1)).astype(F32).astype(BF16)
-    c2 = mm(cc_ref[...], each)
+    st2, ew2, al2 = [mm(wide_ref[k], pick) for k in range(3)]
+    c2 = pltpu.roll(cc_ref[...], lax.rem(BLK - 2 * t, BLK), axis=1)
     r2 = pltpu.roll(cct_ref[...], lax.rem(cct_ref.shape[0] - 2 * t, cct_ref.shape[0]), axis=0)
     h2 = pltpu.roll(heads_ref[...], lax.rem(BLK - 2 * t, BLK), axis=1)
     skip = jnp.where(iota((1, BLK), 1) < BLK // 2, h2[1:2, 0:1], h2[1:2, 1:2])
-    return spread, c2, r2, skip
+    return st2, ew2, ew2 * st2, al2, c2, r2, skip
 
 
 def block_diag(x, low):
@@ -226,7 +218,7 @@
         v_ref[:, lanes] = v
         slope_ref[:, lanes] = slope
         low = iota((1, BLK), 1) < BLK // 2
-        (st2, wq2, al2), c2, r2, skip = pair_setup(t, heads_ref, wide_ref, cc_ref, cct_ref, 3)
+        st2, _, wq2, al2, c2, r2, skip = pair_setup(t, heads_ref, wide_ref, cc_ref, cct_ref)
         vt = (v * st2).astype(BF16)
         vp = (v * wq2).astype(BF16)
         for i in range(length // BLK):
@@ -235,7 +227,7 @@
             ms = []
             for k in range(2):
                 row = r2[k : k + 1, rows]
-                d = jnp.exp2(jnp.minimum(c2[rows, k * BLK : (k + 1) * BLK] - row, 0.0))
+                d = jnp.exp2(jnp.minimum(c2[rows, k : k + 1] - row, 0.0))
                 ms.append((sd_ref[i] * d).astype(BF16))
             yd = mm(jnp.concatenate(ms, axis=1), block_diag(vt[rows], low))
             yd_ref[rows, lanes] = yd
@@ -384,7 +376,7 @@
         x = ci_ref[:, lanes]
         v = v_ref[:, lanes]
         low = iota((1, BLK), 1) < BLK // 2
-        (st2, wq2, al2, ew2), c2, r2, skip = pair_setup(t, heads_ref, wide_ref, cc_ref, cct_ref, 4)
+        st2, ew2, wq2, al2, c2, r2, skip = pair_setup(t, heads_ref, wide_ref, cc_ref, cct_ref)
         vtb = (v * st2).astype(BF16)
         vpb = (v * wq2).astype(BF16)
         g = g_ref[:, lanes]
@@ -405,7 +397,7 @@
             part = jnp.zeros((BLK, BLK), F32)
             for k in range(2):
                 row = r2[k : k + 1, rows]
-                d = jnp.exp2(jnp.minimum(row - c2[rows, k * BLK : (k + 1) * BLK], 0.0))
+                d = jnp.exp2(jnp.minimum(row - c2[rows, k : k + 1], 0.0))
                 ms.append((sdt_ref[i] * d).astype(BF16))
                 part = part + both[:, k * BLK : (k + 1) * BLK] * d
             dsdt_ref[i] += part
@@ -557,8 +549,8 @@
 def scan_scratch(length, inner, taps):
     nheads = -(-2 * inner // (8 * BLK)) * 8
     return [
-        pltpu.VMEM((8, BLK), F32), pltpu.VMEM((length, BLK), F32), pltpu.VMEM((length, 3 * BLK), BF16),
-        pltpu.VMEM((4, length, 2 * BLK), BF16), pltpu.VMEM((nheads, length), F32), pltpu.VMEM((length, BLK), F32),
+        pltpu.VMEM((8, BLK), F32), pltpu.VMEM((length, BLK), F32), pltpu.VMEM((length, BLK), F32),
+        pltpu.VMEM((3, length, 2 * BLK), BF16), pltpu.VMEM((nheads, length), F32), pltpu.VMEM((length, BLK), F32),
         pltpu.VMEM((taps - 1, length, BLK), F32),
     ]
 
@@ -648,19 +640,19 @@
     return [send(part, devices, m) for part, m in zip(parts, stages(devices)[stage])]
 
 
-def stack(pieces):
+def stack(pieces, leave):
     size, rest = pieces[0].shape[0], pieces[0].shape[1:]
     if size % 8 or len(rest) != 1:
         return jnp.concatenate(pieces, axis=0)
-    return call(stack_kernel, held((len(pieces) * size,) + rest, BF16), *pieces)
-
-
-def gather(x, devices):
+    return call(stack_kernel, held((len(pieces) * size,) + rest, BF16), *pieces, leave=leave)
+
+
+def gather(x, devices, leave=()):
     groups = stages(devices)
     core = len(groups) - 1
     pieces = [x]
     for stage in range(core):
-        x = pieces[0] if len(pieces) == 1 else stack(pieces)
+        x = pieces[0] if len(pieces) == 1 else stack(pieces, leave)
         pieces = [x] + send_all([x] * len(groups[stage]), devices, stage)
     return pieces + [send(a, devices, 1) for a in pieces]
 
@@ -733,7 +725,7 @@
         w_gate = w_in[:, :inner]
     cw = gather(w_conv, devices)
     gw = gather(w_gate, devices)
-    ow = gather(w_out, devices)
+    ow = gather(w_out, devices, (w_out,))
     count = len(cw)
 
     heads = [x.reshape(1, nheads) for x in (a_log, d_skip, dt_bias)]

time: 228 us -> 223 us (0.978)
  Pallas kernels: 74.8 us -> 70.8 us
    pallas_call x16, Pallas kernels: 74.8 us -> 70.8 us  [call(): pl.pallas_call(kernel, out_shape=outs, in_specs=specs, out_specs=out_spec...]
    unnamed x54 -> x52, local copies, waits for them, and re-layouts: 14.7 us -> 13.8 us
  transfers between devices with their start and end apart: 51 -> 51, of which waited for: 17 -> 17; matrix products, arithmetic and copies ran while one was open for 2% -> 2% of each run, Pallas kernels for 26% -> 25%
where the time goes in v3:
time: 223 us; the launch traced here: 222 us
  waiting for transfers between devices  73 us (33%)
  Pallas kernels  70.8 us (32%)
  starting transfers between devices  60 us (27%)
  local copies, waits for them, and re-layouts  15.6 us (7%)
    ppermute x51, waiting for transfers between devices, send(): return lax.ppermute(x, 'fsdp', [(i, i ^ mask) for i in range(devices)])  73 us
    pallas_call x16, Pallas kernels, call(): pl.pallas_call(kernel, out_shape=outs, in_specs=specs, out_specs=out_spec...  70.8 us
    ppermute x51, starting transfers between devices, send(): return lax.ppermute(x, 'fsdp', [(i, i ^ mask) for i in range(devices)])  60 us
    unnamed x52, local copies, waits for them, and re-layouts  13.8 us
  transfers between devices with their start and end apart: 51, of which 17 were waited for; matrix products, arithmetic and copies ran while one was open for 2% of the time, Pallas kernels for 25%

profile of v3, /device:TPU:0, one launch (start us, length us, event | category | flops | bytes accessed | tf_op | source)
XLA Modules:
  0.0 221.9 jit_solution(9809735919443105964)
XLA Ops:
  1.8 3.1 %collective-permute-start = (bf16[24,1536]{1,0:T(8,128)(2,1)S(1)}, bf16[24,1536]{1,0:T(8,128)(2,1)S(1)}, u32[]{:S(2)}, u32[]{:S(2)}) collective-permute-start(bf16[24,1536]{1,0:T(8,128)(2,1)S(1)} %get-tuple-element.57.refs_0_), channel_id=1, source_target_pairs={{0,8},{1,9},{2,10},{3,11},{4,12},{5,13},{6,14},{7,15},{8,0},{9,1},... | collective-permute-start | bytes 221192 | tf_op jit(solution)/shard_map/ppermute | solution.py:636
  4.9 2.6 %collective-permute-start.1 = (bf16[24,1536]{1,0:T(8,128)(2,1)S(1)}, bf16[24,1536]{1,0:T(8,128)(2,1)S(1)}, u32[]{:S(2)}, u32[]{:S(2)}) collective-permute-start(bf16[24,1536]{1,0:T(8,128)(2,1)S(1)} %get-tuple-element.57.refs_0_), channel_id=1, source_target_pairs={{0,16},{1,17},{2,18},{3,19},{4,20},{5,21},{6,22},{7,23},{8,24},{9,... | collective-permute-start | bytes 221192 | tf_op jit(solution)/shard_map/ppermute | solution.py:636
  7.5 5.2 %collective-permute-done.1.refs_2_ = bf16[24,1536]{1,0:T(8,128)(2,1)S(1)} collective-permute-done((bf16[24,1536]{1,0:T(8,128)(2,1)S(1)}, bf16[24,1536]{1,0:T(8,128)(2,1)S(1)}, u32[]{:S(2)}, u32[]{:S(2)}) %collective-permute-start.1) | collective-permute-done | bytes 73760 | tf_op jit(solution)/shard_map/ppermute | solution.py:636
  13.8 1.6 collective-permute-start.3
  16.4 1.7 collective-permute-start.11
  20.3 3.6 %collective-permute-start.12 = (bf16[48,768]{1,0:T(8,128)(2,1)}, bf16[48,768]{1,0:T(8,128)(2,1)S(1)}, u32[]{:S(2)}, u32[]{:S(2)}) collective-permute-start(bf16[48,768]{1,0:T(8,128)(2,1)} %refs_0_.3), channel_id=1, source_target_pairs={{0,24},{1,25},{2,26},{3,27},{4,28},{5,29},{6,30},{7,31},{8,16},{9,... | collective-permute-start | bytes 221192 | tf_op jit(solution)/shard_map/ppermute | solution.py:636
  23.9 1.9 collective-permute-done.11.refs_2_
  25.8 4.6 %collective-permute-start.22 = (bf16[24,1920]{1,0:T(8,128)(2,1)S(1)}, bf16[24,1920]{1,0:T(8,128)(2,1)S(1)}, u32[]{:S(2)}, u32[]{:S(2)}) collective-permute-start(bf16[24,1920]{1,0:T(8,128)(2,1)S(1)} %get-tuple-element.58.refs_0_), channel_id=1, source_target_pairs={{0,24},{1,25},{2,26},{3,27},{4,28},{5,29},{6,30},{7,31},{8,16},{9,... | collective-permute-start | bytes 276488 | tf_op jit(solution)/shard_map/ppermute | solution.py:636
  33.4 1.6 collective-permute-start.13
  36.5 3.8 %collective-permute-done.4.refs_2_ = bf16[96,1536]{1,0:T(8,128)(2,1)} collective-permute-done((bf16[96,1536]{1,0:T(8,128)(2,1)S(1)}, bf16[96,1536]{1,0:T(8,128)(2,1)}, u32[]{:S(2)}, u32[]{:S(2)}) %collective-permute-start.4) | collective-permute-done | bytes 294944 | tf_op jit(solution)/shard_map/ppermute | solution.py:636
  41.8 2.2 collective-permute-start.24
  45.2 2.0 collective-permute-done.13.refs_9_
  47.7 20.5 %collective-permute-done.15.refs_11_ = bf16[192,768]{1,0:T(8,128)(2,1)} collective-permute-done((bf16[192,768]{1,0:T(8,128)(2,1)S(1)}, bf16[192,768]{1,0:T(8,128)(2,1)}, u32[]{:S(2)}, u32[]{:S(2)}) %collective-permute-start.15) | collective-permute-done | bytes 294944 | tf_op jit(solution)/shard_map/ppermute | solution.py:636
  81.3 13.8 %shard_map.200 = (bf16[512,768]{1,0:T(8,128)(2,1)S(1)}, f32[8,1792]{1,0:T(8,128)S(1)}, f32[1,2304]{1,0:T(1,128)S(1)}, bf16[768,1920]{1,0:T(8,128)(2,1)S(1)}, f32...) custom-call(bf16[96,1920]{1,0:T(8,128)(2,1)S(1)} %shard_map.199.refs, ...), custom_call_target="tpu_custom_call" | custom-call | tf_op jit(solution)/shard_map/pallas_call | solution.py:613
  96.7 13.2 %shard_map.201 = (bf16[384,3072]{1,0:T(8,128)(2,1)S(1)}, bf16[384,3072]{1,0:T(8,128)(2,1)}, f32[512,1536]{1,0:T(8,128)S(1)}, bf16[512,1536]{1,0:T(8,128)(2,1)S(1...) custom-call(bf16[96,1536]{1,0:T(8,128)(2,1)S(1)} %shard_map.197.refs, ...), custom_call_target="tpu_custom_call" | custom-call | tf_op jit(solution)/shard_map/pallas_call | solution.py:613
  110.0 22.2 %shard_map.203 = (bf16[512,1920]{1,0:T(8,128)(2,1)S(1)}, f32[8,1792]{1,0:T(8,128)S(1)}, f32[1,1536]{1,0:T(1,128)S(1)}, f32[8,128]{1,0:T(8,128)S(1)}) custom-call(f32[512,1536]{1,0:T(8,128)S(1)} %get-tuple-element.69.g_ref, f32[512,1536]{1,0:T(8,128)S(1)} %get-tuple-element.70.yd_ref, f32[512,1536]{1,0:T(8,128)S(1)} %get-tuple-element.71.v_ref, ...), custom_call_target="tpu_custom_call" | custom-call | tf_op jit(solution)/shard_map/pallas_call | solution.py:613
  132.3 3.0 %shard_map.205 = (bf16[384,1920]{1,0:T(8,128)(2,1)S(1)}, bf16[384,1920]{1,0:T(8,128)(2,1)}) custom-call(bf16[512,768]{1,0:T(8,128)(2,1)S(1)} %get-tuple-element.59.refs_17_.xn_ref, bf16[512,1920]{1,0:T(8,128)(2,1)S(1)} %get-tuple-element.76.dp_ref), custom_call_target="tpu_custom_call" | custom-call | tf_op jit(solution)/shard_map/pallas_call | solution.py:613
  135.6 2.7 %shard_map.202 = (bf16[512,768]{1,0:T(8,128)(2,1)}, f32[512,768]{1,0:T(8,128)S(1)}) custom-call(bf16[512,1536]{1,0:T(8,128)(2,1)S(1)} %get-tuple-element.62.mixed_ref, bf16[1536,768]{1,0:T(8,128)(2,1)S(1)} %get-tuple-element.63.wo_ref, bf16[512,768]{1,0:T(8,128)(2,1)S(1)} %copy-done, bf16[512,1536]{1,0:T(8,128)(2,1)S(1)} %get-tuple-element.64.dgate_ref, ...), custom_call_target="tpu_custom_call" | custom-call | tf_op jit(solution)/shard_map/pallas_call | solution.py:613
  138.3 7.5 %shard_map.204 = (f32[512,768]{1,0:T(8,128)}, f32[8,2304]{1,0:T(8,128)S(1)}) custom-call(bf16[768,1920]{1,0:T(8,128)(2,1)S(1)} %copy-done.3, f32[512,768]{1,0:T(8,128)S(1)} %get-tuple-element.68.dng_ref, bf16[512,1920]{1,0:T(8,128)(2,1)S(1)} %get-tuple-element.76.dp_ref, s32[1]{0:T(128)} %bitcast.1.refs_8_.refs_16_.me_ref, ...), custom_call_target="tpu_custom_call" | custom-call | tf_op jit(solution)/shard_map/pallas_call | solution.py:613
  152.0 2.4 %collective-permute-done.47 = f32[8,2304]{1,0:T(8,128)S(1)} collective-permute-done((f32[8,2304]{1,0:T(8,128)S(1)}, f32[8,2304]{1,0:T(8,128)S(1)}, u32[]{:S(2)}, u32[]{:S(2)}) %collective-permute-start.47) | collective-permute-done | bytes 73760 | tf_op jit(solution)/shard_map/ppermute | solution.py:636
  154.4 4.5 %collective-permute-start.48 = (f32[8,2304]{1,0:T(8,128)S(1)}, f32[8,2304]{1,0:T(8,128)}, u32[]{:S(2)}, u32[]{:S(2)}) collective-permute-start(f32[8,2304]{1,0:T(8,128)S(1)} %add_add_fusion.1), channel_id=1, source_target_pairs={{0,8},{1,9},{2,10},{3,11},{4,12},{5,13},{6,14},{7,15},{8,0},{9,1},... | collective-permute-start | bytes 221192 | tf_op jit(solution)/shard_map/ppermute | solution.py:636
  158.9 2.4 %collective-permute-start.50 = (f32[8,2304]{1,0:T(8,128)S(1)}, f32[8,2304]{1,0:T(8,128)}, u32[]{:S(2)}, u32[]{:S(2)}) collective-permute-start(f32[8,2304]{1,0:T(8,128)S(1)} %add_add_fusion.1), channel_id=1, source_target_pairs={{0,24},{1,25},{2,26},{3,27},{4,28},{5,29},{6,30},{7,31},{8,16},{9,... | collective-permute-start | bytes 221192 | tf_op jit(solution)/shard_map/ppermute | solution.py:636
  162.7 2.2 shard_map.206
  166.4 2.2 shard_map.208
  169.9 2.3 %collective-permute-start.40 = (bf16[96,3072]{1,0:T(8,128)(2,1)S(1)}, bf16[96,3072]{1,0:T(8,128)(2,1)S(1)}, u32[]{:S(2)}, u32[]{:S(2)}) collective-permute-start(bf16[96,3072]{1,0:T(8,128)(2,1)S(1)} %get-tuple-element.97), channel_id=1, source_target_pairs={{0,6},{1,7},{2,4},{3,5},{4,2},{5,3},{6,0},{7,1},{8,14},{9,15},{10,... | collective-permute-start | bytes 1769480 | tf_op jit(solution)/shard_map/ppermute | solution.py:636
  173.9 15.1 %collective-permute-done.38.refs_1_ = bf16[96,3072]{1,0:T(8,128)(2,1)S(1)} collective-permute-done((bf16[96,3072]{1,0:T(8,128)(2,1)S(1)}, bf16[96,3072]{1,0:T(8,128)(2,1)S(1)}, u32[]{:S(2)}, u32[]{:S(2)}) %collective-permute-start.38) | collective-permute-done | bytes 589856 | tf_op jit(solution)/shard_map/ppermute | solution.py:636
  189.0 1.6 collective-permute-start.33
  191.2 10.7 %collective-permute-done.40.refs_3_ = bf16[96,3072]{1,0:T(8,128)(2,1)S(1)} collective-permute-done((bf16[96,3072]{1,0:T(8,128)(2,1)S(1)}, bf16[96,3072]{1,0:T(8,128)(2,1)S(1)}, u32[]{:S(2)}, u32[]{:S(2)}) %collective-permute-start.40) | collective-permute-done | bytes 589856 | tf_op jit(solution)/shard_map/ppermute | solution.py:636
  204.3 2.4 %collective-permute-start.43 = (bf16[24,3072]{1,0:T(8,128)(2,1)S(1)}, bf16[24,3072]{1,0:T(8,128)(2,1)S(1)}, u32[]{:S(2)}, u32[]{:S(2)}) collective-permute-start(bf16[24,3072]{1,0:T(8,128)(2,1)S(1)} %get-tuple-element.101), channel_id=1, source_target_pairs={{0,24},{1,25},{2,26},{3,27},{4,28},{5,29},{6,30},{7,31},{8,16},{9,... | collective-permute-start | bytes 442376 | tf_op jit(solution)/shard_map/ppermute | solution.py:636
  208.1 2.3 %collective-permute-done.32.refs_2_ = bf16[96,1920]{1,0:T(8,128)(2,1)S(1)} collective-permute-done((bf16[96,1920]{1,0:T(8,128)(2,1)}, bf16[96,1920]{1,0:T(8,128)(2,1)S(1)}, u32[]{:S(2)}, u32[]{:S(2)}) %collective-permute-start.32) | collective-permute-done | bytes 368672 | tf_op jit(solution)/shard_map/ppermute | solution.py:636
  212.6 2.4 %collective-permute-start.36 = (bf16[24,1920]{1,0:T(8,128)(2,1)S(1)}, bf16[24,1920]{1,0:T(8,128)(2,1)S(1)}, u32[]{:S(2)}, u32[]{:S(2)}) collective-permute-start(bf16[24,1920]{1,0:T(8,128)(2,1)S(1)} %get-tuple-element.91), channel_id=1, source_target_pairs={{0,24},{1,25},{2,26},{3,27},{4,28},{5,29},{6,30},{7,31},{8,16},{9,... | collective-permute-start | bytes 276488 | tf_op jit(solution)/shard_map/ppermute | solution.py:636
  216.6 4.5 %collective-permute-done.35.c_ref = bf16[24,1920]{1,0:T(8,128)(2,1)S(1)} collective-permute-done((bf16[24,1920]{1,0:T(8,128)(2,1)S(1)}, bf16[24,1920]{1,0:T(8,128)(2,1)S(1)}, u32[]{:S(2)}, u32[]{:S(2)}) %collective-permute-start.35) | collective-permute-done | bytes 92192 | tf_op jit(solution)/shard_map/ppermute | solution.py:636
  (149 shorter events, 49.4 us)
Async XLA Ops:
  13.8 21.1 %collective-permute-start.3 = (bf16[96,1536]{1,0:T(8,128)(2,1)S(1)}, bf16[96,1536]{1,0:T(8,128)(2,1)S(1)}, u32[]{:S(2)}, u32[]{:S(2)}) collective-permute-start(bf16[96,1536]{1,0:T(8,128)(2,1)S(1)} %shard_map.197.refs_0_), channel_id=1, source_target_pairs={{0,2},{1,3},{2,0},{3,1},{4,6},{5,7},{6,4},{7,5},{8,10},{9,11},{10,... | collective-permute-start | bytes 884744 | tf_op jit(solution)/shard_map/ppermute | solution.py:636
  18.1 13.8 %collective-permute-start.20 = (bf16[24,1920]{1,0:T(8,128)(2,1)S(1)}, bf16[24,1920]{1,0:T(8,128)(2,1)S(1)}, u32[]{:S(2)}, u32[]{:S(2)}) collective-permute-start(bf16[24,1920]{1,0:T(8,128)(2,1)S(1)} %get-tuple-element.58.refs_0_), channel_id=1, source_target_pairs={{0,8},{1,9},{2,10},{3,11},{4,12},{5,13},{6,14},{7,15},{8,0},{9,1},... | collective-permute-start | bytes 276488 | tf_op jit(solution)/shard_map/ppermute | solution.py:636
  19.5 12.9 %collective-permute-start.21 = (bf16[24,1920]{1,0:T(8,128)(2,1)S(1)}, bf16[24,1920]{1,0:T(8,128)(2,1)S(1)}, u32[]{:S(2)}, u32[]{:S(2)}) collective-permute-start(bf16[24,1920]{1,0:T(8,128)(2,1)S(1)} %get-tuple-element.58.refs_0_), channel_id=1, source_target_pairs={{0,16},{1,17},{2,18},{3,19},{4,20},{5,21},{6,22},{7,23},{8,24},{9,... | collective-permute-start | bytes 276488 | tf_op jit(solution)/shard_map/ppermute | solution.py:636
  20.3 10.1 %collective-permute-start.12 = (bf16[48,768]{1,0:T(8,128)(2,1)}, bf16[48,768]{1,0:T(8,128)(2,1)S(1)}, u32[]{:S(2)}, u32[]{:S(2)}) collective-permute-start(bf16[48,768]{1,0:T(8,128)(2,1)} %refs_0_.3), channel_id=1, source_target_pairs={{0,24},{1,25},{2,26},{3,27},{4,28},{5,29},{6,30},{7,31},{8,16},{9,... | collective-permute-start | bytes 221192 | tf_op jit(solution)/shard_map/ppermute | solution.py:636
  31.9 9.9 %collective-permute-start.5 = (bf16[96,1536]{1,0:T(8,128)(2,1)S(1)}, bf16[96,1536]{1,0:T(8,128)(2,1)}, u32[]{:S(2)}, u32[]{:S(2)}) collective-permute-start(bf16[96,1536]{1,0:T(8,128)(2,1)S(1)} %shard_map.197.refs_0_), channel_id=1, source_target_pairs={{0,6},{1,7},{2,4},{3,5},{4,2},{5,3},{6,0},{7,1},{8,14},{9,15},{10,... | collective-permute-start | bytes 884744 | tf_op jit(solution)/shard_map/ppermute | solution.py:636
  32.4 11.6 %collective-permute-start.6 = (bf16[96,1536]{1,0:T(8,128)(2,1)S(1)}, bf16[96,1536]{1,0:T(8,128)(2,1)S(1)}, u32[]{:S(2)}, u32[]{:S(2)}) collective-permute-start(bf16[96,1536]{1,0:T(8,128)(2,1)S(1)} %shard_map.197.refs_0_), channel_id=1, source_target_pairs={{0,1},{1,0},{2,3},{3,2},{4,5},{5,4},{6,7},{7,6},{8,9},{9,8},{10,11... | collective-permute-start | bytes 884744 | tf_op jit(solution)/shard_map/ppermute | solution.py:636
  33.4 13.8 %collective-permute-start.13 = (bf16[192,768]{1,0:T(8,128)(2,1)S(1)}, bf16[192,768]{1,0:T(8,128)(2,1)}, u32[]{:S(2)}, u32[]{:S(2)}) collective-permute-start(bf16[192,768]{1,0:T(8,128)(2,1)S(1)} %shard_map.198.refs_8_), channel_id=1, source_target_pairs={{0,2},{1,3},{2,0},{3,1},{4,6},{5,7},{6,4},{7,5},{8,10},{9,11},{10,... | collective-permute-start | bytes 884744 | tf_op jit(solution)/shard_map/ppermute | solution.py:636
  34.9 12.8 %collective-permute-start.14 = (bf16[192,768]{1,0:T(8,128)(2,1)S(1)}, bf16[192,768]{1,0:T(8,128)(2,1)}, u32[]{:S(2)}, u32[]{:S(2)}) collective-permute-start(bf16[192,768]{1,0:T(8,128)(2,1)S(1)} %shard_map.198.refs_8_), channel_id=1, source_target_pairs={{0,4},{1,5},{2,6},{3,7},{4,0},{5,1},{6,2},{7,3},{8,12},{9,13},{10,... | collective-permute-start | bytes 884744 | tf_op jit(solution)/shard_map/ppermute | solution.py:636
  40.3 28.0 %collective-permute-start.23 = (bf16[96,1920]{1,0:T(8,128)(2,1)S(1)}, bf16[96,1920]{1,0:T(8,128)(2,1)S(1)}, u32[]{:S(2)}, u32[]{:S(2)}) collective-permute-start(bf16[96,1920]{1,0:T(8,128)(2,1)S(1)} %shard_map.199.refs_0_), channel_id=1, source_target_pairs={{0,2},{1,3},{2,0},{3,1},{4,6},{5,7},{6,4},{7,5},{8,10},{9,11},{10,... | collective-permute-start | bytes 1105928 | tf_op jit(solution)/shard_map/ppermute | solution.py:636
  41.8 26.9 %collective-permute-start.24 = (bf16[96,1920]{1,0:T(8,128)(2,1)S(1)}, bf16[96,1920]{1,0:T(8,128)(2,1)S(1)}, u32[]{:S(2)}, u32[]{:S(2)}) collective-permute-start(bf16[96,1920]{1,0:T(8,128)(2,1)S(1)} %shard_map.199.refs_0_), channel_id=1, source_target_pairs={{0,4},{1,5},{2,6},{3,7},{4,0},{5,1},{6,2},{7,3},{8,12},{9,13},{10,... | collective-permute-start | bytes 1105928 | tf_op jit(solution)/shard_map/ppermute | solution.py:636
  44.7 24.1 %collective-permute-start.25 = (bf16[96,1920]{1,0:T(8,128)(2,1)S(1)}, bf16[96,1920]{1,0:T(8,128)(2,1)S(1)}, u32[]{:S(2)}, u32[]{:S(2)}) collective-permute-start(bf16[96,1920]{1,0:T(8,128)(2,1)S(1)} %shard_map.199.refs_0_), channel_id=1, source_target_pairs={{0,6},{1,7},{2,4},{3,5},{4,2},{5,3},{6,0},{7,1},{8,14},{9,15},{10,... | collective-permute-start | bytes 1105928 | tf_op jit(solution)/shard_map/ppermute | solution.py:636
  47.2 21.0 %collective-permute-start.15 = (bf16[192,768]{1,0:T(8,128)(2,1)S(1)}, bf16[192,768]{1,0:T(8,128)(2,1)}, u32[]{:S(2)}, u32[]{:S(2)}) collective-permute-start(bf16[192,768]{1,0:T(8,128)(2,1)S(1)} %shard_map.198.refs_8_), channel_id=1, source_target_pairs={{0,6},{1,7},{2,4},{3,5},{4,2},{5,3},{6,0},{7,1},{8,14},{9,15},{10,... | collective-permute-start | bytes 884744 | tf_op jit(solution)/shard_map/ppermute | solution.py:636
  47.7 22.3 %collective-permute-start.16 = (bf16[192,768]{1,0:T(8,128)(2,1)S(1)}, bf16[192,768]{1,0:T(8,128)(2,1)S(1)}, u32[]{:S(2)}, u32[]{:S(2)}) collective-permute-start(bf16[192,768]{1,0:T(8,128)(2,1)S(1)} %shard_map.198.refs_8_), channel_id=1, source_target_pairs={{0,1},{1,0},{2,3},{3,2},{4,5},{5,4},{6,7},{7,6},{8,9},{9,8},{10,11... | collective-permute-start | bytes 884744 | tf_op jit(solution)/shard_map/ppermute | solution.py:636
  71.6 25.1 %collective-permute-start.8 = (bf16[96,1536]{1,0:T(8,128)(2,1)}, bf16[96,1536]{1,0:T(8,128)(2,1)}, u32[]{:S(2)}, u32[]{:S(2)}) collective-permute-start(bf16[96,1536]{1,0:T(8,128)(2,1)} %collective-permute-done.4.refs_2_), channel_id=1, source_target_pairs={{0,1},{1,0},{2,3},{3,2},{4,5},{5,4},{6,7},{7,6},{8,9},{9,8},{10,11... | collective-permute-start | bytes 884744 | tf_op jit(solution)/shard_map/ppermute | solution.py:636
  73.1 23.6 %collective-permute-start.9 = (bf16[96,1536]{1,0:T(8,128)(2,1)}, bf16[96,1536]{1,0:T(8,128)(2,1)}, u32[]{:S(2)}, u32[]{:S(2)}) collective-permute-start(bf16[96,1536]{1,0:T(8,128)(2,1)} %collective-permute-done.5.refs_3_), channel_id=1, source_target_pairs={{0,1},{1,0},{2,3},{3,2},{4,5},{5,4},{6,7},{7,6},{8,9},{9,8},{10,11... | collective-permute-start | bytes 884744 | tf_op jit(solution)/shard_map/ppermute | solution.py:636
  74.0 22.7 %collective-permute-start.17 = (bf16[192,768]{1,0:T(8,128)(2,1)}, bf16[192,768]{1,0:T(8,128)(2,1)}, u32[]{:S(2)}, u32[]{:S(2)}) collective-permute-start(bf16[192,768]{1,0:T(8,128)(2,1)} %collective-permute-done.13.refs_9_), channel_id=1, source_target_pairs={{0,1},{1,0},{2,3},{3,2},{4,5},{5,4},{6,7},{7,6},{8,9},{9,8},{10,11... | collective-permute-start | bytes 884744 | tf_op jit(solution)/shard_map/ppermute | solution.py:636
  75.1 21.6 %collective-permute-start.18 = (bf16[192,768]{1,0:T(8,128)(2,1)}, bf16[192,768]{1,0:T(8,128)(2,1)}, u32[]{:S(2)}, u32[]{:S(2)}) collective-permute-start(bf16[192,768]{1,0:T(8,128)(2,1)} %collective-permute-done.14.refs_10_), channel_id=1, source_target_pairs={{0,1},{1,0},{2,3},{3,2},{4,5},{5,4},{6,7},{7,6},{8,9},{9,8},{10,11... | collective-permute-start | bytes 884744 | tf_op jit(solution)/shard_map/ppermute | solution.py:636
  76.0 20.7 %collective-permute-start.19 = (bf16[192,768]{1,0:T(8,128)(2,1)}, bf16[192,768]{1,0:T(8,128)(2,1)}, u32[]{:S(2)}, u32[]{:S(2)}) collective-permute-start(bf16[192,768]{1,0:T(8,128)(2,1)} %collective-permute-done.15.refs_11_), channel_id=1, source_target_pairs={{0,1},{1,0},{2,3},{3,2},{4,5},{5,4},{6,7},{7,6},{8,9},{9,8},{10,11... | collective-permute-start | bytes 884744 | tf_op jit(solution)/shard_map/ppermute | solution.py:636
  109.9 56.6 %collective-permute-start.37 = (bf16[384,3072]{1,0:T(8,128)(2,1)}, bf16[384,3072]{1,0:T(8,128)(2,1)}, u32[]{:S(2)}, u32[]{:S(2)}) collective-permute-start(bf16[384,3072]{1,0:T(8,128)(2,1)} %get-tuple-element.93), channel_id=1, source_target_pairs={{0,1},{1,0},{2,3},{3,2},{4,5},{5,4},{6,7},{7,6},{8,9},{9,8},{10,11... | collective-permute-start | bytes 7077896 | tf_op jit(solution)/shard_map/ppermute | solution.py:636
  135.3 26.1 %collective-permute-start.30 = (bf16[384,1920]{1,0:T(8,128)(2,1)}, bf16[384,1920]{1,0:T(8,128)(2,1)}, u32[]{:S(2)}, u32[]{:S(2)}) collective-permute-start(bf16[384,1920]{1,0:T(8,128)(2,1)} %get-tuple-element.83), channel_id=1, source_target_pairs={{0,1},{1,0},{2,3},{3,2},{4,5},{5,4},{6,7},{7,6},{8,9},{9,8},{10,11... | collective-permute-start | bytes 4423688 | tf_op jit(solution)/shard_map/ppermute | solution.py:636
  154.4 14.8 %collective-permute-start.48 = (f32[8,2304]{1,0:T(8,128)S(1)}, f32[8,2304]{1,0:T(8,128)}, u32[]{:S(2)}, u32[]{:S(2)}) collective-permute-start(f32[8,2304]{1,0:T(8,128)S(1)} %add_add_fusion.1), channel_id=1, source_target_pairs={{0,8},{1,9},{2,10},{3,11},{4,12},{5,13},{6,14},{7,15},{8,0},{9,1},... | collective-permute-start | bytes 221192 | tf_op jit(solution)/shard_map/ppermute | solution.py:636
  158.9 11.0 %collective-permute-start.49 = (f32[8,2304]{1,0:T(8,128)S(1)}, f32[8,2304]{1,0:T(8,128)}, u32[]{:S(2)}, u32[]{:S(2)}) collective-permute-start(f32[8,2304]{1,0:T(8,128)S(1)} %add_add_fusion.1), channel_id=1, source_target_pairs={{0,16},{1,17},{2,18},{3,19},{4,20},{5,21},{6,22},{7,23},{8,24},{9,... | collective-permute-start | bytes 221192 | tf_op jit(solution)/shard_map/ppermute | solution.py:636
  158.9 13.3 %collective-permute-start.50 = (f32[8,2304]{1,0:T(8,128)S(1)}, f32[8,2304]{1,0:T(8,128)}, u32[]{:S(2)}, u32[]{:S(2)}) collective-permute-start(f32[8,2304]{1,0:T(8,128)S(1)} %add_add_fusion.1), channel_id=1, source_target_pairs={{0,24},{1,25},{2,26},{3,27},{4,28},{5,29},{6,30},{7,31},{8,16},{9,... | collective-permute-start | bytes 221192 | tf_op jit(solution)/shard_map/ppermute | solution.py:636
  164.9 39.4 %collective-permute-start.31 = (bf16[96,1920]{1,0:T(8,128)(2,1)S(1)}, bf16[96,1920]{1,0:T(8,128)(2,1)S(1)}, u32[]{:S(2)}, u32[]{:S(2)}) collective-permute-start(bf16[96,1920]{1,0:T(8,128)(2,1)S(1)} %get-tuple-element.85), channel_id=1, source_target_pairs={{0,2},{1,3},{2,0},{3,1},{4,6},{5,7},{6,4},{7,5},{8,10},{9,11},{10,... | collective-permute-start | bytes 1105928 | tf_op jit(solution)/shard_map/ppermute | solution.py:636
  168.6 20.4 %collective-permute-start.38 = (bf16[96,3072]{1,0:T(8,128)(2,1)S(1)}, bf16[96,3072]{1,0:T(8,128)(2,1)S(1)}, u32[]{:S(2)}, u32[]{:S(2)}) collective-permute-start(bf16[96,3072]{1,0:T(8,128)(2,1)S(1)} %get-tuple-element.95), channel_id=1, source_target_pairs={{0,2},{1,3},{2,0},{3,1},{4,6},{5,7},{6,4},{7,5},{8,10},{9,11},{10,... | collective-permute-start | bytes 1769480 | tf_op jit(solution)/shard_map/ppermute | solution.py:636
  169.2 21.9 %collective-permute-start.39 = (bf16[96,3072]{1,0:T(8,128)(2,1)S(1)}, bf16[96,3072]{1,0:T(8,128)(2,1)S(1)}, u32[]{:S(2)}, u32[]{:S(2)}) collective-permute-start(bf16[96,3072]{1,0:T(8,128)(2,1)S(1)} %get-tuple-element.96), channel_id=1, source_target_pairs={{0,4},{1,5},{2,6},{3,7},{4,0},{5,1},{6,2},{7,3},{8,12},{9,13},{10,... | collective-permute-start | bytes 1769480 | tf_op jit(solution)/shard_map/ppermute | solution.py:636
  169.9 32.0 %collective-permute-start.40 = (bf16[96,3072]{1,0:T(8,128)(2,1)S(1)}, bf16[96,3072]{1,0:T(8,128)(2,1)S(1)}, u32[]{:S(2)}, u32[]{:S(2)}) collective-permute-start(bf16[96,3072]{1,0:T(8,128)(2,1)S(1)} %get-tuple-element.97), channel_id=1, source_target_pairs={{0,6},{1,7},{2,4},{3,5},{4,2},{5,3},{6,0},{7,1},{8,14},{9,15},{10,... | collective-permute-start | bytes 1769480 | tf_op jit(solution)/shard_map/ppermute | solution.py:636
  173.2 37.2 %collective-permute-start.32 = (bf16[96,1920]{1,0:T(8,128)(2,1)}, bf16[96,1920]{1,0:T(8,128)(2,1)S(1)}, u32[]{:S(2)}, u32[]{:S(2)}) collective-permute-start(bf16[96,1920]{1,0:T(8,128)(2,1)} %get-tuple-element.86), channel_id=1, source_target_pairs={{0,4},{1,5},{2,6},{3,7},{4,0},{5,1},{6,2},{7,3},{8,12},{9,13},{10,... | collective-permute-start | bytes 1105928 | tf_op jit(solution)/shard_map/ppermute | solution.py:636
  189.0 21.4 %collective-permute-start.33 = (bf16[96,1920]{1,0:T(8,128)(2,1)S(1)}, bf16[96,1920]{1,0:T(8,128)(2,1)S(1)}, u32[]{:S(2)}, u32[]{:S(2)}) collective-permute-start(bf16[96,1920]{1,0:T(8,128)(2,1)S(1)} %get-tuple-element.87), channel_id=1, source_target_pairs={{0,6},{1,7},{2,4},{3,5},{4,2},{5,3},{6,0},{7,1},{8,14},{9,15},{10,... | collective-permute-start | bytes 1105928 | tf_op jit(solution)/shard_map/ppermute | solution.py:636
  202.2 10.4 %collective-permute-start.41 = (bf16[24,3072]{1,0:T(8,128)(2,1)S(1)}, bf16[24,3072]{1,0:T(8,128)(2,1)S(1)}, u32[]{:S(2)}, u32[]{:S(2)}) collective-permute-start(bf16[24,3072]{1,0:T(8,128)(2,1)S(1)} %get-tuple-element.99), channel_id=1, source_target_pairs={{0,8},{1,9},{2,10},{3,11},{4,12},{5,13},{6,14},{7,15},{8,0},{9,1},... | collective-permute-start | bytes 442376 | tf_op jit(solution)/shard_map/ppermute | solution.py:636
  203.3 12.3 %collective-permute-start.42 = (bf16[24,3072]{1,0:T(8,128)(2,1)S(1)}, bf16[24,3072]{1,0:T(8,128)(2,1)S(1)}, u32[]{:S(2)}, u32[]{:S(2)}) collective-permute-start(bf16[24,3072]{1,0:T(8,128)(2,1)S(1)} %get-tuple-element.100), channel_id=1, source_target_pairs={{0,16},{1,17},{2,18},{3,19},{4,20},{5,21},{6,22},{7,23},{8,24},{9,... | collective-permute-start | bytes 442376 | tf_op jit(solution)/shard_map/ppermute | solution.py:636
  204.3 11.3 %collective-permute-start.43 = (bf16[24,3072]{1,0:T(8,128)(2,1)S(1)}, bf16[24,3072]{1,0:T(8,128)(2,1)S(1)}, u32[]{:S(2)}, u32[]{:S(2)}) collective-permute-start(bf16[24,3072]{1,0:T(8,128)(2,1)S(1)} %get-tuple-element.101), channel_id=1, source_target_pairs={{0,24},{1,25},{2,26},{3,27},{4,28},{5,29},{6,30},{7,31},{8,16},{9,... | collective-permute-start | bytes 442376 | tf_op jit(solution)/shard_map/ppermute | solution.py:636
  (45 other events, 415.8 us)

commit v4 on v3

--- a/solution.py
+++ b/solution.py
@@ -500,7 +500,11 @@
     sums_ref[0:5, : dtaps_ref.shape[1]] = dtaps_ref[0:5, :]
     sums_ref[5:6, :width] = jnp.sum(dn * unit, axis=0, keepdims=True)
     sums_ref[5:6, width:] = jnp.sum(ginner_ref[...], axis=0, keepdims=True)
-    sums_ref[6:7, : dskip_ref.shape[1]] = dskip_ref[...]
+    inner_n = dskip_ref.shape[1]
+    lane = iota((inner_n, BLK), 1) * (BLK // 2)
+    channel = iota((inner_n, BLK), 0)
+    group = ((channel >= lane) & (channel < lane + BLK // 2)).astype(F32)
+    sums_ref[6:7, :BLK] = jnp.dot(dskip_ref[...], group, precision=HIGH, preferred_element_type=F32)
     sums_ref[7:8, :BLK] = dheads_ref[0:1, :]
     sums_ref[7:8, BLK : 2 * BLK] = dheads_ref[1:2, :]
     dunit = dn * gains_ref[:, :width]
@@ -536,6 +540,22 @@
     inner = gate_ref.shape[1]
     in_ref[:, :inner] = gate_ref[...]
     in_ref[:, inner:] = total[:, : in_ref.shape[1] - inner]
+
+
+def ends_kernel(me_ref, *refs):
+    taps_ref, gains_ref, alog_ref, skip_ref, bias_ref = refs[-5:]
+    parts = [ref[...] for ref in refs[:-5]]
+    sums = parts[0] + parts[1]
+    if len(parts) == 4:
+        sums = sums + (parts[2] + parts[3])
+    me, width = me_ref[0], sums.shape[1]
+    taps_n, tap_share = taps_ref.shape
+    gain_share, nheads = gains_ref.shape[1], alog_ref.shape[1]
+    taps_ref[...] = pltpu.roll(sums, lax.rem(width - me * tap_share, width), axis=1)[:taps_n, :tap_share]
+    gains_ref[...] = pltpu.roll(sums, lax.rem(width - me * gain_share, width), axis=1)[taps_n : taps_n + 1, :gain_share]
+    skip_ref[...] = sums[6:7, :nheads]
+    alog_ref[...] = sums[7:8, :nheads]
+    bias_ref[...] = sums[7:8, BLK : BLK + nheads]
 
 
 def sds(shape, dtype):
@@ -681,8 +701,9 @@
     for stage in reversed(range(len(stages(devices)))):
         group = stages(devices)[stage]
         got = send_all([x] * len(group), devices, stage)
+        if stage == 0:
+            return [x] + got
         x = x + got[0] if len(got) == 1 else (x + got[0]) + (got[1] + got[2])
-    return x
 
 
 def layer(
@@ -797,11 +818,14 @@
         in_share = jnp.concatenate([total[:, :inner], conv_total], axis=1)[:, :proj]
 
     sums = total_of(sums, devices)
-    taps_share = lax.dynamic_slice_in_dim(sums[:taps_n, :channels], me * tap_share, tap_share, axis=1)
-    gains_share = lax.dynamic_slice_in_dim(sums[5], me * gain_share, gain_share)
+    one = sds((1, nheads), F32)
+    taps_share, gains_share, d_alog, d_dskip, d_bias = call(
+        ends_kernel, (sds((taps_n, tap_share), F32), sds((1, gain_share), F32), one, one, one),
+        mine, *sums, scalar=0,
+    )
     return (
-        output, input_grad, in_share, out_share, taps_share, gains_share,
-        sums[7, :nheads], sums[6, :inner].reshape(nheads, -1).sum(axis=1), sums[7, BLK : BLK + nheads],
+        output, input_grad, in_share, out_share, taps_share, gains_share.reshape(gain_share),
+        d_alog.reshape(nheads), d_dskip.reshape(nheads), d_bias.reshape(nheads),
     )
 
 

time: 223 us -> 233 us (1.045)
  waiting for transfers between devices: 73 us -> 91.2 us
  Pallas kernels: 70.8 us -> 66.2 us
    ppermute x51, waiting for transfers between devices: 73 us -> 91.2 us  [send(): return lax.ppermute(x, 'fsdp', [(i, i ^ mask) for i in range(devices)])]
    pallas_call x16 -> x17, Pallas kernels: 70.8 us -> 66.2 us  [call(): pl.pallas_call(kernel, out_shape=outs, in_specs=specs, out_specs=out_spec...]
    unnamed x52 -> x48, local copies, waits for them, and re-layouts: 13.8 us -> 14.1 us
  transfers between devices with their start and end apart: 51 -> 51, of which waited for: 17 -> 14; matrix products, arithmetic and copies ran while one was open for 2% -> 0% of each run, Pallas kernels for 25% -> 22%
where the time goes in v4:
time: 233 us
  waiting for transfers between devices  91.2 us (39%)
  Pallas kernels  66.2 us (28%)
  starting transfers between devices  60.4 us (26%)
  local copies, waits for them, and re-layouts  14.1 us (6%)
    ppermute x51, waiting for transfers between devices, send(): return lax.ppermute(x, 'fsdp', [(i, i ^ mask) for i in range(devices)])  91.2 us
    pallas_call x17, Pallas kernels, call(): pl.pallas_call(kernel, out_shape=outs, in_specs=specs, out_specs=out_spec...  66.2 us
    ppermute x51, starting transfers between devices, send(): return lax.ppermute(x, 'fsdp', [(i, i ^ mask) for i in range(devices)])  60.4 us
    unnamed x48, local copies, waits for them, and re-layouts  14.1 us
  transfers between devices with their start and end apart: 51, of which 14 were waited for; matrix products, arithmetic and copies ran while one was open for 0% of the time, Pallas kernels for 22%

profile of v4, /device:TPU:0, one launch (start us, length us, event | category | flops | bytes accessed | tf_op | source)
XLA Modules:
  0.0 232.7 jit_solution(15045586181134197669)
XLA Ops:
  1.8 5.1 %collective-permute-start.2 = (bf16[24,1536]{1,0:T(8,128)(2,1)S(1)}, bf16[24,1536]{1,0:T(8,128)(2,1)S(1)}, u32[]{:S(2)}, u32[]{:S(2)}) collective-permute-start(bf16[24,1536]{1,0:T(8,128)(2,1)S(1)} %get-tuple-element.62.refs_0_), channel_id=1, source_target_pairs={{0,24},{1,25},{2,26},{3,27},{4,28},{5,29},{6,30},{7,31},{8,16},{9,... | collective-permute-start | bytes 221192 | tf_op jit(solution)/shard_map/ppermute | solution.py:656
  7.6 2.0 collective-permute-done.2.refs_3_
  9.6 3.5 %collective-permute-done.1.refs_2_ = bf16[24,1536]{1,0:T(8,128)(2,1)S(1)} collective-permute-done((bf16[24,1536]{1,0:T(8,128)(2,1)S(1)}, bf16[24,1536]{1,0:T(8,128)(2,1)S(1)}, u32[]{:S(2)}, u32[]{:S(2)}) %collective-permute-start.1) | collective-permute-done | bytes 73760 | tf_op jit(solution)/shard_map/ppermute | solution.py:656
  14.4 2.2 collective-permute-start.10
  18.1 3.3 %collective-permute-done.11.refs_2_ = bf16[48,768]{1,0:T(8,128)(2,1)S(1)} collective-permute-done((bf16[48,768]{1,0:T(8,128)(2,1)}, bf16[48,768]{1,0:T(8,128)(2,1)S(1)}, u32[]{:S(2)}, u32[]{:S(2)}) %collective-permute-start.11) | collective-permute-done | bytes 73760 | tf_op jit(solution)/shard_map/ppermute | solution.py:656
  21.4 1.9 collective-permute-start.12
  23.3 4.6 %collective-permute-done.12.refs_3_ = bf16[48,768]{1,0:T(8,128)(2,1)S(1)} collective-permute-done((bf16[48,768]{1,0:T(8,128)(2,1)}, bf16[48,768]{1,0:T(8,128)(2,1)S(1)}, u32[]{:S(2)}, u32[]{:S(2)}) %collective-permute-start.12) | collective-permute-done | bytes 73760 | tf_op jit(solution)/shard_map/ppermute | solution.py:656
  27.9 2.4 %collective-permute-start.5 = (bf16[96,1536]{1,0:T(8,128)(2,1)S(1)}, bf16[96,1536]{1,0:T(8,128)(2,1)S(1)}, u32[]{:S(2)}, u32[]{:S(2)}) collective-permute-start(bf16[96,1536]{1,0:T(8,128)(2,1)S(1)} %shard_map.197.refs_0_), channel_id=1, source_target_pairs={{0,6},{1,7},{2,4},{3,5},{4,2},{5,3},{6,0},{7,1},{8,14},{9,15},{10,... | collective-permute-start | bytes 884744 | tf_op jit(solution)/shard_map/ppermute | solution.py:656
  33.9 1.7 collective-permute-start.15
  35.6 2.4 %collective-permute-done.5.refs_3_ = bf16[96,1536]{1,0:T(8,128)(2,1)S(1)} collective-permute-done((bf16[96,1536]{1,0:T(8,128)(2,1)S(1)}, bf16[96,1536]{1,0:T(8,128)(2,1)S(1)}, u32[]{:S(2)}, u32[]{:S(2)}) %collective-permute-start.5) | collective-permute-done | bytes 294944 | tf_op jit(solution)/shard_map/ppermute | solution.py:656
  38.1 3.1 %collective-permute-start.25 = (bf16[96,1920]{1,0:T(8,128)(2,1)S(1)}, bf16[96,1920]{1,0:T(8,128)(2,1)S(1)}, u32[]{:S(2)}, u32[]{:S(2)}) collective-permute-start(bf16[96,1920]{1,0:T(8,128)(2,1)S(1)} %shard_map.199.refs_0_), channel_id=1, source_target_pairs={{0,6},{1,7},{2,4},{3,5},{4,2},{5,3},{6,0},{7,1},{8,14},{9,15},{10,... | collective-permute-start | bytes 1105928 | tf_op jit(solution)/shard_map/ppermute | solution.py:656
  41.1 3.3 %collective-permute-done.4.refs_2_ = bf16[96,1536]{1,0:T(8,128)(2,1)} collective-permute-done((bf16[96,1536]{1,0:T(8,128)(2,1)S(1)}, bf16[96,1536]{1,0:T(8,128)(2,1)}, u32[]{:S(2)}, u32[]{:S(2)}) %collective-permute-start.4) | collective-permute-done | bytes 294944 | tf_op jit(solution)/shard_map/ppermute | solution.py:656
  44.4 2.1 collective-permute-start.24
  48.7 2.3 collective-permute-done.15.refs_11_
  52.4 18.1 %collective-permute-done.14.refs_10_ = bf16[192,768]{1,0:T(8,128)(2,1)} collective-permute-done((bf16[192,768]{1,0:T(8,128)(2,1)S(1)}, bf16[192,768]{1,0:T(8,128)(2,1)}, u32[]{:S(2)}, u32[]{:S(2)}) %collective-permute-start.14) | collective-permute-done | bytes 294944 | tf_op jit(solution)/shard_map/ppermute | solution.py:656
  83.2 13.8 %shard_map.200 = (bf16[512,768]{1,0:T(8,128)(2,1)S(1)}, f32[8,1792]{1,0:T(8,128)S(1)}, f32[1,2304]{1,0:T(1,128)S(1)}, bf16[768,1920]{1,0:T(8,128)(2,1)S(1)}, f32...) custom-call(bf16[96,1920]{1,0:T(8,128)(2,1)S(1)} %shard_map.199.refs, ...), custom_call_target="tpu_custom_call" | custom-call | tf_op jit(solution)/shard_map/pallas_call | solution.py:633
  99.6 13.1 %shard_map.201 = (bf16[384,3072]{1,0:T(8,128)(2,1)S(1)}, bf16[384,3072]{1,0:T(8,128)(2,1)}, f32[512,1536]{1,0:T(8,128)S(1)}, bf16[512,1536]{1,0:T(8,128)(2,1)S(1...) custom-call(bf16[96,1536]{1,0:T(8,128)(2,1)S(1)} %shard_map.197.refs, ...), custom_call_target="tpu_custom_call" | custom-call | tf_op jit(solution)/shard_map/pallas_call | solution.py:633
  112.9 22.1 %shard_map.203 = (bf16[512,1920]{1,0:T(8,128)(2,1)S(1)}, f32[8,1792]{1,0:T(8,128)S(1)}, f32[1,1536]{1,0:T(1,128)S(1)}, f32[8,128]{1,0:T(8,128)S(1)}) custom-call(f32[512,1536]{1,0:T(8,128)S(1)} %get-tuple-element.74.g_ref, f32[512,1536]{1,0:T(8,128)S(1)} %get-tuple-element.75.yd_ref, f32[512,1536]{1,0:T(8,128)S(1)} %get-tuple-element.76.v_ref, ...), custom_call_target="tpu_custom_call" | custom-call | tf_op jit(solution)/shard_map/pallas_call | solution.py:633
  135.0 1.8 shard_map.205
  139.4 2.7 %shard_map.202 = (bf16[512,768]{1,0:T(8,128)(2,1)}, f32[512,768]{1,0:T(8,128)S(1)}) custom-call(bf16[512,1536]{1,0:T(8,128)(2,1)S(1)} %get-tuple-element.67.mixed_ref, bf16[1536,768]{1,0:T(8,128)(2,1)S(1)} %get-tuple-element.68.wo_ref, bf16[512,768]{1,0:T(8,128)(2,1)S(1)} %copy-done, bf16[512,1536]{1,0:T(8,128)(2,1)S(1)} %get-tuple-element.69.dgate_ref, ...), custom_call_target="tpu_custom_call" | custom-call | tf_op jit(solution)/shard_map/pallas_call | solution.py:633
  142.1 7.0 %shard_map.204 = (f32[512,768]{1,0:T(8,128)}, f32[8,2304]{1,0:T(8,128)S(1)}) custom-call(bf16[768,1920]{1,0:T(8,128)(2,1)S(1)} %copy-done.3, f32[512,768]{1,0:T(8,128)S(1)} %get-tuple-element.73.dng_ref, bf16[512,1920]{1,0:T(8,128)(2,1)S(1)} %get-tuple-element.81.dp_ref, s32[1]{0:T(128)} %bitcast.1.refs_8_.refs_16_.me_ref, ...), custom_call_target="tpu_custom_call" | custom-call | tf_op jit(solution)/shard_map/pallas_call | solution.py:633
  156.0 2.0 collective-permute-start.32
  161.0 37.9 %collective-permute-done.39.refs_2_ = bf16[96,3072]{1,0:T(8,128)(2,1)S(1)} collective-permute-done((bf16[96,3072]{1,0:T(8,128)(2,1)S(1)}, bf16[96,3072]{1,0:T(8,128)(2,1)S(1)}, u32[]{:S(2)}, u32[]{:S(2)}) %collective-permute-start.39) | collective-permute-done | bytes 589856 | tf_op jit(solution)/shard_map/ppermute | solution.py:656
  198.9 2.7 %collective-permute-start.50 = (f32[8,2304]{1,0:T(8,128)S(1)}, f32[8,2304]{1,0:T(8,128)S(1)}, u32[]{:S(2)}, u32[]{:S(2)}) collective-permute-start(f32[8,2304]{1,0:T(8,128)S(1)} %add_add_fusion.refs_0_), channel_id=1, source_target_pairs={{0,24},{1,25},{2,26},{3,27},{4,28},{5,29},{6,30},{7,31},{8,16},{9,... | collective-permute-start | bytes 221192 | tf_op jit(solution)/shard_map/ppermute | solution.py:656
  201.9 5.0 %collective-permute-start.41 = (bf16[24,3072]{1,0:T(8,128)(2,1)S(1)}, bf16[24,3072]{1,0:T(8,128)(2,1)S(1)}, u32[]{:S(2)}, u32[]{:S(2)}) collective-permute-start(bf16[24,3072]{1,0:T(8,128)(2,1)S(1)} %get-tuple-element.104), channel_id=1, source_target_pairs={{0,8},{1,9},{2,10},{3,11},{4,12},{5,13},{6,14},{7,15},{8,0},{9,1},... | collective-permute-start | bytes 442376 | tf_op jit(solution)/shard_map/ppermute | solution.py:656
  206.9 3.5 %collective-permute-start.49 = (f32[8,2304]{1,0:T(8,128)S(1)}, f32[8,2304]{1,0:T(8,128)S(1)}, u32[]{:S(2)}, u32[]{:S(2)}) collective-permute-start(f32[8,2304]{1,0:T(8,128)S(1)} %add_add_fusion.refs_0_), channel_id=1, source_target_pairs={{0,16},{1,17},{2,18},{3,19},{4,20},{5,21},{6,22},{7,23},{8,24},{9,... | collective-permute-start | bytes 221192 | tf_op jit(solution)/shard_map/ppermute | solution.py:656
  210.3 2.2 collective-permute-start.42
  212.5 2.2 collective-permute-start.43
  214.9 3.2 %collective-permute-done.49.refs_2_ = f32[8,2304]{1,0:T(8,128)S(1)} collective-permute-done((f32[8,2304]{1,0:T(8,128)S(1)}, f32[8,2304]{1,0:T(8,128)S(1)}, u32[]{:S(2)}, u32[]{:S(2)}) %collective-permute-start.49) | collective-permute-done | bytes 73760 | tf_op jit(solution)/shard_map/ppermute | solution.py:656
  218.1 4.4 %collective-permute-start.36 = (bf16[24,1920]{1,0:T(8,128)(2,1)S(1)}, bf16[24,1920]{1,0:T(8,128)(2,1)S(1)}, u32[]{:S(2)}, u32[]{:S(2)}) collective-permute-start(bf16[24,1920]{1,0:T(8,128)(2,1)S(1)} %get-tuple-element.96), channel_id=1, source_target_pairs={{0,24},{1,25},{2,26},{3,27},{4,28},{5,29},{6,30},{7,31},{8,16},{9,... | collective-permute-start | bytes 276488 | tf_op jit(solution)/shard_map/ppermute | solution.py:656
  223.2 4.4 %collective-permute-done.42.c_ref = bf16[24,3072]{1,0:T(8,128)(2,1)S(1)} collective-permute-done((bf16[24,3072]{1,0:T(8,128)(2,1)S(1)}, bf16[24,3072]{1,0:T(8,128)(2,1)S(1)}, u32[]{:S(2)}, u32[]{:S(2)}) %collective-permute-start.42) | collective-permute-done | bytes 147488 | tf_op jit(solution)/shard_map/ppermute | solution.py:656
  228.4 3.6 %collective-permute-done.35.c_ref = bf16[24,1920]{1,0:T(8,128)(2,1)S(1)} collective-permute-done((bf16[24,1920]{1,0:T(8,128)(2,1)S(1)}, bf16[24,1920]{1,0:T(8,128)(2,1)S(1)}, u32[]{:S(2)}, u32[]{:S(2)}) %collective-permute-start.35) | collective-permute-done | bytes 92192 | tf_op jit(solution)/shard_map/ppermute | solution.py:656
  (137 shorter events, 42.2 us)
Async XLA Ops:
  13.2 20.0 %collective-permute-start.6 = (bf16[96,1536]{1,0:T(8,128)(2,1)S(1)}, bf16[96,1536]{1,0:T(8,128)(2,1)S(1)}, u32[]{:S(2)}, u32[]{:S(2)}) collective-permute-start(bf16[96,1536]{1,0:T(8,128)(2,1)S(1)} %shard_map.197.refs_0_), channel_id=1, source_target_pairs={{0,1},{1,0},{2,3},{3,2},{4,5},{5,4},{6,7},{7,6},{8,9},{9,8},{10,11... | collective-permute-start | bytes 884744 | tf_op jit(solution)/shard_map/ppermute | solution.py:656
  16.6 13.7 %collective-permute-start.22 = (bf16[24,1920]{1,0:T(8,128)(2,1)S(1)}, bf16[24,1920]{1,0:T(8,128)(2,1)S(1)}, u32[]{:S(2)}, u32[]{:S(2)}) collective-permute-start(bf16[24,1920]{1,0:T(8,128)(2,1)S(1)} %get-tuple-element.63.refs_0_), channel_id=1, source_target_pairs={{0,24},{1,25},{2,26},{3,27},{4,28},{5,29},{6,30},{7,31},{8,16},{9,... | collective-permute-start | bytes 276488 | tf_op jit(solution)/shard_map/ppermute | solution.py:656
  17.7 13.1 %collective-permute-start.21 = (bf16[24,1920]{1,0:T(8,128)(2,1)S(1)}, bf16[24,1920]{1,0:T(8,128)(2,1)S(1)}, u32[]{:S(2)}, u32[]{:S(2)}) collective-permute-start(bf16[24,1920]{1,0:T(8,128)(2,1)S(1)} %get-tuple-element.63.refs_0_), channel_id=1, source_target_pairs={{0,16},{1,17},{2,18},{3,19},{4,20},{5,21},{6,22},{7,23},{8,24},{9,... | collective-permute-start | bytes 276488 | tf_op jit(solution)/shard_map/ppermute | solution.py:656
  30.4 14.1 %collective-permute-start.4 = (bf16[96,1536]{1,0:T(8,128)(2,1)S(1)}, bf16[96,1536]{1,0:T(8,128)(2,1)}, u32[]{:S(2)}, u32[]{:S(2)}) collective-permute-start(bf16[96,1536]{1,0:T(8,128)(2,1)S(1)} %shard_map.197.refs_0_), channel_id=1, source_target_pairs={{0,4},{1,5},{2,6},{3,7},{4,0},{5,1},{6,2},{7,3},{8,12},{9,13},{10,... | collective-permute-start | bytes 884744 | tf_op jit(solution)/shard_map/ppermute | solution.py:656
  30.9 15.7 %collective-permute-start.3 = (bf16[96,1536]{1,0:T(8,128)(2,1)S(1)}, bf16[96,1536]{1,0:T(8,128)(2,1)}, u32[]{:S(2)}, u32[]{:S(2)}) collective-permute-start(bf16[96,1536]{1,0:T(8,128)(2,1)S(1)} %shard_map.197.refs_0_), channel_id=1, source_target_pairs={{0,2},{1,3},{2,0},{3,1},{4,6},{5,7},{6,4},{7,5},{8,10},{9,11},{10,... | collective-permute-start | bytes 884744 | tf_op jit(solution)/shard_map/ppermute | solution.py:656
  33.1 13.6 %collective-permute-start.16 = (bf16[192,768]{1,0:T(8,128)(2,1)S(1)}, bf16[192,768]{1,0:T(8,128)(2,1)S(1)}, u32[]{:S(2)}, u32[]{:S(2)}) collective-permute-start(bf16[192,768]{1,0:T(8,128)(2,1)S(1)} %shard_map.198.refs_8_), channel_id=1, source_target_pairs={{0,1},{1,0},{2,3},{3,2},{4,5},{5,4},{6,7},{7,6},{8,9},{9,8},{10,11... | collective-permute-start | bytes 884744 | tf_op jit(solution)/shard_map/ppermute | solution.py:656
  33.9 17.0 %collective-permute-start.15 = (bf16[192,768]{1,0:T(8,128)(2,1)S(1)}, bf16[192,768]{1,0:T(8,128)(2,1)}, u32[]{:S(2)}, u32[]{:S(2)}) collective-permute-start(bf16[192,768]{1,0:T(8,128)(2,1)S(1)} %shard_map.198.refs_8_), channel_id=1, source_target_pairs={{0,6},{1,7},{2,4},{3,5},{4,2},{5,3},{6,0},{7,1},{8,14},{9,15},{10,... | collective-permute-start | bytes 884744 | tf_op jit(solution)/shard_map/ppermute | solution.py:656
  38.1 32.5 %collective-permute-start.25 = (bf16[96,1920]{1,0:T(8,128)(2,1)S(1)}, bf16[96,1920]{1,0:T(8,128)(2,1)S(1)}, u32[]{:S(2)}, u32[]{:S(2)}) collective-permute-start(bf16[96,1920]{1,0:T(8,128)(2,1)S(1)} %shard_map.199.refs_0_), channel_id=1, source_target_pairs={{0,6},{1,7},{2,4},{3,5},{4,2},{5,3},{6,0},{7,1},{8,14},{9,15},{10,... | collective-permute-start | bytes 1105928 | tf_op jit(solution)/shard_map/ppermute | solution.py:656
  44.4 26.6 %collective-permute-start.24 = (bf16[96,1920]{1,0:T(8,128)(2,1)S(1)}, bf16[96,1920]{1,0:T(8,128)(2,1)S(1)}, u32[]{:S(2)}, u32[]{:S(2)}) collective-permute-start(bf16[96,1920]{1,0:T(8,128)(2,1)S(1)} %shard_map.199.refs_0_), channel_id=1, source_target_pairs={{0,4},{1,5},{2,6},{3,7},{4,0},{5,1},{6,2},{7,3},{8,12},{9,13},{10,... | collective-permute-start | bytes 1105928 | tf_op jit(solution)/shard_map/ppermute | solution.py:656
  46.5 24.6 %collective-permute-start.23 = (bf16[96,1920]{1,0:T(8,128)(2,1)S(1)}, bf16[96,1920]{1,0:T(8,128)(2,1)S(1)}, u32[]{:S(2)}, u32[]{:S(2)}) collective-permute-start(bf16[96,1920]{1,0:T(8,128)(2,1)S(1)} %shard_map.199.refs_0_), channel_id=1, source_target_pairs={{0,2},{1,3},{2,0},{3,1},{4,6},{5,7},{6,4},{7,5},{8,10},{9,11},{10,... | collective-permute-start | bytes 1105928 | tf_op jit(solution)/shard_map/ppermute | solution.py:656
  47.4 23.1 %collective-permute-start.14 = (bf16[192,768]{1,0:T(8,128)(2,1)S(1)}, bf16[192,768]{1,0:T(8,128)(2,1)}, u32[]{:S(2)}, u32[]{:S(2)}) collective-permute-start(bf16[192,768]{1,0:T(8,128)(2,1)S(1)} %shard_map.198.refs_8_), channel_id=1, source_target_pairs={{0,4},{1,5},{2,6},{3,7},{4,0},{5,1},{6,2},{7,3},{8,12},{9,13},{10,... | collective-permute-start | bytes 884744 | tf_op jit(solution)/shard_map/ppermute | solution.py:656
  50.9 21.4 %collective-permute-start.13 = (bf16[192,768]{1,0:T(8,128)(2,1)S(1)}, bf16[192,768]{1,0:T(8,128)(2,1)}, u32[]{:S(2)}, u32[]{:S(2)}) collective-permute-start(bf16[192,768]{1,0:T(8,128)(2,1)S(1)} %shard_map.198.refs_8_), channel_id=1, source_target_pairs={{0,2},{1,3},{2,0},{3,1},{4,6},{5,7},{6,4},{7,5},{8,10},{9,11},{10,... | collective-permute-start | bytes 884744 | tf_op jit(solution)/shard_map/ppermute | solution.py:656
  73.8 24.8 %collective-permute-start.8 = (bf16[96,1536]{1,0:T(8,128)(2,1)}, bf16[96,1536]{1,0:T(8,128)(2,1)}, u32[]{:S(2)}, u32[]{:S(2)}) collective-permute-start(bf16[96,1536]{1,0:T(8,128)(2,1)} %collective-permute-done.4.refs_2_), channel_id=1, source_target_pairs={{0,1},{1,0},{2,3},{3,2},{4,5},{5,4},{6,7},{7,6},{8,9},{9,8},{10,11... | collective-permute-start | bytes 884744 | tf_op jit(solution)/shard_map/ppermute | solution.py:656
  75.0 23.6 %collective-permute-start.7 = (bf16[96,1536]{1,0:T(8,128)(2,1)}, bf16[96,1536]{1,0:T(8,128)(2,1)}, u32[]{:S(2)}, u32[]{:S(2)}) collective-permute-start(bf16[96,1536]{1,0:T(8,128)(2,1)} %collective-permute-done.3.refs_1_), channel_id=1, source_target_pairs={{0,1},{1,0},{2,3},{3,2},{4,5},{5,4},{6,7},{7,6},{8,9},{9,8},{10,11... | collective-permute-start | bytes 884744 | tf_op jit(solution)/shard_map/ppermute | solution.py:656
  75.8 22.8 %collective-permute-start.19 = (bf16[192,768]{1,0:T(8,128)(2,1)}, bf16[192,768]{1,0:T(8,128)(2,1)}, u32[]{:S(2)}, u32[]{:S(2)}) collective-permute-start(bf16[192,768]{1,0:T(8,128)(2,1)} %collective-permute-done.15.refs_11_), channel_id=1, source_target_pairs={{0,1},{1,0},{2,3},{3,2},{4,5},{5,4},{6,7},{7,6},{8,9},{9,8},{10,11... | collective-permute-start | bytes 884744 | tf_op jit(solution)/shard_map/ppermute | solution.py:656
  77.0 21.6 %collective-permute-start.18 = (bf16[192,768]{1,0:T(8,128)(2,1)}, bf16[192,768]{1,0:T(8,128)(2,1)}, u32[]{:S(2)}, u32[]{:S(2)}) collective-permute-start(bf16[192,768]{1,0:T(8,128)(2,1)} %collective-permute-done.14.refs_10_), channel_id=1, source_target_pairs={{0,1},{1,0},{2,3},{3,2},{4,5},{5,4},{6,7},{7,6},{8,9},{9,8},{10,11... | collective-permute-start | bytes 884744 | tf_op jit(solution)/shard_map/ppermute | solution.py:656
  77.8 20.8 %collective-permute-start.17 = (bf16[192,768]{1,0:T(8,128)(2,1)}, bf16[192,768]{1,0:T(8,128)(2,1)}, u32[]{:S(2)}, u32[]{:S(2)}) collective-permute-start(bf16[192,768]{1,0:T(8,128)(2,1)} %collective-permute-done.13.refs_9_), channel_id=1, source_target_pairs={{0,1},{1,0},{2,3},{3,2},{4,5},{5,4},{6,7},{7,6},{8,9},{9,8},{10,11... | collective-permute-start | bytes 884744 | tf_op jit(solution)/shard_map/ppermute | solution.py:656
  112.8 24.5 %collective-permute-start.37 = (bf16[384,3072]{1,0:T(8,128)(2,1)}, bf16[384,3072]{1,0:T(8,128)(2,1)S(1)}, u32[]{:S(2)}, u32[]{:S(2)}) collective-permute-start(bf16[384,3072]{1,0:T(8,128)(2,1)} %get-tuple-element.98), channel_id=1, source_target_pairs={{0,1},{1,0},{2,3},{3,2},{4,5},{5,4},{6,7},{7,6},{8,9},{9,8},{10,11... | collective-permute-start | bytes 7077896 | tf_op jit(solution)/shard_map/ppermute | solution.py:656
  136.8 17.1 %collective-permute-start.30 = (bf16[384,1920]{1,0:T(8,128)(2,1)S(1)}, bf16[384,1920]{1,0:T(8,128)(2,1)S(1)}, u32[]{:S(2)}, u32[]{:S(2)}) collective-permute-start(bf16[384,1920]{1,0:T(8,128)(2,1)S(1)} %get-tuple-element.88), channel_id=1, source_target_pairs={{0,1},{1,0},{2,3},{3,2},{4,5},{5,4},{6,7},{7,6},{8,9},{9,8},{10,11... | collective-permute-start | bytes 4423688 | tf_op jit(solution)/shard_map/ppermute | solution.py:656
  137.8 22.2 %collective-permute-start.38 = (bf16[96,3072]{1,0:T(8,128)(2,1)S(1)}, bf16[96,3072]{1,0:T(8,128)(2,1)S(1)}, u32[]{:S(2)}, u32[]{:S(2)}) collective-permute-start(bf16[96,3072]{1,0:T(8,128)(2,1)S(1)} %get-tuple-element.100), channel_id=1, source_target_pairs={{0,2},{1,3},{2,0},{3,1},{4,6},{5,7},{6,4},{7,5},{8,10},{9,11},{10,... | collective-permute-start | bytes 1769480 | tf_op jit(solution)/shard_map/ppermute | solution.py:656
  154.3 56.1 %collective-permute-start.31 = (bf16[96,1920]{1,0:T(8,128)(2,1)S(1)}, bf16[96,1920]{1,0:T(8,128)(2,1)S(1)}, u32[]{:S(2)}, u32[]{:S(2)}) collective-permute-start(bf16[96,1920]{1,0:T(8,128)(2,1)S(1)} %get-tuple-element.90), channel_id=1, source_target_pairs={{0,2},{1,3},{2,0},{3,1},{4,6},{5,7},{6,4},{7,5},{8,10},{9,11},{10,... | collective-permute-start | bytes 1105928 | tf_op jit(solution)/shard_map/ppermute | solution.py:656
  156.0 54.3 %collective-permute-start.32 = (bf16[96,1920]{1,0:T(8,128)(2,1)S(1)}, bf16[96,1920]{1,0:T(8,128)(2,1)S(1)}, u32[]{:S(2)}, u32[]{:S(2)}) collective-permute-start(bf16[96,1920]{1,0:T(8,128)(2,1)S(1)} %get-tuple-element.91), channel_id=1, source_target_pairs={{0,4},{1,5},{2,6},{3,7},{4,0},{5,1},{6,2},{7,3},{8,12},{9,13},{10,... | collective-permute-start | bytes 1105928 | tf_op jit(solution)/shard_map/ppermute | solution.py:656
  158.0 54.5 %collective-permute-start.33 = (bf16[96,1920]{1,0:T(8,128)(2,1)S(1)}, bf16[96,1920]{1,0:T(8,128)(2,1)S(1)}, u32[]{:S(2)}, u32[]{:S(2)}) collective-permute-start(bf16[96,1920]{1,0:T(8,128)(2,1)S(1)} %get-tuple-element.92), channel_id=1, source_target_pairs={{0,6},{1,7},{2,4},{3,5},{4,2},{5,3},{6,0},{7,1},{8,14},{9,15},{10,... | collective-permute-start | bytes 1105928 | tf_op jit(solution)/shard_map/ppermute | solution.py:656
  159.0 39.9 %collective-permute-start.39 = (bf16[96,3072]{1,0:T(8,128)(2,1)S(1)}, bf16[96,3072]{1,0:T(8,128)(2,1)S(1)}, u32[]{:S(2)}, u32[]{:S(2)}) collective-permute-start(bf16[96,3072]{1,0:T(8,128)(2,1)S(1)} %get-tuple-element.101), channel_id=1, source_target_pairs={{0,4},{1,5},{2,6},{3,7},{4,0},{5,1},{6,2},{7,3},{8,12},{9,13},{10,... | collective-permute-start | bytes 1769480 | tf_op jit(solution)/shard_map/ppermute | solution.py:656
  160.0 41.6 %collective-permute-start.40 = (bf16[96,3072]{1,0:T(8,128)(2,1)S(1)}, bf16[96,3072]{1,0:T(8,128)(2,1)S(1)}, u32[]{:S(2)}, u32[]{:S(2)}) collective-permute-start(bf16[96,3072]{1,0:T(8,128)(2,1)S(1)} %get-tuple-element.102), channel_id=1, source_target_pairs={{0,6},{1,7},{2,4},{3,5},{4,2},{5,3},{6,0},{7,1},{8,14},{9,15},{10,... | collective-permute-start | bytes 1769480 | tf_op jit(solution)/shard_map/ppermute | solution.py:656
  201.9 16.2 %collective-permute-start.41 = (bf16[24,3072]{1,0:T(8,128)(2,1)S(1)}, bf16[24,3072]{1,0:T(8,128)(2,1)S(1)}, u32[]{:S(2)}, u32[]{:S(2)}) collective-permute-start(bf16[24,3072]{1,0:T(8,128)(2,1)S(1)} %get-tuple-element.104), channel_id=1, source_target_pairs={{0,8},{1,9},{2,10},{3,11},{4,12},{5,13},{6,14},{7,15},{8,0},{9,1},... | collective-permute-start | bytes 442376 | tf_op jit(solution)/shard_map/ppermute | solution.py:656
  206.9 11.2 %collective-permute-start.49 = (f32[8,2304]{1,0:T(8,128)S(1)}, f32[8,2304]{1,0:T(8,128)S(1)}, u32[]{:S(2)}, u32[]{:S(2)}) collective-permute-start(f32[8,2304]{1,0:T(8,128)S(1)} %add_add_fusion.refs_0_), channel_id=1, source_target_pairs={{0,16},{1,17},{2,18},{3,19},{4,20},{5,21},{6,22},{7,23},{8,24},{9,... | collective-permute-start | bytes 221192 | tf_op jit(solution)/shard_map/ppermute | solution.py:656
  210.3 17.3 %collective-permute-start.42 = (bf16[24,3072]{1,0:T(8,128)(2,1)S(1)}, bf16[24,3072]{1,0:T(8,128)(2,1)S(1)}, u32[]{:S(2)}, u32[]{:S(2)}) collective-permute-start(bf16[24,3072]{1,0:T(8,128)(2,1)S(1)} %get-tuple-element.105), channel_id=1, source_target_pairs={{0,16},{1,17},{2,18},{3,19},{4,20},{5,21},{6,22},{7,23},{8,24},{9,... | collective-permute-start | bytes 442376 | tf_op jit(solution)/shard_map/ppermute | solution.py:656
  212.5 15.2 %collective-permute-start.43 = (bf16[24,3072]{1,0:T(8,128)(2,1)S(1)}, bf16[24,3072]{1,0:T(8,128)(2,1)S(1)}, u32[]{:S(2)}, u32[]{:S(2)}) collective-permute-start(bf16[24,3072]{1,0:T(8,128)(2,1)S(1)} %get-tuple-element.106), channel_id=1, source_target_pairs={{0,24},{1,25},{2,26},{3,27},{4,28},{5,29},{6,30},{7,31},{8,16},{9,... | collective-permute-start | bytes 442376 | tf_op jit(solution)/shard_map/ppermute | solution.py:656
  218.1 10.3 %collective-permute-start.34 = (bf16[24,1920]{1,0:T(8,128)(2,1)S(1)}, bf16[24,1920]{1,0:T(8,128)(2,1)S(1)}, u32[]{:S(2)}, u32[]{:S(2)}) collective-permute-start(bf16[24,1920]{1,0:T(8,128)(2,1)S(1)} %get-tuple-element.94), channel_id=1, source_target_pairs={{0,8},{1,9},{2,10},{3,11},{4,12},{5,13},{6,14},{7,15},{8,0},{9,1},... | collective-permute-start | bytes 276488 | tf_op jit(solution)/shard_map/ppermute | solution.py:656
  218.1 13.8 %collective-permute-start.35 = (bf16[24,1920]{1,0:T(8,128)(2,1)S(1)}, bf16[24,1920]{1,0:T(8,128)(2,1)S(1)}, u32[]{:S(2)}, u32[]{:S(2)}) collective-permute-start(bf16[24,1920]{1,0:T(8,128)(2,1)S(1)} %get-tuple-element.95), channel_id=1, source_target_pairs={{0,16},{1,17},{2,18},{3,19},{4,20},{5,21},{6,22},{7,23},{8,24},{9,... | collective-permute-start | bytes 276488 | tf_op jit(solution)/shard_map/ppermute | solution.py:656
  218.1 13.8 %collective-permute-start.36 = (bf16[24,1920]{1,0:T(8,128)(2,1)S(1)}, bf16[24,1920]{1,0:T(8,128)(2,1)S(1)}, u32[]{:S(2)}, u32[]{:S(2)}) collective-permute-start(bf16[24,1920]{1,0:T(8,128)(2,1)S(1)} %get-tuple-element.96), channel_id=1, source_target_pairs={{0,24},{1,25},{2,26},{3,27},{4,28},{5,29},{6,30},{7,31},{8,16},{9,... | collective-permute-start | bytes 276488 | tf_op jit(solution)/shard_map/ppermute | solution.py:656
  (43 other events, 406.6 us)

commit v5 on v4

--- a/solution.py
+++ b/solution.py
@@ -240,13 +240,19 @@
     lax.fori_loop(0, inner // BLK, body, 0)
 
 
+def gate_kernel(pieces, *refs):
+    xn_ref, gate_ref, wg_ref = refs[pieces:]
+    wg_ref[...] = rows_of(refs[:pieces])
+    gate_ref[...] = mm(xn_ref[...], wg_ref[...])
+
+
 def mid_kernel(pieces, table, *refs):
-    gw_refs, ow_refs = refs[:pieces], refs[pieces : 2 * pieces]
+    ow_refs = refs[:pieces]
     (
-        me_ref, xn_ref, sc_ref, gains_ref, cot_ref,
-        lo_ref, hi_ref, g_ref, dgate_ref, mixed_ref, ginner_ref, wo_ref, wg_ref,
+        me_ref, xn_ref, gate_ref, sc_ref, gains_ref, cot_ref,
+        lo_ref, hi_ref, g_ref, dgate_ref, mixed_ref, ginner_ref, wo_ref,
         dm_ref, nat_ref,
-    ) = refs[2 * pieces :]
+    ) = refs[pieces:]
     me = me_ref[0]
     devices = len(table)
     share = wo_ref.shape[0] // devices
@@ -256,8 +262,6 @@
     width = cot_ref.shape[1]
     rows_in = xn_ref.shape[1] // devices
     xn = xn_ref[...]
-    wg_ref[...] = rows_of(gw_refs)
-    g_ref[...] = mm(xn, wg_ref[...])
     if share % 16:
         wo_ref[...] = rows_of(ow_refs)
     else:
@@ -272,7 +276,7 @@
 
     def body(k, carry):
         rows = pl.ds(pl.multiple_of(k * sub, sub), sub)
-        gate = g_ref[rows, :]
+        gate = gate_ref[rows, :]
         sig = sigmoid(gate)
         silu = gate * sig
         scanned = sc_ref[rows, :]
@@ -775,17 +779,21 @@
         halves = (held((width // 2, inner + 2 * width), BF16), held((width // 2, inner + 2 * width), BF16))
     else:
         halves = (sds((width, inner), BF16), sds((inner, width), BF16))
-    lo, hi, g, dgate, mixed, ginner, wo, wg = call(
+    gate, wg = call(
+        lambda *refs: gate_kernel(count, *refs),
+        (held((length, inner), F32), held((width, inner), BF16)), *gw, xn,
+    )
+    lo, hi, g, dgate, mixed, ginner, wo = call(
         lambda *refs: mid_kernel(count, table, *refs),
         halves + (
             held((length, inner), F32), held((length, inner), BF16), held((length, inner), BF16),
-            held((8, inner), F32), held((inner, width), BF16), held((width, inner), BF16),
+            held((8, inner), F32), held((inner, width), BF16),
         ),
-        *gw, *ow, mine, xn, sc, gains_all, cot,
+        *ow, mine, xn, gate, sc, gains_all, cot,
         scratch=(
             pltpu.VMEM((length, inner), F32), pltpu.VMEM((inner, width), F32),
         ),
-        scalar=2 * count,
+        scalar=count,
     )
     if not aligned:
         gwo = hi.reshape(devices, 2, rows_in, width)[order]

time: 233 us -> 229 us (0.983)
  local copies, waits for them, and re-layouts: 14.1 us -> 7.08 us
  waiting for transfers between devices: 91.2 us -> 94.4 us
    unnamed x48 -> x36, local copies, waits for them, and re-layouts: 14.1 us -> 7.08 us
    ppermute x51, waiting for transfers between devices: 91.2 us -> 94.4 us  [send(): return lax.ppermute(x, 'fsdp', [(i, i ^ mask) for i in range(devices)])]
    pallas_call x17 -> x18, Pallas kernels: 66.2 us -> 67.6 us  [call(): pl.pallas_call(kernel, out_shape=outs, in_specs=specs, out_specs=out_spec...]
  transfers between devices with their start and end apart: 51 -> 51, of which waited for: 14 -> 16; matrix products, arithmetic and copies ran while one was open for 0% -> 0% of each run, Pallas kernels for 22% -> 24%
where the time goes in v5:
time: 229 us; the launch traced here: 228 us
  waiting for transfers between devices  94.4 us (41%)
  Pallas kernels  67.6 us (30%)
  starting transfers between devices  58.2 us (25%)
  local copies, waits for them, and re-layouts  7.08 us (3%)
    ppermute x51, waiting for transfers between devices, send(): return lax.ppermute(x, 'fsdp', [(i, i ^ mask) for i in range(devices)])  94.4 us
    pallas_call x18, Pallas kernels, call(): pl.pallas_call(kernel, out_shape=outs, in_specs=specs, out_specs=out_spec...  67.6 us
    ppermute x51, starting transfers between devices, send(): return lax.ppermute(x, 'fsdp', [(i, i ^ mask) for i in range(devices)])  58.2 us
    unnamed x36, local copies, waits for them, and re-layouts  7.08 us
  transfers between devices with their start and end apart: 51, of which 16 were waited for; matrix products, arithmetic and copies ran while one was open for 0% of the time, Pallas kernels for 24%

profile of v5, /device:TPU:0, one launch (start us, length us, event | category | flops | bytes accessed | tf_op | source)
XLA Modules:
  0.0 228.3 jit_solution(1388630994537495089)
XLA Ops:
  1.8 5.1 %collective-permute-start.22 = (bf16[24,1536]{1,0:T(8,128)(2,1)S(1)}, bf16[24,1536]{1,0:T(8,128)(2,1)S(1)}, u32[]{:S(2)}, u32[]{:S(2)}) collective-permute-start(bf16[24,1536]{1,0:T(8,128)(2,1)S(1)} %get-tuple-element.65.refs_0_), channel_id=1, source_target_pairs={{0,24},{1,25},{2,26},{3,27},{4,28},{5,29},{6,30},{7,31},{8,16},{9,... | collective-permute-start | bytes 221192 | tf_op jit(solution)/shard_map/ppermute | solution.py:660
  7.6 2.0 collective-permute-done.22.refs_3_
  9.6 3.5 %collective-permute-done.21.refs_2_ = bf16[24,1536]{1,0:T(8,128)(2,1)S(1)} collective-permute-done((bf16[24,1536]{1,0:T(8,128)(2,1)S(1)}, bf16[24,1536]{1,0:T(8,128)(2,1)S(1)}, u32[]{:S(2)}, u32[]{:S(2)}) %collective-permute-start.21) | collective-permute-done | bytes 73760 | tf_op jit(solution)/shard_map/ppermute | solution.py:660
  14.4 2.2 collective-permute-start
  18.1 3.3 %collective-permute-done.1.refs_2_ = bf16[48,768]{1,0:T(8,128)(2,1)S(1)} collective-permute-done((bf16[48,768]{1,0:T(8,128)(2,1)}, bf16[48,768]{1,0:T(8,128)(2,1)S(1)}, u32[]{:S(2)}, u32[]{:S(2)}) %collective-permute-start.1) | collective-permute-done | bytes 73760 | tf_op jit(solution)/shard_map/ppermute | solution.py:660
  21.4 1.9 collective-permute-start.2
  23.3 4.6 %collective-permute-done.2.refs_3_ = bf16[48,768]{1,0:T(8,128)(2,1)S(1)} collective-permute-done((bf16[48,768]{1,0:T(8,128)(2,1)}, bf16[48,768]{1,0:T(8,128)(2,1)S(1)}, u32[]{:S(2)}, u32[]{:S(2)}) %collective-permute-start.2) | collective-permute-done | bytes 73760 | tf_op jit(solution)/shard_map/ppermute | solution.py:660
  27.9 2.4 %collective-permute-start.25 = (bf16[96,1536]{1,0:T(8,128)(2,1)S(1)}, bf16[96,1536]{1,0:T(8,128)(2,1)S(1)}, u32[]{:S(2)}, u32[]{:S(2)}) collective-permute-start(bf16[96,1536]{1,0:T(8,128)(2,1)S(1)} %shard_map.200.refs_0_), channel_id=1, source_target_pairs={{0,6},{1,7},{2,4},{3,5},{4,2},{5,3},{6,0},{7,1},{8,14},{9,15},{10,... | collective-permute-start | bytes 884744 | tf_op jit(solution)/shard_map/ppermute | solution.py:660
  38.1 3.1 %collective-permute-start.15 = (bf16[96,1920]{1,0:T(8,128)(2,1)S(1)}, bf16[96,1920]{1,0:T(8,128)(2,1)S(1)}, u32[]{:S(2)}, u32[]{:S(2)}) collective-permute-start(bf16[96,1920]{1,0:T(8,128)(2,1)S(1)} %shard_map.198.refs_0_), channel_id=1, source_target_pairs={{0,6},{1,7},{2,4},{3,5},{4,2},{5,3},{6,0},{7,1},{8,14},{9,15},{10,... | collective-permute-start | bytes 1105928 | tf_op jit(solution)/shard_map/ppermute | solution.py:660
  41.1 13.3 %collective-permute-done.24.refs_2_ = bf16[96,1536]{1,0:T(8,128)(2,1)S(1)} collective-permute-done((bf16[96,1536]{1,0:T(8,128)(2,1)S(1)}, bf16[96,1536]{1,0:T(8,128)(2,1)S(1)}, u32[]{:S(2)}, u32[]{:S(2)}) %collective-permute-start.24) | collective-permute-done | bytes 294944 | tf_op jit(solution)/shard_map/ppermute | solution.py:660
  56.3 6.7 %collective-permute-done.4.refs_2_ = bf16[192,768]{1,0:T(8,128)(2,1)} collective-permute-done((bf16[192,768]{1,0:T(8,128)(2,1)}, bf16[192,768]{1,0:T(8,128)(2,1)}, u32[]{:S(2)}, u32[]{:S(2)}) %collective-permute-start.4) | collective-permute-done | bytes 294944 | tf_op jit(solution)/shard_map/ppermute | solution.py:660
  64.2 6.2 %collective-permute-done.14.refs_2_ = bf16[96,1920]{1,0:T(8,128)(2,1)S(1)} collective-permute-done((bf16[96,1920]{1,0:T(8,128)(2,1)S(1)}, bf16[96,1920]{1,0:T(8,128)(2,1)S(1)}, u32[]{:S(2)}, u32[]{:S(2)}) %collective-permute-start.14) | collective-permute-done | bytes 368672 | tf_op jit(solution)/shard_map/ppermute | solution.py:660
  79.5 13.8 %shard_map.199 = (bf16[512,768]{1,0:T(8,128)(2,1)S(1)}, f32[8,1792]{1,0:T(8,128)S(1)}, f32[1,2304]{1,0:T(1,128)S(1)}, bf16[768,1920]{1,0:T(8,128)(2,1)S(1)}, f32...) custom-call(bf16[96,1920]{1,0:T(8,128)(2,1)S(1)} %shard_map.198.refs, ...), custom_call_target="tpu_custom_call" | custom-call | tf_op jit(solution)/shard_map/pallas_call | solution.py:637
  93.4 3.2 %shard_map.201 = (f32[512,1536]{1,0:T(8,128)S(1)}, bf16[768,1536]{1,0:T(8,128)(2,1)S(1)}) custom-call(bf16[96,1536]{1,0:T(8,128)(2,1)S(1)} %shard_map.200.refs_0_, bf16[96,1536]{1,0:T(8,128)(2,1)} %collective-permute-done.23.refs_1_, bf16[96,1536]{1,0:T(8,128)(2,1)S(1)} %copy-done.13, bf16[96,1536]{1,0:T(8,128)(2,1)S(1)} %copy-done.11, ...), custom_call_target="tpu_custom_call" | custom-call | tf_op jit(solution)/shard_map/pallas_call | solution.py:637
  96.7 10.5 %shard_map.202 = (bf16[384,3072]{1,0:T(8,128)(2,1)S(1)}, bf16[384,3072]{1,0:T(8,128)(2,1)S(1)}, f32[512,1536]{1,0:T(8,128)S(1)}, bf16[512,1536]{1,0:T(8,128)(2,1...) custom-call(bf16[192,768]{1,0:T(8,128)(2,1)} %shard_map.196.refs_0_, ...), custom_call_target="tpu_custom_call" | custom-call | tf_op jit(solution)/shard_map/pallas_call | solution.py:637
  107.8 22.2 %shard_map.204 = (bf16[512,1920]{1,0:T(8,128)(2,1)S(1)}, f32[8,1792]{1,0:T(8,128)S(1)}, f32[1,1536]{1,0:T(1,128)S(1)}, f32[8,128]{1,0:T(8,128)S(1)}) custom-call(f32[512,1536]{1,0:T(8,128)S(1)} %get-tuple-element.76.g_ref, f32[512,1536]{1,0:T(8,128)S(1)} %get-tuple-element.77.yd_ref, f32[512,1536]{1,0:T(8,128)S(1)} %get-tuple-element.78.v_ref, ...), custom_call_target="tpu_custom_call" | custom-call | tf_op jit(solution)/shard_map/pallas_call | solution.py:637
  129.9 1.8 shard_map.206
  132.5 1.8 collective-permute-start.38
  134.3 2.7 %shard_map.203 = (bf16[512,768]{1,0:T(8,128)(2,1)}, f32[512,768]{1,0:T(8,128)S(1)}) custom-call(bf16[512,1536]{1,0:T(8,128)(2,1)S(1)} %get-tuple-element.69.mixed_ref, bf16[1536,768]{1,0:T(8,128)(2,1)S(1)} %get-tuple-element.70.wo_ref, bf16[512,768]{1,0:T(8,128)(2,1)S(1)} %copy-done, bf16[512,1536]{1,0:T(8,128)(2,1)S(1)} %get-tuple-element.71.dgate_ref, ...), custom_call_target="tpu_custom_call" | custom-call | tf_op jit(solution)/shard_map/pallas_call | solution.py:637
  136.9 7.0 %shard_map.205 = (f32[512,768]{1,0:T(8,128)}, f32[8,2304]{1,0:T(8,128)S(1)}) custom-call(bf16[768,1920]{1,0:T(8,128)(2,1)S(1)} %copy-done.3, f32[512,768]{1,0:T(8,128)S(1)} %get-tuple-element.75.dng_ref, bf16[512,1920]{1,0:T(8,128)(2,1)S(1)} %get-tuple-element.83.dp_ref, s32[1]{0:T(128)} %bitcast.refs_8_.me_ref, s32[8,768]{1,0:T(8,128)} %constant.10.clone.refs_9_.tab_ref, ...), custom_call_target="tpu_custom_call" | custom-call | tf_op jit(solution)/shard_map/pallas_call | solution.py:637
  147.1 1.7 collective-permute-start.45
  149.5 1.8 collective-permute-done.47
  156.3 38.0 %collective-permute-done.39.refs_2_ = bf16[96,3072]{1,0:T(8,128)(2,1)S(1)} collective-permute-done((bf16[96,3072]{1,0:T(8,128)(2,1)S(1)}, bf16[96,3072]{1,0:T(8,128)(2,1)S(1)}, u32[]{:S(2)}, u32[]{:S(2)}) %collective-permute-start.39) | collective-permute-done | bytes 589856 | tf_op jit(solution)/shard_map/ppermute | solution.py:660
  194.3 2.8 %collective-permute-start.50 = (f32[8,2304]{1,0:T(8,128)S(1)}, f32[8,2304]{1,0:T(8,128)S(1)}, u32[]{:S(2)}, u32[]{:S(2)}) collective-permute-start(f32[8,2304]{1,0:T(8,128)S(1)} %add_add_fusion.refs_0_), channel_id=1, source_target_pairs={{0,24},{1,25},{2,26},{3,27},{4,28},{5,29},{6,30},{7,31},{8,16},{9,... | collective-permute-start | bytes 221192 | tf_op jit(solution)/shard_map/ppermute | solution.py:660
  197.4 5.0 %collective-permute-start.41 = (bf16[24,3072]{1,0:T(8,128)(2,1)S(1)}, bf16[24,3072]{1,0:T(8,128)(2,1)S(1)}, u32[]{:S(2)}, u32[]{:S(2)}) collective-permute-start(bf16[24,3072]{1,0:T(8,128)(2,1)S(1)} %get-tuple-element.106), channel_id=1, source_target_pairs={{0,8},{1,9},{2,10},{3,11},{4,12},{5,13},{6,14},{7,15},{8,0},{9,1},... | collective-permute-start | bytes 442376 | tf_op jit(solution)/shard_map/ppermute | solution.py:660
  202.4 3.5 %collective-permute-start.49 = (f32[8,2304]{1,0:T(8,128)S(1)}, f32[8,2304]{1,0:T(8,128)S(1)}, u32[]{:S(2)}, u32[]{:S(2)}) collective-permute-start(f32[8,2304]{1,0:T(8,128)S(1)} %add_add_fusion.refs_0_), channel_id=1, source_target_pairs={{0,16},{1,17},{2,18},{3,19},{4,20},{5,21},{6,22},{7,23},{8,24},{9,... | collective-permute-start | bytes 221192 | tf_op jit(solution)/shard_map/ppermute | solution.py:660
  205.9 2.1 collective-permute-start.42
  208.0 2.3 %collective-permute-start.43 = (bf16[24,3072]{1,0:T(8,128)(2,1)S(1)}, bf16[24,3072]{1,0:T(8,128)(2,1)S(1)}, u32[]{:S(2)}, u32[]{:S(2)}) collective-permute-start(bf16[24,3072]{1,0:T(8,128)(2,1)S(1)} %get-tuple-element.108), channel_id=1, source_target_pairs={{0,24},{1,25},{2,26},{3,27},{4,28},{5,29},{6,30},{7,31},{8,16},{9,... | collective-permute-start | bytes 442376 | tf_op jit(solution)/shard_map/ppermute | solution.py:660
  210.5 3.3 %collective-permute-done.49.refs_2_ = f32[8,2304]{1,0:T(8,128)S(1)} collective-permute-done((f32[8,2304]{1,0:T(8,128)S(1)}, f32[8,2304]{1,0:T(8,128)S(1)}, u32[]{:S(2)}, u32[]{:S(2)}) %collective-permute-start.49) | collective-permute-done | bytes 73760 | tf_op jit(solution)/shard_map/ppermute | solution.py:660
  213.8 4.4 %collective-permute-start.36 = (bf16[24,1920]{1,0:T(8,128)(2,1)S(1)}, bf16[24,1920]{1,0:T(8,128)(2,1)S(1)}, u32[]{:S(2)}, u32[]{:S(2)}) collective-permute-start(bf16[24,1920]{1,0:T(8,128)(2,1)S(1)} %get-tuple-element.98), channel_id=1, source_target_pairs={{0,24},{1,25},{2,26},{3,27},{4,28},{5,29},{6,30},{7,31},{8,16},{9,... | collective-permute-start | bytes 276488 | tf_op jit(solution)/shard_map/ppermute | solution.py:660
  218.9 4.4 %collective-permute-done.42.c_ref = bf16[24,3072]{1,0:T(8,128)(2,1)S(1)} collective-permute-done((bf16[24,3072]{1,0:T(8,128)(2,1)S(1)}, bf16[24,3072]{1,0:T(8,128)(2,1)S(1)}, u32[]{:S(2)}, u32[]{:S(2)}) %collective-permute-start.42) | collective-permute-done | bytes 147488 | tf_op jit(solution)/shard_map/ppermute | solution.py:660
  223.9 3.6 %collective-permute-done.35.c_ref = bf16[24,1920]{1,0:T(8,128)(2,1)S(1)} collective-permute-done((bf16[24,1920]{1,0:T(8,128)(2,1)S(1)}, bf16[24,1920]{1,0:T(8,128)(2,1)S(1)}, u32[]{:S(2)}, u32[]{:S(2)}) %collective-permute-start.35) | collective-permute-done | bytes 92192 | tf_op jit(solution)/shard_map/ppermute | solution.py:660
  (126 shorter events, 37.2 us)
Async XLA Ops:
  13.2 22.3 %collective-permute-start.26 = (bf16[96,1536]{1,0:T(8,128)(2,1)S(1)}, bf16[96,1536]{1,0:T(8,128)(2,1)S(1)}, u32[]{:S(2)}, u32[]{:S(2)}) collective-permute-start(bf16[96,1536]{1,0:T(8,128)(2,1)S(1)} %shard_map.200.refs_0_), channel_id=1, source_target_pairs={{0,1},{1,0},{2,3},{3,2},{4,5},{5,4},{6,7},{7,6},{8,9},{9,8},{10,11... | collective-permute-start | bytes 884744 | tf_op jit(solution)/shard_map/ppermute | solution.py:660
  16.6 13.7 %collective-permute-start.12 = (bf16[24,1920]{1,0:T(8,128)(2,1)S(1)}, bf16[24,1920]{1,0:T(8,128)(2,1)S(1)}, u32[]{:S(2)}, u32[]{:S(2)}) collective-permute-start(bf16[24,1920]{1,0:T(8,128)(2,1)S(1)} %get-tuple-element.63.refs_0_), channel_id=1, source_target_pairs={{0,24},{1,25},{2,26},{3,27},{4,28},{5,29},{6,30},{7,31},{8,16},{9,... | collective-permute-start | bytes 276488 | tf_op jit(solution)/shard_map/ppermute | solution.py:660
  17.7 13.1 %collective-permute-start.11 = (bf16[24,1920]{1,0:T(8,128)(2,1)S(1)}, bf16[24,1920]{1,0:T(8,128)(2,1)S(1)}, u32[]{:S(2)}, u32[]{:S(2)}) collective-permute-start(bf16[24,1920]{1,0:T(8,128)(2,1)S(1)} %get-tuple-element.63.refs_0_), channel_id=1, source_target_pairs={{0,16},{1,17},{2,18},{3,19},{4,20},{5,21},{6,22},{7,23},{8,24},{9,... | collective-permute-start | bytes 276488 | tf_op jit(solution)/shard_map/ppermute | solution.py:660
  23.3 10.4 %collective-permute-start.10 = (bf16[24,1920]{1,0:T(8,128)(2,1)S(1)}, bf16[24,1920]{1,0:T(8,128)(2,1)S(1)}, u32[]{:S(2)}, u32[]{:S(2)}) collective-permute-start(bf16[24,1920]{1,0:T(8,128)(2,1)S(1)} %get-tuple-element.63.refs_0_), channel_id=1, source_target_pairs={{0,8},{1,9},{2,10},{3,11},{4,12},{5,13},{6,14},{7,15},{8,0},{9,1},... | collective-permute-start | bytes 276488 | tf_op jit(solution)/shard_map/ppermute | solution.py:660
  30.4 24.1 %collective-permute-start.24 = (bf16[96,1536]{1,0:T(8,128)(2,1)S(1)}, bf16[96,1536]{1,0:T(8,128)(2,1)S(1)}, u32[]{:S(2)}, u32[]{:S(2)}) collective-permute-start(bf16[96,1536]{1,0:T(8,128)(2,1)S(1)} %shard_map.200.refs_0_), channel_id=1, source_target_pairs={{0,4},{1,5},{2,6},{3,7},{4,0},{5,1},{6,2},{7,3},{8,12},{9,13},{10,... | collective-permute-start | bytes 884744 | tf_op jit(solution)/shard_map/ppermute | solution.py:660
  30.9 24.1 %collective-permute-start.23 = (bf16[96,1536]{1,0:T(8,128)(2,1)S(1)}, bf16[96,1536]{1,0:T(8,128)(2,1)}, u32[]{:S(2)}, u32[]{:S(2)}) collective-permute-start(bf16[96,1536]{1,0:T(8,128)(2,1)S(1)} %shard_map.200.refs_0_), channel_id=1, source_target_pairs={{0,2},{1,3},{2,0},{3,1},{4,6},{5,7},{6,4},{7,5},{8,10},{9,11},{10,... | collective-permute-start | bytes 884744 | tf_op jit(solution)/shard_map/ppermute | solution.py:660
  33.7 22.6 %collective-permute-start.5 = (bf16[192,768]{1,0:T(8,128)(2,1)}, bf16[192,768]{1,0:T(8,128)(2,1)}, u32[]{:S(2)}, u32[]{:S(2)}) collective-permute-start(bf16[192,768]{1,0:T(8,128)(2,1)} %shard_map.196.refs_0_), channel_id=1, source_target_pairs={{0,6},{1,7},{2,4},{3,5},{4,2},{5,3},{6,0},{7,1},{8,14},{9,15},{10,... | collective-permute-start | bytes 884744 | tf_op jit(solution)/shard_map/ppermute | solution.py:660
  36.2 26.8 %collective-permute-start.4 = (bf16[192,768]{1,0:T(8,128)(2,1)}, bf16[192,768]{1,0:T(8,128)(2,1)}, u32[]{:S(2)}, u32[]{:S(2)}) collective-permute-start(bf16[192,768]{1,0:T(8,128)(2,1)} %shard_map.196.refs_0_), channel_id=1, source_target_pairs={{0,4},{1,5},{2,6},{3,7},{4,0},{5,1},{6,2},{7,3},{8,12},{9,13},{10,... | collective-permute-start | bytes 884744 | tf_op jit(solution)/shard_map/ppermute | solution.py:660
  38.1 26.1 %collective-permute-start.15 = (bf16[96,1920]{1,0:T(8,128)(2,1)S(1)}, bf16[96,1920]{1,0:T(8,128)(2,1)S(1)}, u32[]{:S(2)}, u32[]{:S(2)}) collective-permute-start(bf16[96,1920]{1,0:T(8,128)(2,1)S(1)} %shard_map.198.refs_0_), channel_id=1, source_target_pairs={{0,6},{1,7},{2,4},{3,5},{4,2},{5,3},{6,0},{7,1},{8,14},{9,15},{10,... | collective-permute-start | bytes 1105928 | tf_op jit(solution)/shard_map/ppermute | solution.py:660
  54.4 16.0 %collective-permute-start.14 = (bf16[96,1920]{1,0:T(8,128)(2,1)S(1)}, bf16[96,1920]{1,0:T(8,128)(2,1)S(1)}, u32[]{:S(2)}, u32[]{:S(2)}) collective-permute-start(bf16[96,1920]{1,0:T(8,128)(2,1)S(1)} %shard_map.198.refs_0_), channel_id=1, source_target_pairs={{0,4},{1,5},{2,6},{3,7},{4,0},{5,1},{6,2},{7,3},{8,12},{9,13},{10,... | collective-permute-start | bytes 1105928 | tf_op jit(solution)/shard_map/ppermute | solution.py:660
  55.0 15.4 %collective-permute-start.13 = (bf16[96,1920]{1,0:T(8,128)(2,1)S(1)}, bf16[96,1920]{1,0:T(8,128)(2,1)S(1)}, u32[]{:S(2)}, u32[]{:S(2)}) collective-permute-start(bf16[96,1920]{1,0:T(8,128)(2,1)S(1)} %shard_map.198.refs_0_), channel_id=1, source_target_pairs={{0,2},{1,3},{2,0},{3,1},{4,6},{5,7},{6,4},{7,5},{8,10},{9,11},{10,... | collective-permute-start | bytes 1105928 | tf_op jit(solution)/shard_map/ppermute | solution.py:660
  56.3 16.0 %collective-permute-start.16 = (bf16[96,1920]{1,0:T(8,128)(2,1)S(1)}, bf16[96,1920]{1,0:T(8,128)(2,1)S(1)}, u32[]{:S(2)}, u32[]{:S(2)}) collective-permute-start(bf16[96,1920]{1,0:T(8,128)(2,1)S(1)} %shard_map.198.refs_0_), channel_id=1, source_target_pairs={{0,1},{1,0},{2,3},{3,2},{4,5},{5,4},{6,7},{7,6},{8,9},{9,8},{10,11... | collective-permute-start | bytes 1105928 | tf_op jit(solution)/shard_map/ppermute | solution.py:660
  64.2 11.3 %collective-permute-start.19 = (bf16[96,1920]{1,0:T(8,128)(2,1)S(1)}, bf16[96,1920]{1,0:T(8,128)(2,1)S(1)}, u32[]{:S(2)}, u32[]{:S(2)}) collective-permute-start(bf16[96,1920]{1,0:T(8,128)(2,1)S(1)} %collective-permute-done.15.refs_3_), channel_id=1, source_target_pairs={{0,1},{1,0},{2,3},{3,2},{4,5},{5,4},{6,7},{7,6},{8,9},{9,8},{10,11... | collective-permute-start | bytes 1105928 | tf_op jit(solution)/shard_map/ppermute | solution.py:660
  74.2 22.4 %collective-permute-start.6 = (bf16[192,768]{1,0:T(8,128)(2,1)}, bf16[192,768]{1,0:T(8,128)(2,1)}, u32[]{:S(2)}, u32[]{:S(2)}) collective-permute-start(bf16[192,768]{1,0:T(8,128)(2,1)} %shard_map.196.refs_0_), channel_id=1, source_target_pairs={{0,1},{1,0},{2,3},{3,2},{4,5},{5,4},{6,7},{7,6},{8,9},{9,8},{10,11... | collective-permute-start | bytes 884744 | tf_op jit(solution)/shard_map/ppermute | solution.py:660
  75.0 18.3 %collective-permute-start.27 = (bf16[96,1536]{1,0:T(8,128)(2,1)}, bf16[96,1536]{1,0:T(8,128)(2,1)}, u32[]{:S(2)}, u32[]{:S(2)}) collective-permute-start(bf16[96,1536]{1,0:T(8,128)(2,1)} %collective-permute-done.23.refs_1_), channel_id=1, source_target_pairs={{0,1},{1,0},{2,3},{3,2},{4,5},{5,4},{6,7},{7,6},{8,9},{9,8},{10,11... | collective-permute-start | bytes 884744 | tf_op jit(solution)/shard_map/ppermute | solution.py:660
  75.5 21.1 %collective-permute-start.9 = (bf16[192,768]{1,0:T(8,128)(2,1)}, bf16[192,768]{1,0:T(8,128)(2,1)}, u32[]{:S(2)}, u32[]{:S(2)}) collective-permute-start(bf16[192,768]{1,0:T(8,128)(2,1)} %collective-permute-done.5.refs_3_), channel_id=1, source_target_pairs={{0,1},{1,0},{2,3},{3,2},{4,5},{5,4},{6,7},{7,6},{8,9},{9,8},{10,11... | collective-permute-start | bytes 884744 | tf_op jit(solution)/shard_map/ppermute | solution.py:660
  76.2 20.4 %collective-permute-start.8 = (bf16[192,768]{1,0:T(8,128)(2,1)}, bf16[192,768]{1,0:T(8,128)(2,1)}, u32[]{:S(2)}, u32[]{:S(2)}) collective-permute-start(bf16[192,768]{1,0:T(8,128)(2,1)} %collective-permute-done.4.refs_2_), channel_id=1, source_target_pairs={{0,1},{1,0},{2,3},{3,2},{4,5},{5,4},{6,7},{7,6},{8,9},{9,8},{10,11... | collective-permute-start | bytes 884744 | tf_op jit(solution)/shard_map/ppermute | solution.py:660
  77.5 19.1 %collective-permute-start.7 = (bf16[192,768]{1,0:T(8,128)(2,1)}, bf16[192,768]{1,0:T(8,128)(2,1)}, u32[]{:S(2)}, u32[]{:S(2)}) collective-permute-start(bf16[192,768]{1,0:T(8,128)(2,1)} %collective-permute-done.3.refs_1_), channel_id=1, source_target_pairs={{0,1},{1,0},{2,3},{3,2},{4,5},{5,4},{6,7},{7,6},{8,9},{9,8},{10,11... | collective-permute-start | bytes 884744 | tf_op jit(solution)/shard_map/ppermute | solution.py:660
  107.2 24.7 %collective-permute-start.37 = (bf16[384,3072]{1,0:T(8,128)(2,1)S(1)}, bf16[384,3072]{1,0:T(8,128)(2,1)S(1)}, u32[]{:S(2)}, u32[]{:S(2)}) collective-permute-start(bf16[384,3072]{1,0:T(8,128)(2,1)S(1)} %get-tuple-element.100), channel_id=1, source_target_pairs={{0,1},{1,0},{2,3},{3,2},{4,5},{5,4},{6,7},{7,6},{8,9},{9,8},{10,11... | collective-permute-start | bytes 7077896 | tf_op jit(solution)/shard_map/ppermute | solution.py:660
  131.8 17.0 %collective-permute-start.30 = (bf16[384,1920]{1,0:T(8,128)(2,1)S(1)}, bf16[384,1920]{1,0:T(8,128)(2,1)S(1)}, u32[]{:S(2)}, u32[]{:S(2)}) collective-permute-start(bf16[384,1920]{1,0:T(8,128)(2,1)S(1)} %get-tuple-element.90), channel_id=1, source_target_pairs={{0,1},{1,0},{2,3},{3,2},{4,5},{5,4},{6,7},{7,6},{8,9},{9,8},{10,11... | collective-permute-start | bytes 4423688 | tf_op jit(solution)/shard_map/ppermute | solution.py:660
  132.5 22.5 %collective-permute-start.38 = (bf16[96,3072]{1,0:T(8,128)(2,1)S(1)}, bf16[96,3072]{1,0:T(8,128)(2,1)S(1)}, u32[]{:S(2)}, u32[]{:S(2)}) collective-permute-start(bf16[96,3072]{1,0:T(8,128)(2,1)S(1)} %get-tuple-element.102), channel_id=1, source_target_pairs={{0,2},{1,3},{2,0},{3,1},{4,6},{5,7},{6,4},{7,5},{8,10},{9,11},{10,... | collective-permute-start | bytes 1769480 | tf_op jit(solution)/shard_map/ppermute | solution.py:660
  149.2 56.7 %collective-permute-start.31 = (bf16[96,1920]{1,0:T(8,128)(2,1)S(1)}, bf16[96,1920]{1,0:T(8,128)(2,1)S(1)}, u32[]{:S(2)}, u32[]{:S(2)}) collective-permute-start(bf16[96,1920]{1,0:T(8,128)(2,1)S(1)} %get-tuple-element.92), channel_id=1, source_target_pairs={{0,2},{1,3},{2,0},{3,1},{4,6},{5,7},{6,4},{7,5},{8,10},{9,11},{10,... | collective-permute-start | bytes 1105928 | tf_op jit(solution)/shard_map/ppermute | solution.py:660
  151.4 54.5 %collective-permute-start.32 = (bf16[96,1920]{1,0:T(8,128)(2,1)S(1)}, bf16[96,1920]{1,0:T(8,128)(2,1)S(1)}, u32[]{:S(2)}, u32[]{:S(2)}) collective-permute-start(bf16[96,1920]{1,0:T(8,128)(2,1)S(1)} %get-tuple-element.93), channel_id=1, source_target_pairs={{0,4},{1,5},{2,6},{3,7},{4,0},{5,1},{6,2},{7,3},{8,12},{9,13},{10,... | collective-permute-start | bytes 1105928 | tf_op jit(solution)/shard_map/ppermute | solution.py:660
  152.3 55.7 %collective-permute-start.33 = (bf16[96,1920]{1,0:T(8,128)(2,1)S(1)}, bf16[96,1920]{1,0:T(8,128)(2,1)S(1)}, u32[]{:S(2)}, u32[]{:S(2)}) collective-permute-start(bf16[96,1920]{1,0:T(8,128)(2,1)S(1)} %get-tuple-element.94), channel_id=1, source_target_pairs={{0,6},{1,7},{2,4},{3,5},{4,2},{5,3},{6,0},{7,1},{8,14},{9,15},{10,... | collective-permute-start | bytes 1105928 | tf_op jit(solution)/shard_map/ppermute | solution.py:660
  153.8 40.6 %collective-permute-start.39 = (bf16[96,3072]{1,0:T(8,128)(2,1)S(1)}, bf16[96,3072]{1,0:T(8,128)(2,1)S(1)}, u32[]{:S(2)}, u32[]{:S(2)}) collective-permute-start(bf16[96,3072]{1,0:T(8,128)(2,1)S(1)} %get-tuple-element.103), channel_id=1, source_target_pairs={{0,4},{1,5},{2,6},{3,7},{4,0},{5,1},{6,2},{7,3},{8,12},{9,13},{10,... | collective-permute-start | bytes 1769480 | tf_op jit(solution)/shard_map/ppermute | solution.py:660
  155.0 42.2 %collective-permute-start.40 = (bf16[96,3072]{1,0:T(8,128)(2,1)S(1)}, bf16[96,3072]{1,0:T(8,128)(2,1)S(1)}, u32[]{:S(2)}, u32[]{:S(2)}) collective-permute-start(bf16[96,3072]{1,0:T(8,128)(2,1)S(1)} %get-tuple-element.104), channel_id=1, source_target_pairs={{0,6},{1,7},{2,4},{3,5},{4,2},{5,3},{6,0},{7,1},{8,14},{9,15},{10,... | collective-permute-start | bytes 1769480 | tf_op jit(solution)/shard_map/ppermute | solution.py:660
  197.4 16.3 %collective-permute-start.41 = (bf16[24,3072]{1,0:T(8,128)(2,1)S(1)}, bf16[24,3072]{1,0:T(8,128)(2,1)S(1)}, u32[]{:S(2)}, u32[]{:S(2)}) collective-permute-start(bf16[24,3072]{1,0:T(8,128)(2,1)S(1)} %get-tuple-element.106), channel_id=1, source_target_pairs={{0,8},{1,9},{2,10},{3,11},{4,12},{5,13},{6,14},{7,15},{8,0},{9,1},... | collective-permute-start | bytes 442376 | tf_op jit(solution)/shard_map/ppermute | solution.py:660
  202.4 11.3 %collective-permute-start.49 = (f32[8,2304]{1,0:T(8,128)S(1)}, f32[8,2304]{1,0:T(8,128)S(1)}, u32[]{:S(2)}, u32[]{:S(2)}) collective-permute-start(f32[8,2304]{1,0:T(8,128)S(1)} %add_add_fusion.refs_0_), channel_id=1, source_target_pairs={{0,16},{1,17},{2,18},{3,19},{4,20},{5,21},{6,22},{7,23},{8,24},{9,... | collective-permute-start | bytes 221192 | tf_op jit(solution)/shard_map/ppermute | solution.py:660
  205.9 17.3 %collective-permute-start.42 = (bf16[24,3072]{1,0:T(8,128)(2,1)S(1)}, bf16[24,3072]{1,0:T(8,128)(2,1)S(1)}, u32[]{:S(2)}, u32[]{:S(2)}) collective-permute-start(bf16[24,3072]{1,0:T(8,128)(2,1)S(1)} %get-tuple-element.107), channel_id=1, source_target_pairs={{0,16},{1,17},{2,18},{3,19},{4,20},{5,21},{6,22},{7,23},{8,24},{9,... | collective-permute-start | bytes 442376 | tf_op jit(solution)/shard_map/ppermute | solution.py:660
  208.0 15.2 %collective-permute-start.43 = (bf16[24,3072]{1,0:T(8,128)(2,1)S(1)}, bf16[24,3072]{1,0:T(8,128)(2,1)S(1)}, u32[]{:S(2)}, u32[]{:S(2)}) collective-permute-start(bf16[24,3072]{1,0:T(8,128)(2,1)S(1)} %get-tuple-element.108), channel_id=1, source_target_pairs={{0,24},{1,25},{2,26},{3,27},{4,28},{5,29},{6,30},{7,31},{8,16},{9,... | collective-permute-start | bytes 442376 | tf_op jit(solution)/shard_map/ppermute | solution.py:660
  213.8 13.8 %collective-permute-start.35 = (bf16[24,1920]{1,0:T(8,128)(2,1)S(1)}, bf16[24,1920]{1,0:T(8,128)(2,1)S(1)}, u32[]{:S(2)}, u32[]{:S(2)}) collective-permute-start(bf16[24,1920]{1,0:T(8,128)(2,1)S(1)} %get-tuple-element.97), channel_id=1, source_target_pairs={{0,16},{1,17},{2,18},{3,19},{4,20},{5,21},{6,22},{7,23},{8,24},{9,... | collective-permute-start | bytes 276488 | tf_op jit(solution)/shard_map/ppermute | solution.py:660
  213.8 13.8 %collective-permute-start.36 = (bf16[24,1920]{1,0:T(8,128)(2,1)S(1)}, bf16[24,1920]{1,0:T(8,128)(2,1)S(1)}, u32[]{:S(2)}, u32[]{:S(2)}) collective-permute-start(bf16[24,1920]{1,0:T(8,128)(2,1)S(1)} %get-tuple-element.98), channel_id=1, source_target_pairs={{0,24},{1,25},{2,26},{3,27},{4,28},{5,29},{6,30},{7,31},{8,16},{9,... | collective-permute-start | bytes 276488 | tf_op jit(solution)/shard_map/ppermute | solution.py:660
  (37 other events, 286.3 us)
